TPU v7x, 32 devices: a whole 2x2x4 slice. The times are simulated.
32 devices in a mesh: replica: 4 (over y, x), shard: 8 (over z, core).
Axes of the slice: x: 2, y: 2, z: 4, core: 2. Of those that a mesh axis runs over, the one named last changes fastest.
Arguments:
- hidden_in: bfloat16 [4096, 2048], P(('replica', 'shard')), may hold values from -6 to 6
- segment_ids: int32 [4096], P(('replica', 'shard')), may hold values from 0 to 4095, as said below
- routes: int32 [4096, 6], P(('replica', 'shard')), may hold values from 0 to 63, all different within a row; in each aligned block of 128 rows (0 to 127, 128 to 255, ...) at most 16 rows name the same one
- norm_gain: bfloat16 [2048], P('shard'), may hold values from 0.5 to 1.5
- query_weight: bfloat16 [2048, 3072], P('shard'), may hold values from -0.125 to 0.125
- kv_down: bfloat16 [2048, 576], P('shard'), may hold values from -0.125 to 0.125
- kv_gain: bfloat16 [512], P('shard'), may hold values from 0.5 to 1.5
- kv_up: bfloat16 [512, 4096], P(None, 'shard'), may hold values from -0.25 to 0.25
- out_weight: bfloat16 [2048, 2048], P('shard'), may hold values from -0.5 to 0.5
- mixer_gain: bfloat16 [2048], P('shard'), may hold values from 0.5 to 1.5
- router_weight: bfloat16 [2048, 64], P('shard'), may hold values from -0.375 to 0.375
- shared_gate: bfloat16 [2048, 2816], P('shard'), may hold values from -0.125 to 0.125
- shared_up: bfloat16 [2048, 2816], P('shard'), may hold values from -0.125 to 0.125
- shared_down: bfloat16 [2816, 2048], P(None, 'shard'), may hold values from -0.109375 to 0.109375
- expert_gate: bfloat16 [1, 2048, 1408], P(None, 'shard'), may hold values from -0.125 to 0.125
- expert_up: bfloat16 [1, 2048, 1408], P(None, 'shard'), may hold values from -0.125 to 0.125
- expert_down: bfloat16 [1, 1408, 2048], P(None, None, 'shard'), may hold values from -2.5 to 2.5
- cotangent: bfloat16 [4096, 2048], P(('replica', 'shard')), may hold values from -6 to 6
Outputs:
- output: bfloat16 [4096, 2048], P(('replica', 'shard'))
- grad_input: float32 [4096, 2048], P(('replica', 'shard'))
- grad_norm_gain: float32 [2048], P('shard')
- grad_query: float32 [2048, 3072], P('shard')
- grad_kv_down: float32 [2048, 576], P('shard')
- grad_kv_gain: float32 [512], P('shard')
- grad_kv_up: float32 [512, 4096], P(None, 'shard')
- grad_out_weight: float32 [2048, 2048], P('shard')
- grad_mixer_gain: float32 [2048], P('shard')
- grad_router: float32 [2048, 64], P('shard')
- grad_shared_gate: float32 [2048, 2816], P('shard')
- grad_shared_up: float32 [2048, 2816], P('shard')
- grad_shared_down: float32 [2816, 2048], P(None, 'shard')
- grad_expert_gate: float32 [1, 2048, 1408], P(None, 'shard')
- grad_expert_up: float32 [1, 2048, 1408], P(None, 'shard')
- grad_expert_down: float32 [1, 1408, 2048], P(None, None, 'shard')
Inputs may be any that keep to these rules, and one draw needn't show every extreme that they name: `segment_ids`: segment numbers never fall, and every segment lies within one aligned block of 128 rows. `routes`: each row names 6 different experts; within the 128 rows of one device no expert is named by more than 16 rows.
All inputs are finite; a program needn't handle non-finite values.
Results may differ from a plain program's by a relative error of at most 0.034.
Values may be sent and summed in bfloat16 or wider, within the bound.
No kernel may reach another device: no remote copies, remote signals or barrier semaphores. Data moves between devices by JAX's collectives and lax.ppermute only.
A program may use at most 320 MiB of HBM per device.

v0:
```python
import jax
import jax.numpy as jnp
from jax import lax
from jax.sharding import PartitionSpec as P

H = 16
DN = 128
DR = 64
DV = 128
KVR = 512
NE = 64
EW = 1
CAP = 16


EPSILON = 1e-06
NEGATIVE = -1e30


def inv_rms(values):
    return lax.rsqrt(jnp.mean(values * values, axis=-1, keepdims=True) + EPSILON)


def mixed_einsum(form, left, right):
    return jnp.einsum(form, left, right, preferred_element_type=jnp.float32)


def exact_dot(left, right):
    return jnp.dot(left, right, precision=lax.Precision.HIGHEST, preferred_element_type=jnp.float32)


def rope_tables(seg_block):
    count = seg_block.shape[0]
    index = jnp.arange(count, dtype=jnp.int32)
    same_seg = seg_block[:, None] == seg_block[None, :]
    start = jnp.min(jnp.where(same_seg, index[None, :], count), axis=1)
    position = (index - start).astype(jnp.float32)
    half_rope = DR // 2
    freq_table = 10000.0 ** (-jnp.arange(half_rope, dtype=jnp.float32) / half_rope)
    angles = position[:, None] * freq_table[None, :]
    allowed = same_seg & (index[None, :] <= index[:, None])
    return (jnp.cos(angles), jnp.sin(angles), allowed)


def rotate(values, cosine, sine):
    half_rope = values.shape[-1] // 2
    first_half = values[..., :half_rope]
    second_half = values[..., half_rope:]
    return jnp.concatenate(
        [first_half * cosine - second_half * sine, second_half * cosine + first_half * sine],
        axis=-1,
    )


def unrotate(grads, cosine, sine):
    half_rope = grads.shape[-1] // 2
    first_half = grads[..., :half_rope]
    second_half = grads[..., half_rope:]
    return jnp.concatenate(
        [first_half * cosine + second_half * sine, second_half * cosine - first_half * sine],
        axis=-1,
    )


def silu_parts(pre_act):
    sigmoid_val = jax.nn.sigmoid(pre_act)
    return (pre_act * sigmoid_val, sigmoid_val * (1.0 + pre_act * (1.0 - sigmoid_val)))


def attention_forward(x_float, seg_block, attn_weights):
    norm_gain, query_weight, kv_down, kv_gain, kv_up, out_weight = attn_weights
    count = x_float.shape[0]
    scale_one = inv_rms(x_float)
    normed_one = (x_float * scale_one * norm_gain.astype(jnp.float32)).astype(jnp.bfloat16)
    query_all = jnp.dot(normed_one, query_weight, preferred_element_type=jnp.float32).reshape(
        count, H, DN + DR
    )
    latent_all = jnp.dot(normed_one, kv_down, preferred_element_type=jnp.float32)
    latent = latent_all[:, :KVR]
    key_rope = latent_all[:, KVR:]
    scale_kv = inv_rms(latent)
    latent_normed = (latent * scale_kv * kv_gain.astype(jnp.float32)).astype(jnp.bfloat16)
    kv_heads = jnp.dot(latent_normed, kv_up, preferred_element_type=jnp.float32).reshape(
        count, H, DN + DV
    )
    cosine, sine, allowed = rope_tables(seg_block)
    query_rot = rotate(query_all[..., DN:], cosine[:, None, :], sine[:, None, :])
    key_rot = rotate(key_rope, cosine, sine)
    score_scale = (DN + DR) ** (-0.5)
    query_b = (jnp.concatenate([query_all[..., :DN], query_rot], axis=-1) * score_scale).astype(
        jnp.bfloat16
    )
    key_b = jnp.concatenate(
        [kv_heads[..., :DN], jnp.broadcast_to(key_rot[:, None, :], (count, H, DR))], axis=-1
    ).astype(jnp.bfloat16)
    value_b = kv_heads[..., DN:].astype(jnp.bfloat16)
    scores = mixed_einsum("thd,shd->hts", query_b, key_b)
    scores = jnp.where(allowed[None], scores, NEGATIVE)
    top_score = jnp.max(scores, axis=-1, keepdims=True)
    expd = jnp.exp(scores - top_score)
    row_total = jnp.sum(expd, axis=-1, keepdims=True)
    log_sum = top_score + jnp.log(row_total)
    weights_b = (expd / row_total).astype(jnp.bfloat16)
    attended = (
        mixed_einsum("hts,shd->thd", weights_b, value_b).astype(jnp.bfloat16).reshape(count, H * DV)
    )
    hidden = x_float + jnp.dot(attended, out_weight, preferred_element_type=jnp.float32)
    saved = (
        normed_one,
        latent,
        scale_kv,
        latent_normed,
        cosine,
        sine,
        allowed,
        query_b,
        key_b,
        value_b,
        log_sum,
        attended,
    )
    return (hidden, saved)


def moe_forward(hidden, route_block, moe_weights):
    (
        mixer_gain,
        router_weight,
        shared_gate,
        shared_up,
        shared_down,
        expert_gate,
        expert_up,
        expert_down,
    ) = moe_weights
    scale_two = inv_rms(hidden)
    normed_two = (hidden * scale_two * mixer_gain.astype(jnp.float32)).astype(jnp.bfloat16)
    logits = jnp.dot(normed_two, router_weight, preferred_element_type=jnp.float32)
    router_probs = jax.nn.softmax(logits, axis=-1)
    selected = jnp.any(
        route_block[:, :, None] == jnp.arange(EW, dtype=jnp.int32)[None, None, :], axis=1
    ).astype(jnp.float32)
    combine = router_probs[:, :EW] * selected
    shared_gpre = jnp.dot(normed_two, shared_gate, preferred_element_type=jnp.float32)
    shared_upre = jnp.dot(normed_two, shared_up, preferred_element_type=jnp.float32)
    shared_hidden = (silu_parts(shared_gpre)[0] * shared_upre).astype(jnp.bfloat16)
    shared_out = jnp.dot(shared_hidden, shared_down, preferred_element_type=jnp.float32)
    slot_ids = jnp.arange(CAP, dtype=jnp.int32)
    chosen = selected[:, 0]
    place = jnp.cumsum(chosen.astype(jnp.int32)) - 1
    dispatch = ((place[None, :] == slot_ids[:, None]) & (chosen[None, :] > 0.5)).astype(jnp.float32)
    dispatch_b = dispatch.astype(jnp.bfloat16)
    rows_in = jnp.dot(dispatch_b, normed_two, preferred_element_type=jnp.float32).astype(
        jnp.bfloat16
    )
    gate_pre = jnp.dot(rows_in, expert_gate[0], preferred_element_type=jnp.float32)
    up_pre = jnp.dot(rows_in, expert_up[0], preferred_element_type=jnp.float32)
    rows_hidden = (silu_parts(gate_pre)[0] * up_pre).astype(jnp.bfloat16)
    rows_out = jnp.dot(rows_hidden, expert_down[0], preferred_element_type=jnp.float32)
    rows_weight = exact_dot(dispatch, combine[:, 0])
    routed_total = exact_dot(dispatch.T, rows_weight[:, None] * rows_out)
    expert_saved = [
        (dispatch, dispatch_b, rows_in, gate_pre, up_pre, rows_hidden, rows_out, rows_weight)
    ]
    total = hidden + shared_out + routed_total
    saved = (
        normed_two,
        scale_two,
        router_probs,
        selected,
        combine,
        shared_gpre,
        shared_upre,
        shared_hidden,
        expert_saved,
    )
    return (total.astype(jnp.bfloat16), saved)


def moe_backward(grad_out, hidden, saved, moe_weights):
    (
        mixer_gain,
        router_weight,
        shared_gate,
        shared_up,
        shared_down,
        expert_gate,
        expert_up,
        expert_down,
    ) = moe_weights
    (
        normed_two,
        scale_two,
        router_probs,
        selected,
        combine,
        shared_gpre,
        shared_upre,
        shared_hidden,
        expert_saved,
    ) = saved
    count = hidden.shape[0]
    grad_float = grad_out.astype(jnp.float32)
    dispatch, dispatch_b, rows_in, gate_pre, up_pre, rows_hidden, rows_out, rows_weight = (
        expert_saved[0]
    )
    rows_grad = jnp.dot(dispatch_b, grad_out, preferred_element_type=jnp.float32)
    combine_grads = [exact_dot(dispatch.T, jnp.sum(rows_grad * rows_out, axis=-1))]
    rows_geo = (rows_weight[:, None] * rows_grad).astype(jnp.bfloat16)
    down_grads = [jnp.dot(rows_hidden.T, rows_geo, preferred_element_type=jnp.float32)]
    rows_geh = jnp.dot(rows_geo, expert_down[0].T, preferred_element_type=jnp.float32)
    rows_act, rows_slope = silu_parts(gate_pre)
    rows_geg = (rows_geh * up_pre * rows_slope).astype(jnp.bfloat16)
    rows_geu = (rows_geh * rows_act).astype(jnp.bfloat16)
    gate_grads = [jnp.dot(rows_in.T, rows_geg, preferred_element_type=jnp.float32)]
    up_grads = [jnp.dot(rows_in.T, rows_geu, preferred_element_type=jnp.float32)]
    rows_back = jnp.dot(rows_geg, expert_gate[0].T, preferred_element_type=jnp.float32) + jnp.dot(
        rows_geu, expert_up[0].T, preferred_element_type=jnp.float32
    )
    grad_routed = exact_dot(dispatch.T, rows_back)
    grad_combine = jnp.stack(combine_grads, axis=1)
    grad_probs = jnp.concatenate(
        [grad_combine * selected, jnp.zeros((count, NE - EW), jnp.float32)], axis=-1
    )
    grad_logits = router_probs * (
        grad_probs - jnp.sum(router_probs * grad_probs, axis=-1, keepdims=True)
    )
    logit_b = grad_logits.astype(jnp.bfloat16)
    grad_router = jnp.dot(normed_two.T, logit_b, preferred_element_type=jnp.float32)
    grad_normed = jnp.dot(logit_b, router_weight.T, preferred_element_type=jnp.float32)
    grad_shared_down = jnp.dot(shared_hidden.T, grad_out, preferred_element_type=jnp.float32)
    grad_sh = jnp.dot(grad_out, shared_down.T, preferred_element_type=jnp.float32)
    shared_act, shared_slope = silu_parts(shared_gpre)
    grad_sg = (grad_sh * shared_upre * shared_slope).astype(jnp.bfloat16)
    grad_su = (grad_sh * shared_act).astype(jnp.bfloat16)
    grad_shared_gate = jnp.dot(normed_two.T, grad_sg, preferred_element_type=jnp.float32)
    grad_shared_up = jnp.dot(normed_two.T, grad_su, preferred_element_type=jnp.float32)
    grad_normed = grad_normed + jnp.dot(grad_sg, shared_gate.T, preferred_element_type=jnp.float32)
    grad_normed = grad_normed + jnp.dot(grad_su, shared_up.T, preferred_element_type=jnp.float32)
    grad_normed = grad_normed + grad_routed
    grad_expert_gate = jnp.stack(gate_grads, axis=0)
    grad_expert_up = jnp.stack(up_grads, axis=0)
    grad_expert_down = jnp.stack(down_grads, axis=0)
    grad_mixer_gain = jnp.sum(grad_normed * hidden * scale_two, axis=0)
    scaled = grad_normed * mixer_gain.astype(jnp.float32)
    grad_hidden = (
        grad_float
        + scale_two * scaled
        - hidden * scale_two**3 * jnp.mean(scaled * hidden, axis=-1, keepdims=True)
    )
    return (
        grad_hidden,
        (
            grad_mixer_gain,
            grad_router,
            grad_shared_gate,
            grad_shared_up,
            grad_shared_down,
            grad_expert_gate,
            grad_expert_up,
            grad_expert_down,
        ),
    )


def attention_backward(grad_hidden, x_float, saved, attn_weights):
    norm_gain, query_weight, kv_down, kv_gain, kv_up, out_weight = attn_weights
    (
        normed_one,
        latent,
        scale_kv,
        latent_normed,
        cosine,
        sine,
        allowed,
        query_b,
        key_b,
        value_b,
        log_sum,
        attended,
    ) = saved
    count = x_float.shape[0]
    grad_hb = grad_hidden.astype(jnp.bfloat16)
    grad_out_weight = jnp.dot(attended.T, grad_hb, preferred_element_type=jnp.float32)
    grad_att = (
        jnp.dot(grad_hb, out_weight.T, preferred_element_type=jnp.float32)
        .astype(jnp.bfloat16)
        .reshape(count, H, DV)
    )
    scores = mixed_einsum("thd,shd->hts", query_b, key_b)
    scores = jnp.where(allowed[None], scores, NEGATIVE)
    probs_f = jnp.exp(scores - log_sum)
    probs_b = probs_f.astype(jnp.bfloat16)
    grad_values = mixed_einsum("hts,thd->shd", probs_b, grad_att)
    grad_probs = mixed_einsum("thd,shd->hts", grad_att, value_b)
    delta = jnp.sum(
        grad_att.astype(jnp.float32) * attended.astype(jnp.float32).reshape(count, H, DV), axis=-1
    ).T
    grad_scores = (probs_f * (grad_probs - delta[:, :, None])).astype(jnp.bfloat16)
    grad_q = mixed_einsum("hts,shd->thd", grad_scores, key_b) * (DN + DR) ** (-0.5)
    grad_k = mixed_einsum("hts,thd->shd", grad_scores, query_b)
    grad_qrot = unrotate(grad_q[..., DN:], cosine[:, None, :], sine[:, None, :])
    grad_qb = (
        jnp.concatenate([grad_q[..., :DN], grad_qrot], axis=-1)
        .reshape(count, H * (DN + DR))
        .astype(jnp.bfloat16)
    )
    grad_query = jnp.dot(normed_one.T, grad_qb, preferred_element_type=jnp.float32)
    grad_normed = jnp.dot(grad_qb, query_weight.T, preferred_element_type=jnp.float32)
    grad_krope = unrotate(jnp.sum(grad_k[..., DN:], axis=1), cosine, sine)
    grad_kvb = (
        jnp.concatenate([grad_k[..., :DN], grad_values], axis=-1)
        .reshape(count, H * (DN + DV))
        .astype(jnp.bfloat16)
    )
    grad_kv_up = jnp.dot(latent_normed.T, grad_kvb, preferred_element_type=jnp.float32)
    grad_latent_normed = jnp.dot(grad_kvb, kv_up.T, preferred_element_type=jnp.float32)
    grad_kv_gain = jnp.sum(grad_latent_normed * latent * scale_kv, axis=0)
    latent_scaled = grad_latent_normed * kv_gain.astype(jnp.float32)
    grad_latent = scale_kv * latent_scaled - latent * scale_kv**3 * jnp.mean(
        latent_scaled * latent, axis=-1, keepdims=True
    )
    grad_downb = jnp.concatenate([grad_latent, grad_krope], axis=-1).astype(jnp.bfloat16)
    grad_kv_down = jnp.dot(normed_one.T, grad_downb, preferred_element_type=jnp.float32)
    grad_normed = grad_normed + jnp.dot(grad_downb, kv_down.T, preferred_element_type=jnp.float32)
    scale_one = inv_rms(x_float)
    grad_norm_gain = jnp.sum(grad_normed * x_float * scale_one, axis=0)
    input_scaled = grad_normed * norm_gain.astype(jnp.float32)
    grad_input = (
        grad_hidden
        + scale_one * input_scaled
        - x_float * scale_one**3 * jnp.mean(input_scaled * x_float, axis=-1, keepdims=True)
    )
    return (
        grad_input,
        (grad_norm_gain, grad_query, grad_kv_down, grad_kv_gain, grad_kv_up, grad_out_weight),
    )


def local(
    hidden_in,
    segment_ids,
    routes,
    norm_gain,
    query_weight,
    kv_down,
    kv_gain,
    kv_up,
    out_weight,
    mixer_gain,
    router_weight,
    shared_gate,
    shared_up,
    shared_down,
    expert_gate,
    expert_up,
    expert_down,
    cotangent,
):
    x_float = hidden_in.astype(jnp.float32)
    attn_full = (
        lax.all_gather(norm_gain, "shard", axis=0, tiled=True),
        lax.all_gather(query_weight, "shard", axis=0, tiled=True),
        lax.all_gather(kv_down, "shard", axis=0, tiled=True),
        lax.all_gather(kv_gain, "shard", axis=0, tiled=True),
        lax.all_gather(kv_up, "shard", axis=1, tiled=True),
        lax.all_gather(out_weight, "shard", axis=0, tiled=True),
    )
    hidden, attn_saved = attention_forward(x_float, segment_ids, attn_full)
    moe_full = (
        lax.all_gather(mixer_gain, "shard", axis=0, tiled=True),
        lax.all_gather(router_weight, "shard", axis=0, tiled=True),
        lax.all_gather(shared_gate, "shard", axis=0, tiled=True),
        lax.all_gather(shared_up, "shard", axis=0, tiled=True),
        lax.all_gather(shared_down, "shard", axis=1, tiled=True),
        lax.all_gather(expert_gate, "shard", axis=1, tiled=True),
        lax.all_gather(expert_up, "shard", axis=1, tiled=True),
        lax.all_gather(expert_down, "shard", axis=2, tiled=True),
    )
    result, moe_saved = moe_forward(hidden, routes, moe_full)
    grad_hidden, moe_partials = moe_backward(cotangent, hidden, moe_saved, moe_full)
    part_mg, part_rw, part_sg, part_su, part_sd, part_eg, part_eu, part_ed = moe_partials
    moe_owned = (
        lax.psum_scatter(
            part_mg.astype(jnp.bfloat16), "shard", scatter_dimension=0, tiled=True
        ).astype(jnp.float32),
        lax.psum_scatter(
            part_rw.astype(jnp.bfloat16), "shard", scatter_dimension=0, tiled=True
        ).astype(jnp.float32),
        lax.psum_scatter(
            part_sg.astype(jnp.bfloat16), "shard", scatter_dimension=0, tiled=True
        ).astype(jnp.float32),
        lax.psum_scatter(
            part_su.astype(jnp.bfloat16), "shard", scatter_dimension=0, tiled=True
        ).astype(jnp.float32),
        lax.psum_scatter(
            part_sd.astype(jnp.bfloat16), "shard", scatter_dimension=1, tiled=True
        ).astype(jnp.float32),
        lax.psum_scatter(
            part_eg.astype(jnp.bfloat16), "shard", scatter_dimension=1, tiled=True
        ).astype(jnp.float32),
        lax.psum_scatter(
            part_eu.astype(jnp.bfloat16), "shard", scatter_dimension=1, tiled=True
        ).astype(jnp.float32),
        lax.psum_scatter(
            part_ed.astype(jnp.bfloat16), "shard", scatter_dimension=2, tiled=True
        ).astype(jnp.float32),
    )
    attn_back = (
        lax.all_gather(norm_gain, "shard", axis=0, tiled=True),
        lax.all_gather(query_weight, "shard", axis=0, tiled=True),
        lax.all_gather(kv_down, "shard", axis=0, tiled=True),
        lax.all_gather(kv_gain, "shard", axis=0, tiled=True),
        lax.all_gather(kv_up, "shard", axis=1, tiled=True),
        lax.all_gather(out_weight, "shard", axis=0, tiled=True),
    )
    grad_input, attn_partials = attention_backward(grad_hidden, x_float, attn_saved, attn_back)
    part_ng, part_qw, part_kd, part_kg, part_ku, part_ow = attn_partials
    attn_owned = (
        lax.psum_scatter(
            part_ng.astype(jnp.bfloat16), "shard", scatter_dimension=0, tiled=True
        ).astype(jnp.float32),
        lax.psum_scatter(
            part_qw.astype(jnp.bfloat16), "shard", scatter_dimension=0, tiled=True
        ).astype(jnp.float32),
        lax.psum_scatter(
            part_kd.astype(jnp.bfloat16), "shard", scatter_dimension=0, tiled=True
        ).astype(jnp.float32),
        lax.psum_scatter(
            part_kg.astype(jnp.bfloat16), "shard", scatter_dimension=0, tiled=True
        ).astype(jnp.float32),
        lax.psum_scatter(
            part_ku.astype(jnp.bfloat16), "shard", scatter_dimension=1, tiled=True
        ).astype(jnp.float32),
        lax.psum_scatter(
            part_ow.astype(jnp.bfloat16), "shard", scatter_dimension=0, tiled=True
        ).astype(jnp.float32),
    )
    own_ng, own_qw, own_kd, own_kg, own_ku, own_ow = attn_owned
    own_mg, own_rw, own_sg, own_su, own_sd, own_eg, own_eu, own_ed = moe_owned
    summed_all = (
        lax.psum(own_ng.astype(jnp.bfloat16), "replica").astype(jnp.float32),
        lax.psum(own_qw.astype(jnp.bfloat16), "replica").astype(jnp.float32),
        lax.psum(own_kd.astype(jnp.bfloat16), "replica").astype(jnp.float32),
        lax.psum(own_kg.astype(jnp.bfloat16), "replica").astype(jnp.float32),
        lax.psum(own_ku.astype(jnp.bfloat16), "replica").astype(jnp.float32),
        lax.psum(own_ow.astype(jnp.bfloat16), "replica").astype(jnp.float32),
        lax.psum(own_mg.astype(jnp.bfloat16), "replica").astype(jnp.float32),
        lax.psum(own_rw.astype(jnp.bfloat16), "replica").astype(jnp.float32),
        lax.psum(own_sg.astype(jnp.bfloat16), "replica").astype(jnp.float32),
        lax.psum(own_su.astype(jnp.bfloat16), "replica").astype(jnp.float32),
        lax.psum(own_sd.astype(jnp.bfloat16), "replica").astype(jnp.float32),
        lax.psum(own_eg.astype(jnp.bfloat16), "replica").astype(jnp.float32),
        lax.psum(own_eu.astype(jnp.bfloat16), "replica").astype(jnp.float32),
        lax.psum(own_ed.astype(jnp.bfloat16), "replica").astype(jnp.float32),
    )
    (
        own_ng,
        own_qw,
        own_kd,
        own_kg,
        own_ku,
        own_ow,
        own_mg,
        own_rw,
        own_sg,
        own_su,
        own_sd,
        own_eg,
        own_eu,
        own_ed,
    ) = summed_all
    return (
        result,
        grad_input,
        own_ng,
        own_qw,
        own_kd,
        own_kg,
        own_ku,
        own_ow,
        own_mg,
        own_rw,
        own_sg,
        own_su,
        own_sd,
        own_eg,
        own_eu,
        own_ed,
    )


def solution(mesh):
    placed = (
        P(("replica", "shard"), None),
        P(("replica", "shard")),
        P(("replica", "shard"), None),
        P("shard"),
        P("shard", None),
        P("shard", None),
        P("shard"),
        P(None, "shard"),
        P("shard", None),
        P("shard"),
        P("shard", None),
        P("shard", None),
        P("shard", None),
        P(None, "shard"),
        P(None, "shard", None),
        P(None, "shard", None),
        P(None, None, "shard"),
        P(("replica", "shard"), None),
    )
    return jax.shard_map(
        local,
        mesh=mesh,
        in_specs=placed,
        out_specs=(
            P(("replica", "shard"), None),
            P(("replica", "shard"), None),
            P("shard"),
            P("shard", None),
            P("shard", None),
            P("shard"),
            P(None, "shard"),
            P("shard", None),
            P("shard"),
            P("shard", None),
            P("shard", None),
            P("shard", None),
            P(None, "shard"),
            P(None, "shard", None),
            P(None, "shard", None),
            P(None, None, "shard"),
        ),
        check_vma=False,
    )
```

profile of v0, /device:TPU:0, one launch (start us, length us, event | category | flops | bytes accessed | tf_op | source)
XLA Modules:
  0.0 1971.9 jit_solution(7320207235084554191)
XLA Ops:
  14.1 13.7 all-gather
  29.4 14.5 all-reduce.1
  43.9 8.4 all-gather.1
  54.0 15.3 all_gather.58
  70.3 2.5 fusion.106
  73.7 20.8 %all-gather.15.cloned.1.call-done = bf16[512,4096]{1,0:T(8,128)(2,1)} async-done(((bf16[512,512]{1,0:T(8,128)(2,1)}), bf16[512,4096]{1,0:T(8,128)(2,1)}) %all-gather.15.cloned.1.call-update) | async-done | bytes 4194320 | tf_op jit(solution)/shard_map/all_gather | solution.py:366
  94.5 4.1 convolution_convert_fusion.9
  98.6 1.6 copy.87
  101.1 102.3 %all-gather.25.cloned.1.call-done = bf16[2816,2048]{1,0:T(8,128)(2,1)} async-done(((bf16[2816,256]{1,0:T(8,128)(2,1)}), bf16[2816,2048]{1,0:T(8,128)(2,1)}) %all-gather.25.cloned.1.call-update) | async-done | bytes 11534352 | tf_op jit(solution)/shard_map/all_gather | solution.py:375
  203.4 9.3 fusion.113
  212.7 107.1 %all-gather.17.cloned.1.call-done = bf16[2048,3072]{1,0:T(8,128)(2,1)} async-done(((bf16[256,3072]{1,0:T(8,128)(2,1)}), bf16[2048,3072]{1,0:T(8,128)(2,1)}) %all-gather.17.cloned.1.call-update) | async-done | bytes 12582928 | tf_op jit(solution)/shard_map/all_gather | solution.py:363
  319.8 8.2 fusion.104
  330.2 71.3 %all-gather.19.cloned.1.call-done = bf16[2048,2048]{1,0:T(8,128)(2,1)} async-done(((bf16[256,2048]{1,0:T(8,128)(2,1)}), bf16[2048,2048]{1,0:T(8,128)(2,1)}) %all-gather.19.cloned.1.call-update) | async-done | bytes 8388624 | tf_op jit(solution)/shard_map/all_gather | solution.py:367
  401.5 4.7 multiply_reduce_fusion.3
  408.1 53.8 %all-gather.27.cloned.1.call-done = bf16[1,2048,1408]{2,1,0:T(8,128)(2,1)} async-done(((bf16[1,256,1408]{2,1,0:T(8,128)(2,1)}), bf16[1,2048,1408]{2,1,0:T(8,128)(2,1)}) %all-gather.27.cloned.1.call-update) | async-done | bytes 5767184 | tf_op jit(solution)/shard_map/all_gather | solution.py:376
  461.9 3.5 fusion.13
  465.4 57.2 %all-gather.29.cloned.1.call-done = bf16[1,2048,1408]{2,1,0:T(8,128)(2,1)} async-done(((bf16[1,256,1408]{2,1,0:T(8,128)(2,1)}), bf16[1,2048,1408]{2,1,0:T(8,128)(2,1)}) %all-gather.29.cloned.1.call-update) | async-done | bytes 5767184 | tf_op jit(solution)/shard_map/all_gather | solution.py:377
  522.6 4.1 multiply_convert_fusion.8
  526.8 57.0 %all-gather.31.cloned.1.call-done = bf16[1,1408,2048]{2,1,0:T(8,128)(2,1)} async-done(((bf16[1,1408,256]{2,1,0:T(8,128)(2,1)}), bf16[1,1408,2048]{2,1,0:T(8,128)(2,1)}) %all-gather.31.cloned.1.call-update) | async-done | bytes 5767184 | tf_op jit(solution)/shard_map/all_gather | solution.py:378
  583.8 3.5 fusion.5
  590.4 101.3 %all-gather.23.cloned.1.call-done = bf16[2048,2816]{1,0:T(8,128)(2,1)} async-done(((bf16[256,2816]{1,0:T(8,128)(2,1)}), bf16[2048,2816]{1,0:T(8,128)(2,1)}) %all-gather.23.cloned.1.call-update) | async-done | bytes 11534352 | tf_op jit(solution)/shard_map/all_gather | solution.py:374
  691.7 7.0 fusion.112
  698.7 100.8 %all-gather.21.cloned.1.call-done = bf16[2048,2816]{1,0:T(8,128)(2,1)} async-done(((bf16[256,2816]{1,0:T(8,128)(2,1)}), bf16[2048,2816]{1,0:T(8,128)(2,1)}) %all-gather.21.cloned.1.call-update) | async-done | bytes 11534352 | tf_op jit(solution)/shard_map/all_gather | solution.py:373
  799.5 8.3 multiply_convert_fusion.1
  807.8 8.6 fusion.114
  816.6 4.0 fusion.115
  821.0 4.5 multiply_convert_fusion.7
  825.5 4.4 fusion.7
  829.9 1.6 fusion.17
  833.4 3.7 convolution_convert_fusion.11
  837.1 2.0 copy.69
  840.6 1.9 fusion.24
  842.5 1.9 fusion.23
  845.3 2.0 copy-done.14
  847.3 1.9 multiply_reduce_fusion.4
  850.2 2.3 convolution_convert_fusion.10
  852.5 4.5 convolution_convert_fusion.8
  857.9 4.8 fusion.2
  863.5 4.2 fusion
  868.4 4.3 fusion.1
  872.8 6.8 convolution_convert_fusion.7
  879.7 7.1 convolution_convert_fusion.2
  886.8 7.1 convolution_convert_fusion.1
  894.1 9.0 convolution_convert_fusion
  906.8 6.7 convolution_convert_fusion.3
  915.1 23.9 %reduce-scatter.16.cloned.1.call-done = bf16[512,512]{1,0:T(8,128)(2,1)} async-done(((bf16[512,4096]{1,0:T(8,128)(2,1)}), bf16[512,512]{1,0:T(8,128)(2,1)}) %reduce-scatter.16.cloned.1.call-update) | async-done | bytes 524304 | tf_op jit(solution)/shard_map/reduce_scatter | solution.py:432
  939.0 65.6 %reduce-scatter.32.cloned.1.call-done = bf16[1,1408,256]{2,1,0:T(8,128)(2,1)} async-done(((bf16[1,1408,2048]{2,1,0:T(8,128)(2,1)}), bf16[1,1408,256]{2,1,0:T(8,128)(2,1)}) %reduce-scatter.32.cloned.1.call-update) | async-done | bytes 720912 | tf_op jit(solution)/shard_map/reduce_scatter | solution.py:405
  1004.6 65.4 %reduce-scatter.28.cloned.1.call-done = bf16[1,256,1408]{2,1,0:T(8,128)(2,1)} async-done(((bf16[1,2048,1408]{2,1,0:T(8,128)(2,1)}), bf16[1,256,1408]{2,1,0:T(8,128)(2,1)}) %reduce-scatter.28.cloned.1.call-update) | async-done | bytes 720912 | tf_op jit(solution)/shard_map/reduce_scatter | solution.py:399
  1070.0 65.4 %reduce-scatter.30.cloned.1.call-done = bf16[1,256,1408]{2,1,0:T(8,128)(2,1)} async-done(((bf16[1,2048,1408]{2,1,0:T(8,128)(2,1)}), bf16[1,256,1408]{2,1,0:T(8,128)(2,1)}) %reduce-scatter.30.cloned.1.call-update) | async-done | bytes 720912 | tf_op jit(solution)/shard_map/reduce_scatter | solution.py:402
  1135.4 90.2 %reduce-scatter.18.cloned.1.call-done = bf16[256,2048]{1,0:T(8,128)(2,1)} async-done(((bf16[2048,2048]{1,0:T(8,128)(2,1)}), bf16[256,2048]{1,0:T(8,128)(2,1)}) %reduce-scatter.18.cloned.1.call-update) | async-done | bytes 1048592 | tf_op jit(solution)/shard_map/reduce_scatter | solution.py:435
  1225.6 119.9 %reduce-scatter.22.cloned.1.call-done = bf16[256,2816]{1,0:T(8,128)(2,1)} async-done(((bf16[2048,2816]{1,0:T(8,128)(2,1)}), bf16[256,2816]{1,0:T(8,128)(2,1)}) %reduce-scatter.22.cloned.1.call-update) | async-done | bytes 1441808 | tf_op jit(solution)/shard_map/reduce_scatter | solution.py:390
  1345.4 119.9 %reduce-scatter.24.cloned.1.call-done = bf16[256,2816]{1,0:T(8,128)(2,1)} async-done(((bf16[2048,2816]{1,0:T(8,128)(2,1)}), bf16[256,2816]{1,0:T(8,128)(2,1)}) %reduce-scatter.24.cloned.1.call-update) | async-done | bytes 1441808 | tf_op jit(solution)/shard_map/reduce_scatter | solution.py:393
  1465.3 120.0 %reduce-scatter.26.cloned.1.call-done = bf16[2816,256]{1,0:T(8,128)(2,1)} async-done(((bf16[2816,2048]{1,0:T(8,128)(2,1)}), bf16[2816,256]{1,0:T(8,128)(2,1)}) %reduce-scatter.26.cloned.1.call-update) | async-done | bytes 1441808 | tf_op jit(solution)/shard_map/reduce_scatter | solution.py:396
  1585.4 129.8 %reduce-scatter.12.cloned.1.call-done = bf16[256,3072]{1,0:T(8,128)(2,1)} async-done(((bf16[2048,3072]{1,0:T(8,128)(2,1)}), bf16[256,3072]{1,0:T(8,128)(2,1)}) %reduce-scatter.12.cloned.1.call-update) | async-done | bytes 1572880 | tf_op jit(solution)/shard_map/reduce_scatter | solution.py:423
  1716.5 9.3 fusion.116
  1725.9 1.8 fusion.34
  1727.7 14.5 all-reduce.5
  1742.5 6.3 convolution_add_fusion.4
  1751.5 19.1 all-reduce.6
  1773.0 175.8 %all-reduce.10.cloned.1.call-done = (bf16[256,3072]{1,0:T(8,128)(2,1)}, bf16[256,576]{0,1:T(8,128)(2,1)}, bf16[512,512]{1,0:T(8,128)(2,1)}, bf16[256,2048]{1,0:T...) async-done(((bf16[256,3072]{1,0:T(8,128)(2,1)}, ...) | async-done | bytes 9928720 | tf_op jit(solution)/shard_map/psum | solution.py:443
  1948.7 3.6 convert_element_type.306
  1952.3 1.8 convert_element_type.320
  1954.1 1.8 convert_element_type.322
  1955.9 1.8 convert_element_type.324
  (341 shorter events, 44.7 us)
Async XLA Ops:
  7.2 63.1 %all-gather.13.cloned.1.call-start = ((), (), s32[]{:S(2)}) async-start(), calls=%async_computation.11 | async-start | bytes 2654208 | tf_op jit(solution)/shard_map/all_gather | solution.py:364
  7.9 86.6 %all-gather.15.cloned.1.call-start = ((), (), s32[]{:S(2)}) async-start(), calls=%async_computation.12 | async-start | bytes 4718592 | tf_op jit(solution)/shard_map/all_gather | solution.py:366
  8.7 194.7 %all-gather.25.cloned.1.call-start = ((), (), s32[]{:S(2)}) async-start(), calls=%async_computation.17 | async-start | bytes 12976128 | tf_op jit(solution)/shard_map/all_gather | solution.py:375
  9.4 18.4 copy-start.92
  9.4 19.7 copy-start.100
  9.4 34.4 %copy-start.101 = (bf16[256]{0:T(256)(128)(2,1)S(1)}, bf16[256]{0:T(256)(128)(2,1)}, u32[]{:S(2)}) copy-start(bf16[256]{0:T(256)(128)(2,1)} %param.27) | copy-start | bytes 1540
  9.4 42.9 %copy-start.90 = (s32[128,6]{0,1:T(8,128)S(1)}, s32[128,6]{0,1:T(8,128)}, u32[]{:S(2)}) copy-start(s32[128,6]{0,1:T(8,128)} %param.20) | copy-start | bytes 9220
  9.5 43.8 %copy-start.91 = (s32[128]{0:T(128)S(1)}, s32[128]{0:T(128)}, u32[]{:S(2)}) copy-start(s32[128]{0:T(128)} %param.19) | copy-start | bytes 1540
  9.5 44.5 %copy-start.65 = (bf16[256,64]{0,1:T(8,128)(2,1)S(1)}, bf16[256,64]{0,1:T(8,128)(2,1)}, u32[]{:S(2)}) copy-start(bf16[256,64]{0,1:T(8,128)(2,1)} %param.28) | copy-start | bytes 98308
  9.5 59.9 %copy-start = (bf16[128,2048]{1,0:T(8,128)(2,1)S(1)}, bf16[128,2048]{1,0:T(8,128)(2,1)}, u32[]{:S(2)}) copy-start(bf16[128,2048]{1,0:T(8,128)(2,1)} %param.18) | copy-start | bytes 1572868
  9.5 310.4 %all-gather.17.cloned.1.call-start = ((), (), s32[]{:S(2)}) async-start(), calls=%async_computation.13 | async-start | bytes 14155776 | tf_op jit(solution)/shard_map/all_gather | solution.py:363
  10.1 391.5 %all-gather.19.cloned.1.call-start = ((), (), s32[]{:S(2)}) async-start(), calls=%async_computation.14 | async-start | bytes 9437184 | tf_op jit(solution)/shard_map/all_gather | solution.py:367
  10.6 451.3 %all-gather.27.cloned.1.call-start = ((), (), s32[]{:S(2)}) async-start(), calls=%async_computation.18 | async-start | bytes 6488064 | tf_op jit(solution)/shard_map/all_gather | solution.py:376
  11.2 511.4 %all-gather.29.cloned.1.call-start = ((), (), s32[]{:S(2)}) async-start(), calls=%async_computation.19 | async-start | bytes 6488064 | tf_op jit(solution)/shard_map/all_gather | solution.py:377
  12.0 571.8 %all-gather.31.cloned.1.call-start = ((), (), s32[]{:S(2)}) async-start(), calls=%async_computation.20 | async-start | bytes 6488064 | tf_op jit(solution)/shard_map/all_gather | solution.py:378
  12.7 678.9 %all-gather.23.cloned.1.call-start = ((), (), s32[]{:S(2)}) async-start(), calls=%async_computation.16 | async-start | bytes 12976128 | tf_op jit(solution)/shard_map/all_gather | solution.py:374
  13.5 786.0 %all-gather.21.cloned.1.call-start = ((), (), s32[]{:S(2)}) async-start(), calls=%async_computation.15 | async-start | bytes 12976128 | tf_op jit(solution)/shard_map/all_gather | solution.py:373
  14.0 901.1 %reduce-scatter.14.cloned.1.call-start = ((), (), s32[]{:S(2)}) async-start(), calls=%async_computation.22 | async-start | bytes 2654208 | tf_op jit(solution)/shard_map/reduce_scatter | solution.py:426
  43.9 54.7 %copy-start.54 = (f32[512]{0:T(512)}, f32[512]{0:T(512)S(1)}, u32[]{:S(2)}) copy-start(f32[512]{0:T(512)S(1)} %convert_element_type.270) | copy-start | bytes 6148
  52.4 20.6 %copy-start.96 = (pred[128]{0:T(512)(128)(4,1)}, pred[128]{0:T(512)(128)(4,1)S(1)}, u32[]{:S(2)}) copy-start(pred[128]{0:T(512)(128)(4,1)S(1)} %compare_reduce_fusion) | copy-start | bytes 388
  53.3 19.7 %copy-start.84 = (f32[32]{0:T(128)}, f32[32]{0:T(128)S(1)}, u32[]{:S(2)}) copy-start(f32[32]{0:T(128)S(1)} %multiply_power_fusion) | copy-start | bytes 388
  69.3 338.2 %copy-start.17 = (bf16[2048,64]{0,1:T(8,128)(2,1)}, bf16[2048,64]{0,1:T(8,128)(2,1)S(1)}, u32[]{:S(2)}) copy-start(bf16[2048,64]{0,1:T(8,128)(2,1)S(1)} %all_gather.58) | copy-start | bytes 786436
  69.5 29.0 %copy-start.86 = (f32[128]{0:T(128)}, f32[128]{0:T(128)S(1)}, u32[]{:S(2)}) copy-start(f32[128]{0:T(128)S(1)} %subtract_convert_fusion.2) | copy-start | bytes 1540
  70.1 249.8 %copy-start.66 = (f32[128]{0:T(128)}, f32[128]{0:T(128)S(1)}, u32[]{:S(2)}) copy-start(f32[128]{0:T(128)S(1)} %get-tuple-element.59) | copy-start | bytes 1540
  70.3 257.9 %copy-start.50 = (f32[128,32]{0,1:T(8,128)}, f32[128,32]{0,1:T(8,128)S(1)}, u32[]{:S(2)}) copy-start(f32[128,32]{0,1:T(8,128)S(1)} %get-tuple-element.54) | copy-start | bytes 49156
  70.3 257.9 %copy-start.52 = (f32[128,32]{0,1:T(8,128)}, f32[128,32]{0,1:T(8,128)S(1)}, u32[]{:S(2)}) copy-start(f32[128,32]{0,1:T(8,128)S(1)} %get-tuple-element.55) | copy-start | bytes 49156
  73.7 27.4 %copy-start.75 = (f32[128]{0:T(128)}, f32[128]{0:T(128)S(1)}, u32[]{:S(2)}) copy-start(f32[128]{0:T(128)S(1)} %get-tuple-element.61) | copy-start | bytes 1540
  94.5 108.9 %copy-start.4 = (bf16[128,2048]{1,0:T(8,128)(2,1)S(1)}, bf16[128,2048]{1,0:T(8,128)(2,1)}, u32[]{:S(2)}) copy-start(bf16[128,2048]{1,0:T(8,128)(2,1)} %param.35) | copy-start | bytes 1572868
  100.2 112.5 %copy-start.12 = (bf16[128,4096]{0,1:T(8,128)(2,1)}, bf16[128,4096]{0,1:T(8,128)(2,1)S(1)}, u32[]{:S(2)}) copy-start(bf16[128,4096]{0,1:T(8,128)(2,1)S(1)} %copy.87) | copy-start | bytes 3145732
  319.8 8.5 copy-start.19
  328.9 77.4 %copy-start.61 = (f32[16,128]{1,0:T(8,128)}, f32[16,128]{1,0:T(8,128)S(1)}, u32[]{:S(2)}) copy-start(f32[16,128]{1,0:T(8,128)S(1)} %get-tuple-element.66) | copy-start | bytes 24580
  329.9 76.4 %copy-start.63 = (f32[16,128]{1,0:T(8,128)}, f32[16,128]{1,0:T(8,128)S(1)}, u32[]{:S(2)}) copy-start(f32[16,128]{1,0:T(8,128)S(1)} %fusion.35) | copy-start | bytes 24580
  330.2 76.1 %copy-start.1 = (bf16[16,128,128]{2,1,0:T(8,128)(2,1)}, bf16[16,128,128]{2,1,0:T(8,128)(2,1)S(1)}, u32[]{:S(2)}) copy-start(bf16[16,128,128]{2,1,0:T(8,128)(2,1)S(1)} %convolution_convert_fusion.15) | copy-start | bytes 1572868
  465.4 118.3 %copy-start.36 = (f32[16,1408]{1,0:T(8,128)}, f32[16,1408]{1,0:T(8,128)S(1)}, u32[]{:S(2)}) copy-start(f32[16,1408]{1,0:T(8,128)S(1)} %fusion.13) | copy-start | bytes 270340
  526.8 171.9 %copy-start.41 = (bf16[16,1408]{1,0:T(8,128)(2,1)}, bf16[16,1408]{1,0:T(8,128)(2,1)S(1)}, u32[]{:S(2)}) copy-start(bf16[16,1408]{1,0:T(8,128)(2,1)S(1)} %get-tuple-element.70) | copy-start | bytes 135172
  526.8 61.4 %copy-start.97 = (pred[128]{0:T(512)(128)(4,1)S(1)}, pred[128]{0:T(512)(128)(4,1)}, u32[]{:S(2)}) copy-start(pred[128]{0:T(512)(128)(4,1)} %copy-done.96) | copy-start | bytes 388
  526.8 63.0 %copy-start.62 = (f32[16,128]{1,0:T(8,128)S(1)}, f32[16,128]{1,0:T(8,128)}, u32[]{:S(2)}) copy-start(f32[16,128]{1,0:T(8,128)} %copy-done.61) | copy-start | bytes 24580
  526.8 63.0 %copy-start.64 = (f32[16,128]{1,0:T(8,128)S(1)}, f32[16,128]{1,0:T(8,128)}, u32[]{:S(2)}) copy-start(f32[16,128]{1,0:T(8,128)} %copy-done.63) | copy-start | bytes 24580
  587.2 111.5 %copy-start.27 = (f32[16,2048]{1,0:T(8,128)}, f32[16,2048]{1,0:T(8,128)S(1)}, u32[]{:S(2)}) copy-start(f32[16,2048]{1,0:T(8,128)S(1)} %fusion.5) | copy-start | bytes 393220
  588.4 110.3 %copy-start.79 = (f32[128,1]{0,1:T(1,128)}, f32[128,1]{0,1:T(1,128)S(1)}, u32[]{:S(2)}) copy-start(f32[128,1]{0,1:T(1,128)S(1)} %fusion.26) | copy-start | bytes 1540
  799.5 17.0 slice-start
  799.5 17.0 slice-start.1
  807.8 8.6 copy-start.16
  807.8 8.7 copy-start.15
  807.8 8.7 slice-start.2
  820.6 9.3 slice-start.5
  821.0 8.9 slice-start.6
  825.5 7.9 slice-start.3
  852.5 86.5 %reduce-scatter.16.cloned.1.call-start = ((), (), s32[]{:S(2)}) async-start(), calls=%async_computation.23 | async-start | bytes 4718592 | tf_op jit(solution)/shard_map/reduce_scatter | solution.py:432
  857.1 147.5 %reduce-scatter.32.cloned.1.call-start = ((), (), s32[]{:S(2)}) async-start(), calls=%async_computation.31 | async-start | bytes 6488064 | tf_op jit(solution)/shard_map/reduce_scatter | solution.py:405
  862.7 207.3 %reduce-scatter.28.cloned.1.call-start = ((), (), s32[]{:S(2)}) async-start(), calls=%async_computation.29 | async-start | bytes 6488064 | tf_op jit(solution)/shard_map/reduce_scatter | solution.py:399
  867.7 267.7 %reduce-scatter.30.cloned.1.call-start = ((), (), s32[]{:S(2)}) async-start(), calls=%async_computation.30 | async-start | bytes 6488064 | tf_op jit(solution)/shard_map/reduce_scatter | solution.py:402
  872.8 352.8 %reduce-scatter.18.cloned.1.call-start = ((), (), s32[]{:S(2)}) async-start(), calls=%async_computation.24 | async-start | bytes 9437184 | tf_op jit(solution)/shard_map/reduce_scatter | solution.py:435
  879.6 465.8 %reduce-scatter.22.cloned.1.call-start = ((), (), s32[]{:S(2)}) async-start(), calls=%async_computation.26 | async-start | bytes 12976128 | tf_op jit(solution)/shard_map/reduce_scatter | solution.py:390
  886.8 578.6 %reduce-scatter.24.cloned.1.call-start = ((), (), s32[]{:S(2)}) async-start(), calls=%async_computation.27 | async-start | bytes 12976128 | tf_op jit(solution)/shard_map/reduce_scatter | solution.py:393
  893.9 691.5 %reduce-scatter.26.cloned.1.call-start = ((), (), s32[]{:S(2)}) async-start(), calls=%async_computation.28 | async-start | bytes 12976128 | tf_op jit(solution)/shard_map/reduce_scatter | solution.py:396
  903.1 812.1 %reduce-scatter.12.cloned.1.call-start = ((), (), s32[]{:S(2)}) async-start(), calls=%async_computation.21 | async-start | bytes 14155776 | tf_op jit(solution)/shard_map/reduce_scatter | solution.py:423
  913.5 838.1 %reduce-scatter.20.cloned.1.call-start = ((), (), s32[]{:S(2)}) async-start(), calls=%async_computation.25 | async-start | bytes 294912 | tf_op jit(solution)/shard_map/reduce_scatter | solution.py:387
  915.1 1033.7 %all-reduce.10.cloned.1.call-start = ((), (), s32[]{:S(2)}) async-start(), calls=%async_computation.32 | async-start | bytes 19857408 | tf_op jit(solution)/shard_map/psum | solution.py:443
  1716.5 9.3 copy-start.2
  1716.5 9.3 copy-start.24
  1716.5 9.3 copy-start.57
  1716.5 9.3 copy-start.59
  1742.5 7.8 copy-start.8
  (67 other events, 226.5 us)
Sparse Core Ops, SparseCore 0:
  9.6 35.6 all-gather.12
  46.9 47.5 all-gather.14
  96.1 107.2 all-gather.24
  204.9 114.8 all-gather.16
  321.3 80.2 all-gather.18
  403.0 58.8 all-gather.26
  463.6 59.0 all-gather.28
  524.2 59.4 all-gather.30
  585.4 106.2 all-gather.22
  693.2 106.2 all-gather.20
  852.6 35.2 reduce-scatter.13
  890.1 48.8 reduce-scatter.15
  941.3 63.2 reduce-scatter.31
  1006.7 63.2 reduce-scatter.27
  1072.1 63.2 reduce-scatter.29
  1137.6 87.9 reduce-scatter.17
  1227.7 117.6 reduce-scatter.21
  1347.6 117.6 reduce-scatter.23
  1467.6 117.6 reduce-scatter.25
  1587.5 127.6 reduce-scatter.11
  1718.0 29.2 reduce-scatter.19
  1752.7 195.9 all-reduce.9
where the time goes:
time: 1980 us; the launch traced here: 1970 us
  waiting for transfers between devices  1650 us (83%)
  matrix products  171 us (9%)
  blocking collectives  85.6 us (4%)
  other arithmetic  27.4 us (1%)
    psum x1, waiting for transfers between devices, local(): lax.psum(own_qw.astype(jnp.bfloat16), 'replica').astype(jnp.float32)  176 us
    reduce_scatter x1, waiting for transfers between devices, local(): lax.psum_scatter(part_qw.astype(jnp.bfloat16), 'shard', scatter_dimension...  130 us
    reduce_scatter x1, waiting for transfers between devices, local(): lax.psum_scatter(part_sd.astype(jnp.bfloat16), 'shard', scatter_dimension...  120 us
    reduce_scatter x1, waiting for transfers between devices, local(): lax.psum_scatter(part_su.astype(jnp.bfloat16), 'shard', scatter_dimension...  120 us
    reduce_scatter x1, waiting for transfers between devices, local(): lax.psum_scatter(part_sg.astype(jnp.bfloat16), 'shard', scatter_dimension...  120 us
    all_gather x1, waiting for transfers between devices, local(): lax.all_gather(query_weight, 'shard', axis=0, tiled=True)  107 us
    all_gather x1, waiting for transfers between devices, local(): lax.all_gather(shared_down, 'shard', axis=1, tiled=True)  102 us
    all_gather x1, waiting for transfers between devices, local(): lax.all_gather(shared_up, 'shard', axis=0, tiled=True)  101 us
  transfers between devices with their start and end apart: 22, of which 19 were waited for; matrix products, arithmetic and copies ran while one was open for 7% of the time, Pallas kernels for 0%

commit v1 on v0

v1 whole, which is shorter than its diff:
```python
import jax
import jax.numpy as jnp
from jax import lax
from jax.experimental import pallas as pl
from jax.experimental.layout import Layout, with_layout_constraint
from jax.experimental.pallas import tpu as pltpu
from jax.sharding import PartitionSpec as P

D = 2048
H = 16
DN = 128
DR = 64
DV = 128
KVR = 512
NE = 64
CAP = 16
FF = 1408
SH = 2816
TOK = 128

EPSILON = 1e-06
NEGATIVE = -1e30
BF = jnp.bfloat16
F32 = jnp.float32
SCALE = (DN + DR) ** (-0.5)


def dot(left, right):
    return jnp.dot(left, right, preferred_element_type=F32)


def dot_t(left, right):
    return lax.dot_general(left, right, (((1,), (1,)), ((), ())), preferred_element_type=F32)


def t_dot(left, right):
    return lax.dot_general(left, right, (((0,), (0,)), ((), ())), preferred_element_type=F32)


def ein(form, left, right):
    return jnp.einsum(form, left, right, preferred_element_type=F32)


def inv_rms(values):
    return lax.rsqrt(jnp.mean(values * values, axis=-1, keepdims=True) + EPSILON)


def silu_parts(pre_act):
    sigmoid_val = jax.nn.sigmoid(pre_act)
    return (pre_act * sigmoid_val, sigmoid_val * (1.0 + pre_act * (1.0 - sigmoid_val)))


def by_rows(values):
    return with_layout_constraint(values, Layout(major_to_minor=(0, 1)))


def fold(values, rows):
    n, c = values.shape
    f = rows // n
    if f <= 1:
        return values
    return values.reshape(n, f, c // f).transpose(1, 0, 2).reshape(rows, c // f)


def unfold(values, rows):
    n, c = values.shape
    f = n // rows
    if f <= 1:
        return values
    return values.reshape(f, rows, c).transpose(1, 0, 2).reshape(rows, f * c)


def roll_sum(values):
    values = values + pltpu.roll(values, 64, 1)
    return values + pltpu.roll(values, 32, 1)


def lane_index():
    return lax.broadcasted_iota(jnp.int32, (TOK, 128), 1)


def attention_kernel(R, HR, q_ref, rope_ref, kv_ref, cos_ref, sin_ref, bias_ref, out_w_ref,
                     att_ref, probs_ref, qb_ref, krb_ref, *part_refs):
    HN = HR * DN
    lane = lane_index()
    cos, sin = cos_ref[...], sin_ref[...]
    rope = rope_ref[...]
    k_1 = roll_sum(jnp.where(lane < 32, rope, 0.0))
    k_2 = roll_sum(jnp.where((lane >= 32) & (lane < 64), rope, 0.0))
    kr_1 = (k_1 * cos - k_2 * sin).astype(BF)
    kr_2 = (k_2 * cos + k_1 * sin).astype(BF)
    krb_ref[:, :128] = kr_1
    krb_ref[:, 128:] = kr_2
    q_1, q_2 = q_ref[:, HN : HN + 128], q_ref[:, HN + 128 :]
    qr_1 = (q_1 * cos - q_2 * sin) * SCALE
    qr_2 = (q_2 * cos + q_1 * sin) * SCALE
    q_n = (q_ref[:, :HN] * SCALE).astype(BF)
    qb_ref[:, :HN] = q_n
    qb_ref[:, HN : HN + 128] = qr_1.astype(BF)
    qb_ref[:, HN + 128 :] = qr_2.astype(BF)
    bias = bias_ref[0]
    for h in range(HR):
        head = (lane >= 32 * h) & (lane < 32 * h + 32)
        scores = (
            dot_t(q_n[:, h * DN : (h + 1) * DN], kv_ref[:, h * DN : (h + 1) * DN])
            + dot_t(jnp.where(head, qr_1, 0.0).astype(BF), kr_1)
            + dot_t(jnp.where(head, qr_2, 0.0).astype(BF), kr_2)
            + bias
        )
        expd = jnp.exp(scores - jnp.max(scores, axis=-1, keepdims=True))
        probs = expd / jnp.sum(expd, axis=-1, keepdims=True)
        probs_ref[h] = probs
        value = kv_ref[:, HN + h * DV : HN + (h + 1) * DV]
        att_ref[:, h * DV : (h + 1) * DV] = dot(probs.astype(BF), value).astype(BF)
    part = dot(att_ref[...], out_w_ref[...]).astype(BF)
    for k in range(R):

        @pl.when(pl.program_id(0) == k)
        def _():
            part_refs[k][...] = part


def attention_grad_kernel(R, HR, *refs):
    grad_refs = refs[:R]
    (att_ref, probs_ref, kv_ref, qb_ref, krb_ref, cos_ref, sin_ref, out_w_ref, kvu_ref,
     gq_ref, gkv_ref) = refs[R : R + 11]
    glat_refs = refs[R + 11 : 2 * R + 11]
    ghb_ref = refs[2 * R + 11]
    HN = HR * DN
    step = pl.program_id(0)
    for k in range(R):

        @pl.when(step == k)
        def _():
            ghb_ref[...] = grad_refs[k][...]

    ghb = ghb_ref[...]
    g_att = dot_t(ghb, out_w_ref[...]).astype(BF)
    lane = lane_index()
    cos, sin = cos_ref[...], sin_ref[...]
    kr_1, kr_2 = krb_ref[:, :128], krb_ref[:, 128:]
    qr_1 = qb_ref[:, HN : HN + 128].astype(F32)
    qr_2 = qb_ref[:, HN + 128 :].astype(F32)
    zero = jnp.zeros((TOK, 128), F32)
    gq_1, gq_2, gk_1, gk_2 = zero, zero, zero, zero
    for h in range(HR):
        cut = slice(h * DN, (h + 1) * DN)
        cut_v = slice(HN + h * DV, HN + (h + 1) * DV)
        head = (lane >= 32 * h) & (lane < 32 * h + 32)
        ga = g_att[:, cut]
        probs = probs_ref[h]
        gkv_ref[:, cut_v] = t_dot(probs.astype(BF), ga).astype(BF)
        delta = jnp.sum(ga.astype(F32) * att_ref[:, cut].astype(F32), axis=-1, keepdims=True)
        gs = (probs * (dot_t(ga, kv_ref[:, cut_v]) - delta)).astype(BF)
        gq_ref[:, cut] = (dot(gs, kv_ref[:, cut]) * SCALE).astype(BF)
        gq_1 = gq_1 + jnp.where(head, dot(gs, kr_1), 0.0)
        gq_2 = gq_2 + jnp.where(head, dot(gs, kr_2), 0.0)
        gkv_ref[:, cut] = t_dot(gs, qb_ref[:, cut]).astype(BF)
        gk_1 = gk_1 + t_dot(gs, jnp.where(head, qr_1, 0.0).astype(BF))
        gk_2 = gk_2 + t_dot(gs, jnp.where(head, qr_2, 0.0).astype(BF))
    gq_ref[:, HN : HN + 128] = ((gq_1 * cos + gq_2 * sin) * SCALE).astype(BF)
    gq_ref[:, HN + 128 :] = ((gq_2 * cos - gq_1 * sin) * SCALE).astype(BF)
    u_1, u_2 = roll_sum(gk_1), roll_sum(gk_2)
    r_1, r_2 = u_1 * cos + u_2 * sin, u_2 * cos - u_1 * sin
    g_rope = jnp.where(lane < 32, r_1, jnp.where(lane < 64, r_2, 0.0)).astype(BF)
    g_lat = dot_t(gkv_ref[...], kvu_ref[...]).astype(BF)
    for k in range(R):

        @pl.when(step == k)
        def _():
            glat_refs[k][:, :KVR] = g_lat
            glat_refs[k][:, KVR:] = g_rope


def exact_dot(left, right):
    return jnp.dot(left, right, precision=lax.Precision.HIGHEST, preferred_element_type=F32)


REP, SHD = "replica", "shard"


STEPS = 4
CHUNK = D // STEPS


def ffn_grad_kernel(R, SR, FR, cot_ref, rest_ref, in_ref, act_ref, slope_ref, e_hid_ref, e_act_ref,
                    e_slope_ref, rows_geo_ref, rows_g_ref, spread_ref, probs_ref, chosen_ref,
                    router_ref, geg_ref, e_geg_ref, rows_out_ref, gc_ref, *refs):
    part_refs = refs[:R]
    acc_ref, e_acc_ref, gc_acc_ref, lg_ref = refs[R:]
    step = pl.program_id(0)

    @pl.when(step < STEPS)
    def _():
        w_edt = rest_ref[:, SR:]
        s_gh = dot(cot_ref[...], rest_ref[:, :SR])
        e_gh = dot(rows_geo_ref[...], w_edt)
        rows_out = dot_t(e_hid_ref[...], w_edt)
        rows_out_ref[...] = rows_out
        gc_rows = jnp.sum(rows_g_ref[...] * rows_out, axis=-1, keepdims=True)
        gc_rows = jnp.broadcast_to(gc_rows, gc_acc_ref.shape)

        @pl.when(step == 0)
        def _():
            acc_ref[...] = s_gh
            e_acc_ref[...] = e_gh
            gc_acc_ref[...] = gc_rows

        @pl.when(step > 0)
        def _():
            acc_ref[...] += s_gh
            e_acc_ref[...] += e_gh
            gc_acc_ref[...] += gc_rows

    @pl.when(step == STEPS - 1)
    def _():
        s_gh = acc_ref[...]
        geg_ref[:, :SR] = (s_gh * slope_ref[...]).astype(BF)
        geg_ref[:, SR:] = (s_gh * act_ref[...]).astype(BF)
        e_gh = e_acc_ref[...]
        e_geg_ref[:, :FR] = (e_gh * e_slope_ref[...]).astype(BF)
        e_geg_ref[:, FR:] = (e_gh * e_act_ref[...]).astype(BF)
        for k in range(R):
            tok, row = slice(k * TOK, (k + 1) * TOK), slice(k * CAP, (k + 1) * CAP)
            gc = exact_dot(spread_ref[tok, :], gc_acc_ref[row, :])
            gc_ref[tok, :] = gc
            p = (gc * chosen_ref[tok, :])[:, :NE]
            probs = probs_ref[tok, :]
            first = lax.broadcasted_iota(jnp.int32, (TOK, NE), 1) == 0
            lg = probs * (jnp.where(first, p, 0.0) - probs[:, :1] * p)
            lg_ref[tok, :] = lg.astype(BF)

    @pl.when(step >= STEPS)
    def _():
        g_n2 = dot_t(geg_ref[...], in_ref[:, : 2 * SR]) + dot_t(lg_ref[...], router_ref[...])
        rows_back = dot_t(e_geg_ref[...], in_ref[:, 2 * SR :])
        for k in range(R):
            tok, row = slice(k * TOK, (k + 1) * TOK), slice(k * CAP, (k + 1) * CAP)
            part = g_n2[tok] + exact_dot(spread_ref[tok, :], rows_back[row])
            part_refs[k][...] = part.astype(BF)


def ffn_out_kernel(R, SR, s_hid_ref, rest_ref, spread_ref, rows_w_ref, rows_out_ref, *part_refs):
    w_sdt = rest_ref[:, :SR]
    for k in range(R):
        tok, row = slice(k * TOK, (k + 1) * TOK), slice(k * CAP, (k + 1) * CAP)
        part = dot_t(s_hid_ref[tok, :], w_sdt) + exact_dot(
            spread_ref[tok, :], rows_w_ref[row, :] * rows_out_ref[row, :]
        )
        part_refs[k][...] = part.astype(BF)


def add_kernel(hidden_ref, *refs):
    total = hidden_ref[...]
    for ref in refs[:-1]:
        total = total + ref[...].astype(F32)
    refs[-1][...] = total.astype(BF)


def ffn_weight_kernel(SR, FR, n2_ref, geg_ref, rows_in_ref, e_geg_ref, rows_geo_ref, e_hid_ref, out_ref):
    cut = 2 * SR + 2 * FR
    out_ref[:, : 2 * SR] = t_dot(n2_ref[...], geg_ref[...]).astype(BF)
    out_ref[:, 2 * SR : cut] = t_dot(rows_in_ref[...], e_geg_ref[...]).astype(BF)
    out_ref[:, cut:] = t_dot(rows_geo_ref[...], e_hid_ref[...]).astype(BF)


def product_kernel(left_ref, right_ref, out_ref):
    out_ref[...] = t_dot(left_ref[...], right_ref[...]).astype(BF)


def attention_weight_kernel(R, QW, r_ref, n1_ref, gq_ref, *refs):
    grad_refs, att_refs = refs[:R], refs[R : 2 * R]
    out_ref, ghb_ref, att_ref = refs[2 * R :]
    step = pl.program_id(0)

    @pl.when(step == 0)
    def _():
        for k in range(R):
            ghb_ref[k * TOK : (k + 1) * TOK, :] = grad_refs[k][...]

    for k in range(R):

        @pl.when((r_ref[0] ^ step) == k)
        def _():
            for i in range(R):
                att_ref[i * TOK : (i + 1) * TOK, :] = att_refs[k][
                    (i ^ k) * TOK : ((i ^ k) + 1) * TOK, :
                ]

    out_ref[:, :QW] = t_dot(n1_ref[...], gq_ref[...]).astype(BF)
    out_ref[:, QW:] = t_dot(att_ref[...], ghb_ref[...]).astype(BF)


def whole_block(shape):
    return pl.BlockSpec(shape, lambda *_: (0,) * len(shape))


def join_ffn_kernel(R, SR, FR, blocks, gate_ref, up_ref, e_gate_ref, e_up_ref, e_down_ref):
    cut = 2 * SR
    for j in range(R):
        gate_ref[:, j * SR : (j + 1) * SR] = blocks[j, :, :SR].astype(F32)
        up_ref[:, j * SR : (j + 1) * SR] = blocks[j, :, SR:cut].astype(F32)
        e_gate_ref[:, j * FR : (j + 1) * FR] = blocks[j, :, cut : cut + FR].astype(F32)
        e_up_ref[:, j * FR : (j + 1) * FR] = blocks[j, :, cut + FR : cut + 2 * FR].astype(F32)
        e_down_ref[j * FR : (j + 1) * FR, :] = blocks[j, :, cut + 2 * FR :].astype(F32).T


def join_down_kernel(R, SR, blocks, down_ref):
    for j in range(R):
        down_ref[j * SR : (j + 1) * SR, :] = blocks[j].astype(F32).T


def join_attention_kernel(R, HR, blocks, query_ref, out_ref):
    HN, W, half = HR * DN, DN + DR, DR // 2
    DC = D // R
    for j in range(R):
        for h in range(HR):
            at = (j * HR + h) * W
            one, two = HN + h * half, HN + 128 + h * half
            query_ref[:, at : at + DN] = blocks[j, :, h * DN : (h + 1) * DN].astype(F32)
            query_ref[:, at + DN : at + DN + half] = blocks[j, :, one : one + half].astype(F32)
            query_ref[:, at + DN + half : at + W] = blocks[j, :, two : two + half].astype(F32)
        out_ref[:, j * DC : (j + 1) * DC] = blocks[j, :, HN + 256 :].astype(F32)


def join_tail_kernel(R, HS, KR, LR, blocks, up_ref, down_ref, router_ref):
    W, NR = DN + DV, NE // R
    for j in range(R):
        for h in range(HS):
            up_ref[j * KR : (j + 1) * KR, h * W : (h + 1) * W] = blocks[
                j, h * KR : (h + 1) * KR, :W
            ].astype(F32)
        down_ref[j * LR : (j + 1) * LR, :] = blocks[j, :, W : W + LR].astype(F32).T
        router_ref[j * NR : (j + 1) * NR, :] = blocks[j, :, W + LR :].astype(F32).T


def join_blocks(kernel, R, r, pieces, outs):
    rows, width = pieces[0][2].shape

    def body(r_ref, *refs):
        block_ref = refs[-1]
        for (k, row, values), ref in zip(pieces, refs):
            block_ref[r_ref[0] ^ k, row : row + values.shape[0], :] = ref[...]
        kernel(block_ref, *refs[len(pieces) : -1])

    return pl.pallas_call(
        body,
        in_specs=[pl.BlockSpec(memory_space=pltpu.SMEM)]
        + [whole_block(values.shape) for _, _, values in pieces],
        out_specs=[whole_block(s) for s in outs],
        out_shape=[jax.ShapeDtypeStruct(s, F32) for s in outs],
        scratch_shapes=[pltpu.VMEM((R, rows, width), BF)],
    )(r.reshape(1), *[values for _, _, values in pieces])


def make_local(R, S):
    DL = D // S
    HR = H // R
    HS = H // S
    KR = KVR // R
    DC = D // R
    FR = FF // R
    SR = SH // R
    LR = (KVR + DR) // R
    NR = NE // R
    T = R * TOK
    QW = HR * DN + 256
    half = DR // 2
    HL = HR * half
    GR = DL // 64
    links = [[(i, i ^ k) for i in range(R)] for k in range(R)]

    def send(values, k):
        return lax.ppermute(values, REP, links[k])

    def gather(values):
        return [values] + [send(values, k) for k in range(1, R)]

    def local(
        hidden_in,
        segment_ids,
        routes,
        norm_gain,
        query_weight,
        kv_down,
        kv_gain,
        kv_up,
        out_weight,
        mixer_gain,
        router_weight,
        shared_gate,
        shared_up,
        shared_down,
        expert_gate,
        expert_up,
        expert_down,
        cotangent,
    ):
        r = lax.axis_index(REP)

        def part(values, width, axis=1):
            return lax.dynamic_slice_in_dim(values, r * width, width, axis)

        def natural(blocks):
            stacked = jnp.stack(blocks)
            return [
                lax.dynamic_index_in_dim(stacked, r ^ j, 0, keepdims=False) for j in range(R)
            ]

        def reduce_parts(parts):
            own = parts[0].astype(F32)
            received = [send(parts[k].astype(BF), k) for k in range(1, R)]
            for part_sum in received:
                own = own + part_sum.astype(F32)
            return own

        def reduce_blocks(total):
            return reduce_parts([total[k * TOK : (k + 1) * TOK] for k in range(R)])

        def gather_pieces(values):
            if R != 4:
                return [(k, 0, block) for k, block in enumerate(gather(values))]
            mid = values.shape[0] // 2
            values = by_rows(values)
            side, other = by_rows(send(values, 1)), by_rows(send(values, 2))
            top, low = by_rows(send(other[:mid], 1)), by_rows(send(side[mid:], 2))
            return [(0, 0, values), (1, 0, side), (2, 0, other), (3, 0, top), (3, mid, low)]

        def shard_gather(values):
            return lax.all_gather(values, SHD, axis=0, tiled=True)

        def shard_reduce(values):
            return lax.psum_scatter(values, SHD, scatter_dimension=0, tiled=True)

        index = jnp.arange(TOK, dtype=jnp.int32)
        same_own = segment_ids[:, None] == segment_ids[None, :]
        start_own = jnp.min(jnp.where(same_own, index[None, :], TOK), axis=1)
        chosen_own = jnp.any(routes == 0, axis=1)
        meta_own = jnp.concatenate(
            [
                start_own.astype(BF)[None],
                chosen_own.astype(BF)[None],
                jnp.zeros((6, TOK), BF),
            ]
        )
        meta = jnp.stack(gather(meta_own))
        x_all = jnp.concatenate(gather(hidden_in))
        cot_all = jnp.concatenate(gather(cotangent))

        kv_piece = (
            part(kv_up, KR, 0).reshape(KR, HS, DN + DV).transpose(1, 0, 2).reshape(HS * KR, DN + DV)
        )
        head_own = jnp.concatenate([part(out_weight, DC), fold(kv_piece, DL)], axis=1)
        head_all = shard_gather(head_own)
        kvu_all = unfold_all(head_all[:, DC:], S, DL, HS * KR).reshape(H, KR, DN + DV)
        out_all = head_all[:, :DC]
        head_blocks = []
        for k in range(R):
            rk = r ^ k
            piece = jnp.concatenate(
                [
                    lax.dynamic_slice_in_dim(out_all, rk * HR * DV, HR * DV, 0),
                    fold(
                        lax.dynamic_slice_in_dim(kvu_all, rk * HR, HR, 0).reshape(
                            HR * KR, DN + DV
                        ),
                        HR * DV,
                    ),
                ],
                axis=1,
            )
            head_blocks.append(send(piece, k) if k else piece)
        head_nat = natural(head_blocks)
        out_w = jnp.concatenate([b[:, :DC] for b in head_nat], axis=1)
        kvu = jnp.concatenate(
            [unfold(b[:, DC:], HR * KR).reshape(HR, KR, DN + DV) for b in head_nat], axis=1
        )
        kvu2 = jnp.concatenate(
            [
                kvu[:, :, :DN].transpose(1, 0, 2).reshape(KVR, HR * DN),
                kvu[:, :, DN:].transpose(1, 0, 2).reshape(KVR, HR * DV),
            ],
            axis=1,
        )

        def gain_rows(one, two, kv):
            lead = one.shape[:-1]
            pads = [(0, 0)] * len(lead)
            rows = jnp.concatenate(
                [
                    one.reshape(lead + (GR, 64)),
                    two.reshape(lead + (GR, 64)),
                    jnp.pad(kv, pads + [(0, 64 - KVR // S)]).reshape(lead + (1, 64)),
                ],
                axis=-2,
            )
            return jnp.pad(rows, pads + [(0, DL - 2 * GR - 1), (0, 0)])

        q_own = part(query_weight, HR * (DN + DR)).reshape(DL, HR, DN + DR)
        rope_pad = ((0, 0), (0, 128 - HL))
        attn_own = jnp.concatenate(
            [
                q_own[..., :DN].reshape(DL, HR * DN),
                jnp.pad(q_own[..., DN : DN + half].reshape(DL, HL), rope_pad),
                jnp.pad(q_own[..., DN + half :].reshape(DL, HL), rope_pad),
                kv_down,
                router_weight,
                gain_rows(norm_gain, mixer_gain, kv_gain),
            ],
            axis=1,
        )
        attn_all = shard_gather(attn_own)
        CD, CR, CG = QW, QW + KVR + DR, QW + KVR + DR + NE
        w_q = attn_all[:, :QW]
        w_down = attn_all[:, CD:CR]
        w_router = attn_all[:, CR:CG]
        gain_all = attn_all[:, CG:].reshape(S, DL, 64).astype(F32)
        gain_one = gain_all[:, :GR].reshape(D)
        gain_two = gain_all[:, GR : 2 * GR].reshape(D)
        gain_kv = gain_all[:, 2 * GR, : KVR // S].reshape(KVR)

        in_all = shard_gather(
            jnp.concatenate(
                [
                    part(shared_gate, SR),
                    part(shared_up, SR),
                    part(expert_gate[0], FR),
                    part(expert_up[0], FR),
                ],
                axis=1,
            ),
        )
        w_gu, w_egu = in_all[:, : 2 * SR], in_all[:, 2 * SR :]
        rest_all = shard_gather(
            jnp.concatenate([part(shared_down, SR, 0).T, part(expert_down[0], FR, 0).T], axis=1),
        )

        xf = x_all.astype(F32)
        scale_one = inv_rms(xf)
        n1 = (xf * scale_one * gain_one).astype(BF)
        qlat = dot(n1, attn_all)
        latent = qlat[:, CD : CD + KVR]
        scale_kv = inv_rms(latent)
        lat_n = (latent * scale_kv * gain_kv).astype(BF)
        kv = dot(lat_n, kvu2).astype(BF)

        start = meta[:, 0].astype(F32)
        position = index.astype(F32)[None] - start
        freq = 10000.0 ** (-jnp.arange(half, dtype=F32) / half)
        angles = position.reshape(T, 1) * jnp.tile(freq, 4)[None]
        cosine, sine = jnp.cos(angles), jnp.sin(angles)
        allowed = (start[:, :, None] == start[:, None, :]) & (index[None, :] <= index[:, None])[None]
        bias = jnp.where(allowed, 0.0, NEGATIVE).astype(F32)

        def rows(width, column=0):
            return pl.BlockSpec((TOK, width), lambda i: (i, column))

        def whole(*shape):
            return pl.BlockSpec(shape, lambda i: (0,) * len(shape))

        HN = HR * DN
        forward = pl.pallas_call(
            lambda *refs: attention_kernel(R, HR, *refs),
            grid=(R,),
            in_specs=[
                rows(QW),
                rows(128, (CD + KVR) // 128),
                rows(2 * HN),
                rows(128),
                rows(128),
                pl.BlockSpec((1, TOK, TOK), lambda i: (i, 0, 0)),
                whole(HN, D),
            ],
            out_specs=[
                rows(HN),
                pl.BlockSpec((HR, TOK, TOK), lambda i: (i, 0, 0)),
                rows(QW),
                rows(256),
            ]
            + [whole(TOK, D)] * R,
            out_shape=[
                jax.ShapeDtypeStruct((T, HN), BF),
                jax.ShapeDtypeStruct((R * HR, TOK, TOK), F32),
                jax.ShapeDtypeStruct((T, QW), BF),
                jax.ShapeDtypeStruct((T, 256), BF),
            ]
            + [jax.ShapeDtypeStruct((TOK, D), BF)] * R,
        )
        att, probs, q_b, kr_b, *out_parts = forward(
            qlat, qlat, kv, cosine, sine, bias, out_w
        )
        x_own = hidden_in.astype(F32)
        hidden = x_own + reduce_parts(out_parts)

        scale_two = inv_rms(hidden)
        n2_own = (hidden * scale_two * gain_two).astype(BF)
        n2 = jnp.concatenate(gather(n2_own))
        att_all = gather(att)
        probs_r = jax.nn.softmax(dot(n2, w_router), axis=-1)
        chosen = meta[:, 1].astype(F32)
        combine = probs_r[:, 0].reshape(R, TOK) * chosen
        place = jnp.cumsum(chosen.astype(jnp.int32), axis=1) - 1
        slots = jnp.arange(CAP, dtype=jnp.int32)
        dispatch = (
            (place[:, None, :] == slots[None, :, None]) & (chosen[:, None, :] > 0.5)
        ).astype(F32)
        dispatch_b = dispatch.astype(BF)
        n2_b = n2.reshape(R, TOK, D)
        cot_b = cot_all.reshape(R, TOK, D)
        rows_in = ein("bct,btd->bcd", dispatch_b, n2_b).astype(BF).reshape(R * CAP, D)
        rows_g = ein("bct,btd->bcd", dispatch_b, cot_b).reshape(R * CAP, D)
        rows_w = jnp.sum(dispatch * combine[:, None, :], axis=-1).reshape(R * CAP, 1)

        pre = dot(n2, w_gu)
        g_pre, u_pre = pre[:, :SR], pre[:, SR:]
        act, slope = silu_parts(g_pre)
        s_hid = (act * u_pre).astype(BF)
        down_part = pl.pallas_call(
            product_kernel,
            grid=(STEPS,),
            in_specs=[pl.BlockSpec((T, CHUNK), lambda i: (0, i)), whole_block((T, SR))],
            out_specs=pl.BlockSpec((CHUNK, SR), lambda i: (i, 0)),
            out_shape=jax.ShapeDtypeStruct((D, SR), BF),
        )(cot_all, s_hid)
        down_red = shard_reduce(down_part)
        e_pre = dot(rows_in, w_egu)
        e_g, e_u = e_pre[:, :FR], e_pre[:, FR:]
        e_act, e_slope = silu_parts(e_g)
        e_hid = (e_act * e_u).astype(BF)
        rows_geo = (rows_w * rows_g).astype(BF)
        spread = dispatch.transpose(0, 2, 1).reshape(T, CAP)
        chosen_wide = jnp.broadcast_to(chosen.reshape(T, 1), (T, 128))
        operands = (
            cot_all,
            rest_all,
            in_all,
            act,
            u_pre * slope,
            e_hid,
            e_act,
            e_u * e_slope,
            rows_geo,
            rows_g,
            spread,
            probs_r,
            chosen_wide,
            w_router,
        )
        RC = R * CAP

        def early(i):
            return jnp.minimum(i, STEPS - 1)

        def late(i):
            return jnp.maximum(i - STEPS, 0)

        specs = {
            0: pl.BlockSpec((T, CHUNK), lambda i: (0, early(i))),
            1: pl.BlockSpec((CHUNK, SR + FR), lambda i: (early(i), 0)),
            2: pl.BlockSpec((CHUNK, 2 * SR + 2 * FR), lambda i: (late(i), 0)),
            8: pl.BlockSpec((RC, CHUNK), lambda i: (0, early(i))),
            9: pl.BlockSpec((RC, CHUNK), lambda i: (0, early(i))),
            13: pl.BlockSpec((CHUNK, NE), lambda i: (late(i), 0)),
        }
        shapes = [
            ((T, 2 * SR), BF),
            ((RC, 2 * FR), BF),
            ((RC, D), F32),
            ((T, 128), F32),
        ] + [((TOK, D), BF)] * R
        s_geg, e_geg, rows_out, gc_wide, *gn2_parts = pl.pallas_call(
            lambda *refs: ffn_grad_kernel(R, SR, FR, *refs),
            grid=(2 * STEPS,),
            in_specs=[specs.get(n, whole_block(v.shape)) for n, v in enumerate(operands)],
            out_specs=[
                whole_block(shapes[0][0]),
                whole_block(shapes[1][0]),
                pl.BlockSpec((RC, CHUNK), lambda i: (0, early(i))),
                whole_block(shapes[3][0]),
            ]
            + [pl.BlockSpec((TOK, CHUNK), lambda i: (0, late(i)))] * R,
            out_shape=[jax.ShapeDtypeStruct(s, t) for s, t in shapes],
            scratch_shapes=[
                pltpu.VMEM((T, SR), F32),
                pltpu.VMEM((RC, FR), F32),
                pltpu.VMEM((RC, 128), F32),
                pltpu.VMEM((T, NE), BF),
            ],
        )(*operands)
        gc_part = gc_wide[:, 0].reshape(R, TOK)

        def logits_grad(gc):
            p = (gc * chosen).reshape(T, 1)
            first = (jnp.arange(NE) == 0).astype(F32)[None]
            return (probs_r * (p * first - probs_r[:, :1] * p)).astype(BF)

        gn2 = reduce_parts(gn2_parts)

        def columns(values):
            return pl.BlockSpec((values.shape[0], CHUNK), lambda i: (0, i))

        GW = 2 * SR + 3 * FR
        gu_part = pl.pallas_call(
            lambda *refs: ffn_weight_kernel(SR, FR, *refs),
            grid=(STEPS,),
            in_specs=[
                columns(n2),
                whole_block(s_geg.shape),
                columns(rows_in),
                whole_block(e_geg.shape),
                columns(rows_geo),
                whole_block(e_hid.shape),
            ],
            out_specs=pl.BlockSpec((CHUNK, GW), lambda i: (i, 0)),
            out_shape=jax.ShapeDtypeStruct((D, GW), BF),
        )(n2, s_geg, rows_in, e_geg, rows_geo, e_hid)
        gu_red = shard_reduce(gu_part)
        operands = (s_hid, rest_all, spread, rows_w, rows_out)
        out_ffn = pl.pallas_call(
            lambda *refs: ffn_out_kernel(R, SR, *refs),
            in_specs=[whole_block(v.shape) for v in operands],
            out_specs=[whole_block((TOK, D))] * R,
            out_shape=[jax.ShapeDtypeStruct((TOK, D), BF)] * R,
        )(*operands)
        out_ffn = [out_ffn[0]] + [send(out_ffn[k], k) for k in range(1, R)]
        result = pl.pallas_call(
            add_kernel, out_shape=jax.ShapeDtypeStruct((TOK, D), BF)
        )(hidden, *out_ffn)
        gc_all = gather(gc_part)
        gc_total = gc_all[0]
        for j in range(1, R):
            gc_total = gc_total + jnp.stack([gc_all[j][k ^ j] for k in range(R)])

        g_mixer = jnp.sum(gn2 * hidden * scale_two, axis=0)
        scaled = gn2 * gain_two
        grad_hidden = (
            cotangent.astype(F32)
            + scale_two * scaled
            - hidden * scale_two**3 * jnp.mean(scaled * hidden, axis=-1, keepdims=True)
        )

        backward = pl.pallas_call(
            lambda *refs: attention_grad_kernel(R, HR, *refs),
            grid=(R,),
            in_specs=[whole(TOK, D)] * R
            + [
                rows(HN),
                pl.BlockSpec((HR, TOK, TOK), lambda i: (i, 0, 0)),
                rows(2 * HN),
                rows(QW),
                rows(256),
                rows(128),
                rows(128),
                whole(HN, D),
                whole(KVR, 2 * HN),
            ],
            out_specs=[rows(QW), rows(2 * HN)] + [whole(TOK, KVR + 128)] * R,
            out_shape=[
                jax.ShapeDtypeStruct((T, QW), BF),
                jax.ShapeDtypeStruct((T, 2 * HN), BF),
            ]
            + [jax.ShapeDtypeStruct((TOK, KVR + 128), BF)] * R,
            scratch_shapes=[pltpu.VMEM((TOK, D), BF)],
        )
        ghb = gather(grad_hidden.astype(BF))
        gq, g_kv, *glat_parts = backward(
            *ghb, att, probs, kv, q_b, kr_b, cosine, sine, out_w, kvu2
        )
        attn_part = pl.pallas_call(
            lambda *refs: attention_weight_kernel(R, QW, *refs),
            grid_spec=pltpu.PrefetchScalarGridSpec(
                num_scalar_prefetch=1,
                grid=(R,),
                in_specs=[
                    pl.BlockSpec((T, DC), lambda i, r_ref: (0, i)),
                    whole_block((T, QW)),
                ]
                + [pl.BlockSpec((TOK, DC), lambda i, r_ref: (0, r_ref[0]))] * R
                + [whole_block((T, HN))] * R,
                out_specs=pl.BlockSpec((DC, QW + DC), lambda i, r_ref: (i, 0)),
                scratch_shapes=[pltpu.VMEM((T, DC), BF), pltpu.VMEM((T, HN), BF)],
            ),
            out_shape=jax.ShapeDtypeStruct((D, QW + DC), BF),
        )(r.reshape(1), n1, gq, *ghb, *att_all)
        glat = reduce_parts(glat_parts)
        latent_own, scale_kv_own = latent[:TOK], scale_kv[:TOK]
        gl_n = glat[:, :KVR]
        g_kvgain = jnp.sum(gl_n * latent_own * scale_kv_own, axis=0)
        lat_scaled = gl_n * gain_kv
        g_latent = scale_kv_own * lat_scaled - latent_own * scale_kv_own**3 * jnp.mean(
            lat_scaled * latent_own, axis=-1, keepdims=True
        )
        gd_own = jnp.concatenate([g_latent, glat[:, KVR : KVR + DR]], axis=1).astype(BF)
        gd = part(jnp.concatenate(gather(gd_own)), LR)
        gn1_part = dot_t(gq, w_q) + dot_t(gd, part(w_down, LR))
        gn1 = reduce_blocks(gn1_part)
        scale_own = scale_one[:TOK]
        scaled_one = gn1 * gain_one
        grad_input = (
            grad_hidden
            + scale_own * scaled_one
            - x_own * scale_own**3 * jnp.mean(scaled_one * x_own, axis=-1, keepdims=True)
        )
        g_norm = jnp.sum(gn1_part * xf * scale_one, axis=0)

        g_kvu2 = t_dot(lat_n, g_kv).astype(BF)
        g_kvu = jnp.concatenate(
            [
                g_kvu2[:, :HN].reshape(KVR, HR, DN),
                g_kvu2[:, HN:].reshape(KVR, HR, DV),
            ],
            axis=2,
        ).transpose(1, 0, 2)
        kvu_blocks = []
        for k in range(R):
            b = lax.dynamic_slice_in_dim(g_kvu, (r ^ k) * KR, KR, 1)
            kvu_blocks.append(send(b, k) if k else b)
        g_kvu_all = jnp.concatenate(natural(kvu_blocks))
        g_kvu_all = fold_all(g_kvu_all.reshape(H * KR, DN + DV), S, DL)

        g_router = t_dot(n2, part(logits_grad(gc_total), NR))
        g_down = t_dot(n1, gd)
        vectors = jnp.concatenate([g_norm, g_mixer, g_kvgain])
        summed = sum(gather(vectors))
        g_gains = gain_rows(
            summed[:D].reshape(S, DL),
            summed[D : 2 * D].reshape(S, DL),
            summed[2 * D :].reshape(S, KVR // S),
        ).reshape(D, 64)
        attn_red = shard_reduce(attn_part)
        pad = (-(LR + NR + 64)) % 128
        tail_red = shard_reduce(
            jnp.concatenate(
                [
                    g_kvu_all,
                    g_down.astype(BF),
                    g_router.astype(BF),
                    g_gains.astype(BF),
                    jnp.zeros((D, pad), BF),
                ],
                axis=1,
            ),
        )

        KW = HS * KR * (DN + DV) // DL
        (own_sd,) = join_blocks(
            lambda *refs: join_down_kernel(R, SR, *refs), R, r, gather_pieces(down_red), [(SH, DL)]
        )
        own_sg, own_su, own_eg, own_eu, own_ed = join_blocks(
            lambda *refs: join_ffn_kernel(R, SR, FR, *refs),
            R,
            r,
            gather_pieces(gu_red),
            [(DL, SH), (DL, SH), (DL, FF), (DL, FF), (FF, DL)],
        )
        own_qw, own_ow = join_blocks(
            lambda *refs: join_attention_kernel(R, HR, *refs),
            R,
            r,
            gather_pieces(attn_red),
            [(DL, H * (DN + DR)), (DL, D)],
        )
        tail_pieces = gather(tail_red[:, : KW + LR + NR])
        gains_red = tail_red[:, KW + LR + NR : KW + LR + NR + 64].astype(F32)
        if KW == DN + DV:
            own_ku, own_kd, own_rw = join_blocks(
                lambda *refs: join_tail_kernel(R, HS, KR, LR, *refs),
                R,
                r,
                [(k, 0, block) for k, block in enumerate(tail_pieces)],
                [(KVR, HS * (DN + DV)), (KVR + DR, DL), (NE, DL)],
            )
            own_kd, own_rw = own_kd.T, own_rw.T
        else:
            tail_nat = natural(tail_pieces)
            own_ku = jnp.concatenate(
                [
                    unfold(b[:, :KW], HS * KR)
                    .reshape(HS, KR, DN + DV)
                    .transpose(1, 0, 2)
                    .reshape(KR, HS * (DN + DV))
                    for b in tail_nat
                ]
            ).astype(F32)
            own_kd = jnp.concatenate([b[:, KW : KW + LR] for b in tail_nat], axis=1).astype(F32)
            own_rw = jnp.concatenate([b[:, KW + LR :] for b in tail_nat], axis=1).astype(F32)
        return (
            result,
            grad_input,
            gains_red[:GR].reshape(DL),
            own_qw,
            own_kd,
            gains_red[2 * GR, : KVR // S],
            own_ku,
            own_ow,
            gains_red[GR : 2 * GR].reshape(DL),
            own_rw,
            own_sg,
            own_su,
            own_sd,
            own_eg[None],
            own_eu[None],
            own_ed[None],
        )

    return local


def unfold_all(values, S, DL, rows):
    _, c = values.shape
    f = DL // rows
    if f <= 1:
        return values
    return values.reshape(S, f, rows, c).transpose(0, 2, 1, 3).reshape(S * rows, f * c)


def fold_all(values, S, DL):
    n, c = values.shape
    f = S * DL // n
    if f <= 1:
        return values
    return values.reshape(S, n // S, f, c // f).transpose(0, 2, 1, 3).reshape(S * DL, c // f)


def solution(mesh):
    tokens = P((REP, SHD), None)
    rows, cols = P(SHD, None), P(None, SHD)
    placed = (
        tokens,
        P((REP, SHD)),
        tokens,
        P(SHD),
        rows,
        rows,
        P(SHD),
        cols,
        rows,
        P(SHD),
        rows,
        rows,
        rows,
        cols,
        P(None, SHD, None),
        P(None, SHD, None),
        P(None, None, SHD),
        tokens,
    )
    outs = (tokens, tokens) + placed[3:17]
    body = make_local(mesh.shape[REP], mesh.shape[SHD])

    return jax.shard_map(
        body,
        mesh=mesh,
        in_specs=placed,
        out_specs=outs,
        check_vma=False,
    )
```

time: 1980 us -> 614 us (0.31)
  waiting for transfers between devices: 1650 us -> 269 us
  matrix products: 171 us -> 30.4 us
  Pallas kernels: 0 us -> 102 us
  blocking collectives: 85.6 us -> 0 us
  starting transfers between devices: 1.45 us -> 84 us
  local copies, waits for them, and re-layouts: 14.6 us -> 68.4 us
    reduce_scatter x11 -> x4, waiting for transfers between devices: 800 us -> 8.05 us  [shard_reduce(): return lax.psum_scatter(values, SHD, scatter_dimension=0, tiled=True)]
    all_gather x10 -> x4, waiting for transfers between devices: 672 us -> 33 us  [shard_gather(): return lax.all_gather(values, SHD, axis=0, tiled=True)]
    ppermute x0 -> x63, waiting for transfers between devices: none -> 227 us  [send(): return lax.ppermute(values, REP, links[k])]
    psum x1 -> x0, waiting for transfers between devices: 176 us -> none  [local(): lax.psum(own_qw.astype(jnp.bfloat16), 'replica').astype(jnp.float32)]
    dot_general x45 -> x12, matrix products: 171 us -> 30.4 us  [the longest x5 20.4 us: dot(): return jnp.dot(left, right, preferred_element_type=F32)]
    pallas_call x0 -> x12, Pallas kernels: none -> 102 us  [the longest x1 19.7 us: local(): pl.pallas_call(lambda *refs: ffn_grad_kernel(R, SR, FR, *refs), grid=(2 *...]
    ppermute x0 -> x63, starting transfers between devices: none -> 83.1 us  [send(): return lax.ppermute(values, REP, links[k])]
    all_gather x3 -> x0, blocking collectives: 37.5 us -> none  [the longest x1 15.3 us: local(): lax.all_gather(router_weight, 'shard', axis=0, tiled=True)]
  transfers between devices with their start and end apart: 22 -> 71, of which waited for: 19 -> 39; matrix products, arithmetic and copies ran while one was open for 7% -> 20% of each run, Pallas kernels for 0% -> 11%
where the time goes in v1:
time: 614 us; the launch traced here: 609 us
  waiting for transfers between devices  269 us (44%)
  Pallas kernels  102 us (17%)
  starting transfers between devices  84 us (14%)
  local copies, waits for them, and re-layouts  68.4 us (11%)
  other arithmetic  39.7 us (6%)
  matrix products  30.4 us (5%)
  between operations  15.8 us (3%)
    ppermute x63, waiting for transfers between devices, send(): return lax.ppermute(values, REP, links[k])  227 us
    ppermute x63, starting transfers between devices, send(): return lax.ppermute(values, REP, links[k])  83.1 us
    all_gather x4, waiting for transfers between devices, shard_gather(): return lax.all_gather(values, SHD, axis=0, tiled=True)  33 us
    dot_general x5, matrix products, dot(): return jnp.dot(left, right, preferred_element_type=F32)  20.4 us
    pallas_call x1, Pallas kernels, local(): pl.pallas_call(lambda *refs: ffn_grad_kernel(R, SR, FR, *refs), grid=(2 *...  19.7 us
    pallas_call x4, Pallas kernels, join_blocks(): pl.pallas_call(body, in_specs=[pl.BlockSpec(memory_space=pltpu.SMEM)] + [...  19.2 us
    pallas_call x1, Pallas kernels, local(): backward(*ghb, att, probs, kv, q_b, kr_b, cosine, sine, out_w, kvu2)  13.5 us
    pallas_call x1, Pallas kernels, local(): forward(qlat, qlat, kv, cosine, sine, bias, out_w)  13.3 us
  transfers between devices with their start and end apart: 71, of which 39 were waited for; matrix products, arithmetic and copies ran while one was open for 20% of the time, Pallas kernels for 11%

profile of v1, /device:TPU:0, one launch (start us, length us, event | category | flops | bytes accessed | tf_op | source)
XLA Modules:
  0.0 609.3 jit_solution(1286071712234890476)
XLA Ops:
  15.6 2.1 concatenate.84
  17.8 3.9 collective-permute-start.2
  24.3 1.9 collective-permute-start.6
  29.9 3.9 collective-permute-done.8
  35.6 9.4 %collective-permute-done.7 = bf16[8,128]{1,0:T(8,128)(2,1)S(1)} collective-permute-done((bf16[8,128]{1,0:T(8,128)(2,1)S(1)}, bf16[8,128]{1,0:T(8,128)(2,1)S(1)}, u32[]{:S(2)}, u32[]{:S(2)}) %collective-permute-start.7) | collective-permute-done | bytes 2080 | tf_op jit(solution)/shard_map/ppermute | solution.py:374
  46.9 4.6 all-gather.7.cloned.1.call-done
  54.5 2.4 collective-permute-start.5
  59.8 16.2 %collective-permute-done.5 = bf16[512,768]{1,0:T(8,128)(2,1)S(1)} collective-permute-done((bf16[512,768]{1,0:T(8,128)(2,1)S(1)}, bf16[512,768]{1,0:T(8,128)(2,1)S(1)}, u32[]{:S(2)}, u32[]{:S(2)}) %collective-permute-start.5) | collective-permute-done | bytes 786464 | tf_op jit(solution)/shard_map/ppermute | solution.py:374
  76.0 16.1 %collective-permute-done.4 = bf16[512,768]{1,0:T(8,128)(2,1)S(1)} collective-permute-done((bf16[512,768]{1,0:T(8,128)(2,1)S(1)}, bf16[512,768]{1,0:T(8,128)(2,1)S(1)}, u32[]{:S(2)}, u32[]{:S(2)}) %collective-permute-start.4) | collective-permute-done | bytes 786464 | tf_op jit(solution)/shard_map/ppermute | solution.py:374
  97.6 19.7 %all-gather.5.cloned.1.call-done = bf16[2048,1472]{1,0:T(8,128)(2,1)} async-done(((bf16[256,1472]{1,0:T(8,128)(2,1)}), bf16[2048,1472]{1,0:T(8,128)(2,1)}) %all-gather.5.cloned.1.call-update) | async-done | bytes 6029328 | tf_op jit(solution)/shard_map/all_gather | solution.py:430
  117.3 2.2 fusion.65
  119.7 3.4 fusion.4.refs_1_
  124.4 5.9 fusion.78
  130.4 2.6 copy.208.refs_0_.refs_1_
  133.2 3.1 convolution_convert_fusion.4.refs_2_.refs_6_
  136.3 13.3 %shard_map.297 = (bf16[512,512]{1,0:T(8,128)(2,1)}, f32[16,128,128]{2,1,0:T(8,128)}, bf16[512,768]{1,0:T(8,128)(2,1)}, bf16[512,256]{1,0:T(8,128)(2,1)}, bf16[12...) custom-call(f32[512,1472]{1,0:T(8,128)} %copy.208.refs_0_.refs_1_, ...), custom_call_target="tpu_custom_call" | custom-call | tf_op jit(solution)/shard_map/pallas_call | solution.py:589
  149.6 2.4 collective-permute-start.11
  158.4 7.3 %collective-permute-done.11 = bf16[128,2048]{1,0:T(8,128)(2,1)S(1)} collective-permute-done((bf16[128,2048]{1,0:T(8,128)(2,1)}, bf16[128,2048]{1,0:T(8,128)(2,1)S(1)}, u32[]{:S(2)}, u32[]{:S(2)}) %collective-permute-start.11) | collective-permute-done | bytes 524320 | tf_op jit(solution)/shard_map/ppermute | solution.py:374
  165.7 2.4 collective-permute-start.17
  168.0 8.2 %collective-permute-done.10 = bf16[128,2048]{1,0:T(8,128)(2,1)S(1)} collective-permute-done((bf16[128,2048]{1,0:T(8,128)(2,1)}, bf16[128,2048]{1,0:T(8,128)(2,1)S(1)}, u32[]{:S(2)}, u32[]{:S(2)}) %collective-permute-start.10) | collective-permute-done | bytes 524320 | tf_op jit(solution)/shard_map/ppermute | solution.py:374
  177.0 2.2 multiply_reduce_fusion.2
  180.0 2.4 collective-permute-start.14
  183.0 5.2 collective-permute-done.15
  191.9 7.6 %collective-permute-done.17 = bf16[128,2048]{1,0:T(8,128)(2,1)S(1)} collective-permute-done((bf16[128,2048]{1,0:T(8,128)(2,1)}, bf16[128,2048]{1,0:T(8,128)(2,1)S(1)}, u32[]{:S(2)}, u32[]{:S(2)}) %collective-permute-start.17) | collective-permute-done | bytes 524320 | tf_op jit(solution)/shard_map/ppermute | solution.py:374
  199.5 11.1 %collective-permute-done.14 = bf16[128,2048]{1,0:T(8,128)(2,1)S(1)} collective-permute-done((bf16[128,2048]{1,0:T(8,128)(2,1)S(1)}, bf16[128,2048]{1,0:T(8,128)(2,1)S(1)}, u32[]{:S(2)}, u32[]{:S(2)}) %collective-permute-start.14) | collective-permute-done | bytes 524320 | tf_op jit(solution)/shard_map/ppermute | solution.py:374
  210.6 10.4 %collective-permute-done.13 = bf16[128,2048]{1,0:T(8,128)(2,1)S(1)} collective-permute-done((bf16[128,2048]{1,0:T(8,128)(2,1)S(1)}, bf16[128,2048]{1,0:T(8,128)(2,1)S(1)}, u32[]{:S(2)}, u32[]{:S(2)}) %collective-permute-start.13) | collective-permute-done | bytes 524320 | tf_op jit(solution)/shard_map/ppermute | solution.py:374
  221.3 3.0 fusion.77
  235.7 2.6 fusion.9
  239.1 5.8 fusion
  244.9 2.7 multiply_multiply_fusion
  247.6 8.7 %all-gather.11.cloned.1.call-done.refs_1_ = bf16[2048,1056]{1,0:T(8,128)(2,1)} async-done(((bf16[256,1056]{1,0:T(8,128)(2,1)}), bf16[2048,1056]{1,0:T(8,128)(2,1)}) %all-gather.11.cloned.1.call-update) | async-done | bytes 4325392 | tf_op jit(solution)/shard_map/all_gather | solution.py:430
  257.1 19.7 %shard_map.298 = (bf16[512,1408]{1,0:T(8,128)(2,1)}, bf16[64,704]{1,0:T(8,128)(2,1)}, f32[64,2048]{1,0:T(8,128)}, f32[512,128]{1,0:T(8,128)}, bf16[128,2048]{1,0...) custom-call(bf16[512,2048]{1,0:T(8,128)(2,1)} %copy-done.7, ...), custom_call_target="tpu_custom_call" | custom-call | tf_op jit(solution)/shard_map/pallas_call | solution.py:671
  276.9 9.2 %shard_map.305 = bf16[2048,2464]{1,0:T(8,128)(2,1)} custom-call(bf16[512,2048]{1,0:T(8,128)(2,1)} %copy-done.2, bf16[512,1408]{1,0:T(8,128)(2,1)} %get-tuple-element.81.refs_1_, bf16[64,2048]{1,0:T(8,128)(2,1)} %bitcast.156, bf16[64,704]{1,0:T(8,128)(2,1)} %get-tuple-element.82.refs_3_, bf16[64,2048]{1,0:T(8,128)(2,1)} %multiply_convert_fusion.3.refs_8_.refs_4_, ...), custom_call_target="tpu_custom_call" | custom-call | tf_op jit(solution)/shard_map/pallas_call | solution.py:703
  286.4 2.4 collective-permute-start.23
  290.1 12.3 %collective-permute-done.23 = bf16[128,2048]{1,0:T(8,128)(2,1)S(1)} collective-permute-done((bf16[128,2048]{1,0:T(8,128)(2,1)}, bf16[128,2048]{1,0:T(8,128)(2,1)S(1)}, u32[]{:S(2)}, u32[]{:S(2)}) %collective-permute-start.23) | collective-permute-done | bytes 524320 | tf_op jit(solution)/shard_map/ppermute | solution.py:374
  302.4 10.4 %collective-permute-done.22 = bf16[128,2048]{1,0:T(8,128)(2,1)S(1)} collective-permute-done((bf16[128,2048]{1,0:T(8,128)(2,1)S(1)}, bf16[128,2048]{1,0:T(8,128)(2,1)S(1)}, u32[]{:S(2)}, u32[]{:S(2)}) %collective-permute-start.22) | collective-permute-done | bytes 524320 | tf_op jit(solution)/shard_map/ppermute | solution.py:374
  313.5 2.7 fusion.63
  322.2 8.8 %collective-permute-done.24.refs_1_.refs_4_ = bf16[128,2048]{1,0:T(8,128)(2,1)S(1)} collective-permute-done((bf16[128,2048]{1,0:T(8,128)(2,1)S(1)}, bf16[128,2048]{1,0:T(8,128)(2,1)S(1)}, u32[]{:S(2)}, u32[]{:S(2)}) %collective-permute-start.24) | collective-permute-done | bytes 524320 | tf_op jit(solution)/shard_map/ppermute | solution.py:374
  332.9 10.8 %collective-permute-done.25.refs_2_.refs_5_ = bf16[128,2048]{1,0:T(8,128)(2,1)S(1)} collective-permute-done((bf16[128,2048]{1,0:T(8,128)(2,1)S(1)}, bf16[128,2048]{1,0:T(8,128)(2,1)S(1)}, u32[]{:S(2)}, u32[]{:S(2)}) %collective-permute-start.25) | collective-permute-done | bytes 524320 | tf_op jit(solution)/shard_map/ppermute | solution.py:374
  344.7 13.5 %shard_map.301 = (bf16[512,768]{1,0:T(8,128)(2,1)}, bf16[512,1024]{1,0:T(8,128)(2,1)}, bf16[128,640]{1,0:T(8,128)(2,1)}, bf16[128,640]{1,0:T(8,128)(2,1)}, bf16[...) custom-call(bf16[128,2048]{1,0:T(8,128)(2,1)} %copy-done.16, bf16[128,2048]{1,0:T(8,128)(2,1)} %copy-done.21, ...), custom_call_target="tpu_custom_call" | custom-call | tf_op jit(solution)/shard_map/pallas_call | solution.py:766
  358.2 6.9 %collective-permute-done.46.refs_9_ = bf16[512,512]{1,0:T(8,128)(2,1)} collective-permute-done((bf16[512,512]{1,0:T(8,128)(2,1)S(1)}, bf16[512,512]{1,0:T(8,128)(2,1)}, u32[]{:S(2)}, u32[]{:S(2)}) %collective-permute-start.46) | collective-permute-done | bytes 524320 | tf_op jit(solution)/shard_map/ppermute | solution.py:374
  365.1 7.8 %shard_map.302 = bf16[2048,1280]{1,0:T(8,128)(2,1)} custom-call(s32[1]{0:T(128)} %bitcast.74.refs_0_.r_ref, bf16[512,2048]{1,0:T(8,128)(2,1)} %copy-done.4, bf16[512,768]{1,0:T(8,128)(2,1)} %get-tuple-element.69.refs_2_, bf16[128,2048]{1,0:T(8,128)(2,1)} %copy-done.16, bf16[128,2048]{1,0:T(8,128)(2,1)} %copy-done.21, bf16[128,2048]{1,0:T(8,128)(2,1)} %copy-done.22, ...), custom_call_target="tpu_custom_call" | custom-call | tf_op jit(solution)/shard_map/pallas_call | solution.py:769
  388.6 2.0 convolution_convert_fusion.3
  395.5 3.3 collective-permute-done.28
  414.2 3.9 fusion.6
  426.1 5.6 concatenate.93
  432.0 5.5 shard_map.307
  438.2 11.1 %shard_map.299 = (bf16[128,2048]{1,0:T(8,128)(2,1)}, bf16[128,2048]{1,0:T(8,128)(2,1)}, bf16[128,2048]{1,0:T(8,128)(2,1)}, bf16[128,2048]{1,0:T(8,128)(2,1)}) custom-call(bf16[512,704]{1,0:T(8,128)(2,1)} %get-tuple-element.109.refs_0_.right_ref, bf16[2048,1056]{1,0:T(8,128)(2,1)} %all-gather.11.cloned.1.call-done.refs_1_, ...), custom_call_target="tpu_custom_call" | custom-call | tf_op jit(solution)/shard_map/pallas_call | solution.py:719
  452.9 2.4 copy.227
  458.6 5.7 collective-permute-done.18.refs_1_
  466.0 10.3 %collective-permute-done.19.refs_2_ = bf16[128,2048]{1,0:T(8,128)(2,1)} collective-permute-done((bf16[128,2048]{1,0:T(8,128)(2,1)}, bf16[128,2048]{1,0:T(8,128)(2,1)}, u32[]{:S(2)}, u32[]{:S(2)}) %collective-permute-start.19) | collective-permute-done | bytes 524320 | tf_op jit(solution)/shard_map/ppermute | solution.py:374
  478.2 3.0 shard_map.300
  481.2 32.7 %collective-permute-done.35 = bf16[128,2048]{1,0:T(8,128)(2,1)S(1)} collective-permute-done((bf16[128,2048]{1,0:T(8,128)(2,1)}, bf16[128,2048]{1,0:T(8,128)(2,1)S(1)}, u32[]{:S(2)}, u32[]{:S(2)}) %collective-permute-start.35) | collective-permute-done | bytes 524320 | tf_op jit(solution)/shard_map/ppermute | solution.py:374
  513.9 6.9 %collective-permute-done.34 = bf16[128,2048]{1,0:T(8,128)(2,1)S(1)} collective-permute-done((bf16[128,2048]{1,0:T(8,128)(2,1)}, bf16[128,2048]{1,0:T(8,128)(2,1)S(1)}, u32[]{:S(2)}, u32[]{:S(2)}) %collective-permute-start.34) | collective-permute-done | bytes 524320 | tf_op jit(solution)/shard_map/ppermute | solution.py:374
  526.3 8.0 %reduce-scatter.11.cloned.1.call-done.refs_0_ = bf16[256,704]{1,0:T(8,128)(2,1)} async-done(((bf16[2048,704]{1,0:T(8,128)(2,1)}), bf16[256,704]{1,0:T(8,128)(2,1)}) %reduce-scatter.11.cloned.1.call-update) | async-done | bytes 360464 | tf_op jit(solution)/shard_map/reduce_scatter | solution.py:433
  537.3 2.7 fusion.16
  555.2 2.8 collective-permute-done.53.refs_2_
  560.1 2.1 collective-permute-start.51
  564.4 10.6 %collective-permute-done.61.refs_3_ = bf16[128,704]{1,0:T(8,128)(2,1)S(1)} collective-permute-done((bf16[128,704]{1,0:T(8,128)(2,1)}, bf16[128,704]{1,0:T(8,128)(2,1)S(1)}, u32[]{:S(2)}, u32[]{:S(2)}) %collective-permute-start.61) | collective-permute-done | bytes 180256 | tf_op jit(solution)/shard_map/ppermute | solution.py:374
  575.0 2.3 collective-permute-start.62
  578.6 2.9 shard_map.304
  582.2 3.5 shard_map.308
  587.1 5.1 shard_map.303
  594.5 7.7 %shard_map.306 = (f32[256,2816]{1,0:T(8,128)}, f32[256,2816]{1,0:T(8,128)}, f32[256,1408]{1,0:T(8,128)}, f32[256,1408]{1,0:T(8,128)}, f32[1408,256]{1,0:T(8,128)}) custom-call(s32[1]{0:T(128)} %bitcast.74.refs_0_.r_ref, bf16[256,2464]{1,0:T(8,128)(2,1)} %reduce-scatter.9.cloned.1.call-done.refs_0_, bf16[256,2464]{1,0:T(8,128)(2,1)} %copy-done.13, ...), custom_call_target="tpu_custom_call" | custom-call | tf_op jit(solution)/shard_map/pallas_call | solution.py:346
  (438 shorter events, 155.7 us)
Async XLA Ops:
  7.2 44.2 %all-gather.7.cloned.1.call-start = ((), (), s32[]{:S(2)}) async-start(), calls=%async_computation.5 | async-start | bytes 3538944 | tf_op jit(solution)/shard_map/all_gather | solution.py:430
  10.3 106.9 %all-gather.5.cloned.1.call-start = ((), (), s32[]{:S(2)}) async-start(), calls=%async_computation.4 | async-start | bytes 7077888 | tf_op jit(solution)/shard_map/all_gather | solution.py:430
  12.7 223.0 %all-gather.9.cloned.1.call-start = ((), (), s32[]{:S(2)}) async-start(), calls=%async_computation.6 | async-start | bytes 10027008 | tf_op jit(solution)/shard_map/all_gather | solution.py:430
  17.8 238.5 %all-gather.11.cloned.1.call-start = ((), (), s32[]{:S(2)}) async-start(), calls=%async_computation.7 | async-start | bytes 5308416 | tf_op jit(solution)/shard_map/all_gather | solution.py:430
  17.8 39.9 %collective-permute-start.2 = (bf16[128,2048]{1,0:T(8,128)(2,1)S(1)}, bf16[128,2048]{1,0:T(8,128)(2,1)S(1)}, u32[]{:S(2)}, u32[]{:S(2)}) collective-permute-start(bf16[128,2048]{1,0:T(8,128)(2,1)S(1)} %copy-done.9), channel_id=1, source_target_pairs={{0,24},{8,16},{16,8},{24,0},{1,25},{9,17},{17,9},{25,1},{2,26},{10... | collective-permute-start | bytes 1572872 | tf_op jit(solution)/shard_map/ppermute | solution.py:374
  21.8 37.4 %collective-permute-start.1 = (bf16[128,2048]{1,0:T(8,128)(2,1)S(1)}, bf16[128,2048]{1,0:T(8,128)(2,1)S(1)}, u32[]{:S(2)}, u32[]{:S(2)}) collective-permute-start(bf16[128,2048]{1,0:T(8,128)(2,1)S(1)} %copy-done.9), channel_id=1, source_target_pairs={{0,16},{8,24},{16,0},{24,8},{1,17},{9,25},{17,1},{25,9},{2,18},{10... | collective-permute-start | bytes 1572872 | tf_op jit(solution)/shard_map/ppermute | solution.py:374
  22.7 11.1 %collective-permute-start.8 = (bf16[8,128]{1,0:T(8,128)(2,1)S(1)}, bf16[8,128]{1,0:T(8,128)(2,1)S(1)}, u32[]{:S(2)}, u32[]{:S(2)}) collective-permute-start(bf16[8,128]{1,0:T(8,128)(2,1)S(1)} %get-tuple-element.160), channel_id=1, source_target_pairs={{0,24},{8,16},{16,8},{24,0},{1,25},{9,17},{17,9},{25,1},{2,26},{10... | collective-permute-start | bytes 6152 | tf_op jit(solution)/shard_map/ppermute | solution.py:374
  24.2 20.8 %collective-permute-start.7 = (bf16[8,128]{1,0:T(8,128)(2,1)S(1)}, bf16[8,128]{1,0:T(8,128)(2,1)S(1)}, u32[]{:S(2)}, u32[]{:S(2)}) collective-permute-start(bf16[8,128]{1,0:T(8,128)(2,1)S(1)} %get-tuple-element.160), channel_id=1, source_target_pairs={{0,16},{8,24},{16,0},{24,8},{1,17},{9,25},{17,1},{25,9},{2,18},{10... | collective-permute-start | bytes 6152 | tf_op jit(solution)/shard_map/ppermute | solution.py:374
  24.3 20.7 %collective-permute-start.6 = (bf16[8,128]{1,0:T(8,128)(2,1)S(1)}, bf16[8,128]{1,0:T(8,128)(2,1)S(1)}, u32[]{:S(2)}, u32[]{:S(2)}) collective-permute-start(bf16[8,128]{1,0:T(8,128)(2,1)S(1)} %get-tuple-element.160), channel_id=1, source_target_pairs={{0,8},{8,0},{16,24},{24,16},{1,9},{9,1},{17,25},{25,17},{2,10},{10... | collective-permute-start | bytes 6152 | tf_op jit(solution)/shard_map/ppermute | solution.py:374
  29.5 423.4 %reduce-scatter.9.cloned.1.call-start = ((), (), s32[]{:S(2)}) async-start(), calls=%async_computation.10 | async-start | bytes 11796480 | tf_op jit(solution)/shard_map/reduce_scatter | solution.py:433
  33.8 25.4 %collective-permute-start = (bf16[128,2048]{1,0:T(8,128)(2,1)S(1)}, bf16[128,2048]{1,0:T(8,128)(2,1)S(1)}, u32[]{:S(2)}, u32[]{:S(2)}) collective-permute-start(bf16[128,2048]{1,0:T(8,128)(2,1)S(1)} %copy-done.9), channel_id=1, source_target_pairs={{0,8},{8,0},{16,24},{24,16},{1,9},{9,1},{17,25},{25,17},{2,10},{10... | collective-permute-start | bytes 1572872 | tf_op jit(solution)/shard_map/ppermute | solution.py:374
  54.5 21.4 %collective-permute-start.5 = (bf16[512,768]{1,0:T(8,128)(2,1)S(1)}, bf16[512,768]{1,0:T(8,128)(2,1)S(1)}, u32[]{:S(2)}, u32[]{:S(2)}) collective-permute-start(bf16[512,768]{1,0:T(8,128)(2,1)S(1)} %pad_maximum_fusion.8), channel_id=1, source_target_pairs={{0,24},{8,16},{16,8},{24,0},{1,25},{9,17},{17,9},{25,1},{2,26},{10... | collective-permute-start | bytes 2359304 | tf_op jit(solution)/shard_map/ppermute | solution.py:374
  57.0 35.0 %collective-permute-start.4 = (bf16[512,768]{1,0:T(8,128)(2,1)S(1)}, bf16[512,768]{1,0:T(8,128)(2,1)S(1)}, u32[]{:S(2)}, u32[]{:S(2)}) collective-permute-start(bf16[512,768]{1,0:T(8,128)(2,1)S(1)} %pad_maximum_fusion.7), channel_id=1, source_target_pairs={{0,16},{8,24},{16,0},{24,8},{1,17},{9,25},{17,1},{25,9},{2,18},{10... | collective-permute-start | bytes 2359304 | tf_op jit(solution)/shard_map/ppermute | solution.py:374
  57.7 34.4 %collective-permute-start.3 = (bf16[512,768]{1,0:T(8,128)(2,1)S(1)}, bf16[512,768]{1,0:T(8,128)(2,1)S(1)}, u32[]{:S(2)}, u32[]{:S(2)}) collective-permute-start(bf16[512,768]{1,0:T(8,128)(2,1)S(1)} %pad_maximum_fusion.6), channel_id=1, source_target_pairs={{0,8},{8,0},{16,24},{24,16},{1,9},{9,1},{17,25},{25,17},{2,10},{10... | collective-permute-start | bytes 2359304 | tf_op jit(solution)/shard_map/ppermute | solution.py:374
  149.6 16.0 %collective-permute-start.11 = (bf16[128,2048]{1,0:T(8,128)(2,1)}, bf16[128,2048]{1,0:T(8,128)(2,1)S(1)}, u32[]{:S(2)}, u32[]{:S(2)}) collective-permute-start(bf16[128,2048]{1,0:T(8,128)(2,1)} %get-tuple-element.55), channel_id=1, source_target_pairs={{0,24},{8,16},{16,8},{24,0},{1,25},{9,17},{17,9},{25,1},{2,26},{10... | collective-permute-start | bytes 1572872 | tf_op jit(solution)/shard_map/ppermute | solution.py:374
  152.1 24.2 %collective-permute-start.10 = (bf16[128,2048]{1,0:T(8,128)(2,1)}, bf16[128,2048]{1,0:T(8,128)(2,1)S(1)}, u32[]{:S(2)}, u32[]{:S(2)}) collective-permute-start(bf16[128,2048]{1,0:T(8,128)(2,1)} %get-tuple-element.54), channel_id=1, source_target_pairs={{0,16},{8,24},{16,0},{24,8},{1,17},{9,25},{17,1},{25,9},{2,18},{10... | collective-permute-start | bytes 1572872 | tf_op jit(solution)/shard_map/ppermute | solution.py:374
  152.6 24.4 %collective-permute-start.9 = (bf16[128,2048]{1,0:T(8,128)(2,1)}, bf16[128,2048]{1,0:T(8,128)(2,1)}, u32[]{:S(2)}, u32[]{:S(2)}) collective-permute-start(bf16[128,2048]{1,0:T(8,128)(2,1)} %get-tuple-element.53), channel_id=1, source_target_pairs={{0,8},{8,0},{16,24},{24,16},{1,9},{9,1},{17,25},{25,17},{2,10},{10... | collective-permute-start | bytes 1572872 | tf_op jit(solution)/shard_map/ppermute | solution.py:374
  153.2 35.0 %collective-permute-start.15 = (bf16[128,2048]{1,0:T(8,128)(2,1)}, bf16[128,2048]{1,0:T(8,128)(2,1)}, u32[]{:S(2)}, u32[]{:S(2)}) collective-permute-start(bf16[128,2048]{1,0:T(8,128)(2,1)} %param.35), channel_id=1, source_target_pairs={{0,8},{8,0},{16,24},{24,16},{1,9},{9,1},{17,25},{25,17},{2,10},{10... | collective-permute-start | bytes 1572872 | tf_op jit(solution)/shard_map/ppermute | solution.py:374
  154.6 36.1 %collective-permute-start.16 = (bf16[128,2048]{1,0:T(8,128)(2,1)}, bf16[128,2048]{1,0:T(8,128)(2,1)}, u32[]{:S(2)}, u32[]{:S(2)}) collective-permute-start(bf16[128,2048]{1,0:T(8,128)(2,1)} %param.35), channel_id=1, source_target_pairs={{0,16},{8,24},{16,0},{24,8},{1,17},{9,25},{17,1},{25,9},{2,18},{10... | collective-permute-start | bytes 1572872 | tf_op jit(solution)/shard_map/ppermute | solution.py:374
  165.7 33.8 %collective-permute-start.17 = (bf16[128,2048]{1,0:T(8,128)(2,1)}, bf16[128,2048]{1,0:T(8,128)(2,1)S(1)}, u32[]{:S(2)}, u32[]{:S(2)}) collective-permute-start(bf16[128,2048]{1,0:T(8,128)(2,1)} %param.35), channel_id=1, source_target_pairs={{0,24},{8,16},{16,8},{24,0},{1,25},{9,17},{17,9},{25,1},{2,26},{10... | collective-permute-start | bytes 1572872 | tf_op jit(solution)/shard_map/ppermute | solution.py:374
  180.0 30.6 %collective-permute-start.14 = (bf16[128,2048]{1,0:T(8,128)(2,1)S(1)}, bf16[128,2048]{1,0:T(8,128)(2,1)S(1)}, u32[]{:S(2)}, u32[]{:S(2)}) collective-permute-start(bf16[128,2048]{1,0:T(8,128)(2,1)S(1)} %multiply_convert_fusion.1), channel_id=1, source_target_pairs={{0,24},{8,16},{16,8},{24,0},{1,25},{9,17},{17,9},{25,1},{2,26},{10... | collective-permute-start | bytes 1572872 | tf_op jit(solution)/shard_map/ppermute | solution.py:374
  182.4 38.6 %collective-permute-start.13 = (bf16[128,2048]{1,0:T(8,128)(2,1)S(1)}, bf16[128,2048]{1,0:T(8,128)(2,1)S(1)}, u32[]{:S(2)}, u32[]{:S(2)}) collective-permute-start(bf16[128,2048]{1,0:T(8,128)(2,1)S(1)} %multiply_convert_fusion.1), channel_id=1, source_target_pairs={{0,16},{8,24},{16,0},{24,8},{1,17},{9,25},{17,1},{25,9},{2,18},{10... | collective-permute-start | bytes 1572872 | tf_op jit(solution)/shard_map/ppermute | solution.py:374
  188.2 32.9 %collective-permute-start.12 = (bf16[128,2048]{1,0:T(8,128)(2,1)S(1)}, bf16[128,2048]{1,0:T(8,128)(2,1)S(1)}, u32[]{:S(2)}, u32[]{:S(2)}) collective-permute-start(bf16[128,2048]{1,0:T(8,128)(2,1)S(1)} %multiply_convert_fusion.1), channel_id=1, source_target_pairs={{0,8},{8,0},{16,24},{24,16},{1,9},{9,1},{17,25},{25,17},{2,10},{10... | collective-permute-start | bytes 1572872 | tf_op jit(solution)/shard_map/ppermute | solution.py:374
  286.2 236.3 %reduce-scatter.7.cloned.1.call-start = ((), (), s32[]{:S(2)}) async-start(), calls=%async_computation.9 | async-start | bytes 5898240 | tf_op jit(solution)/shard_map/reduce_scatter | solution.py:433
  286.4 16.0 %collective-permute-start.23 = (bf16[128,2048]{1,0:T(8,128)(2,1)}, bf16[128,2048]{1,0:T(8,128)(2,1)S(1)}, u32[]{:S(2)}, u32[]{:S(2)}) collective-permute-start(bf16[128,2048]{1,0:T(8,128)(2,1)} %get-tuple-element.64), channel_id=1, source_target_pairs={{0,24},{8,16},{16,8},{24,0},{1,25},{9,17},{17,9},{25,1},{2,26},{10... | collective-permute-start | bytes 1572872 | tf_op jit(solution)/shard_map/ppermute | solution.py:374
  288.8 24.0 %collective-permute-start.22 = (bf16[128,2048]{1,0:T(8,128)(2,1)S(1)}, bf16[128,2048]{1,0:T(8,128)(2,1)S(1)}, u32[]{:S(2)}, u32[]{:S(2)}) collective-permute-start(bf16[128,2048]{1,0:T(8,128)(2,1)S(1)} %copy-done.64), channel_id=1, source_target_pairs={{0,16},{8,24},{16,0},{24,8},{1,17},{9,25},{17,1},{25,9},{2,18},{10... | collective-permute-start | bytes 1572872 | tf_op jit(solution)/shard_map/ppermute | solution.py:374
  289.4 23.5 %collective-permute-start.21 = (bf16[128,2048]{1,0:T(8,128)(2,1)S(1)}, bf16[128,2048]{1,0:T(8,128)(2,1)S(1)}, u32[]{:S(2)}, u32[]{:S(2)}) collective-permute-start(bf16[128,2048]{1,0:T(8,128)(2,1)S(1)} %copy-done.63), channel_id=1, source_target_pairs={{0,8},{8,0},{16,24},{24,16},{1,9},{9,1},{17,25},{25,17},{2,10},{10... | collective-permute-start | bytes 1572872 | tf_op jit(solution)/shard_map/ppermute | solution.py:374
  316.2 14.8 %collective-permute-start.24 = (bf16[128,2048]{1,0:T(8,128)(2,1)S(1)}, bf16[128,2048]{1,0:T(8,128)(2,1)S(1)}, u32[]{:S(2)}, u32[]{:S(2)}) collective-permute-start(bf16[128,2048]{1,0:T(8,128)(2,1)S(1)} %get-tuple-element.94.refs_0_.refs_3_), channel_id=1, source_target_pairs={{0,8},{8,0},{16,24},{24,16},{1,9},{9,1},{17,25},{25,17},{2,10},{10... | collective-permute-start | bytes 1572872 | tf_op jit(solution)/shard_map/ppermute | solution.py:374
  317.7 26.0 %collective-permute-start.25 = (bf16[128,2048]{1,0:T(8,128)(2,1)S(1)}, bf16[128,2048]{1,0:T(8,128)(2,1)S(1)}, u32[]{:S(2)}, u32[]{:S(2)}) collective-permute-start(bf16[128,2048]{1,0:T(8,128)(2,1)S(1)} %get-tuple-element.94.refs_0_.refs_3_), channel_id=1, source_target_pairs={{0,16},{8,24},{16,0},{24,8},{1,17},{9,25},{17,1},{25,9},{2,18},{10... | collective-permute-start | bytes 1572872 | tf_op jit(solution)/shard_map/ppermute | solution.py:374
  318.7 25.0 %collective-permute-start.26 = (bf16[128,2048]{1,0:T(8,128)(2,1)S(1)}, bf16[128,2048]{1,0:T(8,128)(2,1)S(1)}, u32[]{:S(2)}, u32[]{:S(2)}) collective-permute-start(bf16[128,2048]{1,0:T(8,128)(2,1)S(1)} %get-tuple-element.94.refs_0_.refs_3_), channel_id=1, source_target_pairs={{0,24},{8,16},{16,8},{24,0},{1,25},{9,17},{17,9},{25,1},{2,26},{10... | collective-permute-start | bytes 1572872 | tf_op jit(solution)/shard_map/ppermute | solution.py:374
  319.7 38.5 %collective-permute-start.45 = (bf16[512,512]{1,0:T(8,128)(2,1)S(1)}, bf16[512,512]{1,0:T(8,128)(2,1)S(1)}, u32[]{:S(2)}, u32[]{:S(2)}) collective-permute-start(bf16[512,512]{1,0:T(8,128)(2,1)S(1)} %copy-done.20), channel_id=1, source_target_pairs={{0,8},{8,0},{16,24},{24,16},{1,9},{9,1},{17,25},{25,17},{2,10},{10... | collective-permute-start | bytes 1572872 | tf_op jit(solution)/shard_map/ppermute | solution.py:374
  321.2 43.9 %collective-permute-start.46 = (bf16[512,512]{1,0:T(8,128)(2,1)S(1)}, bf16[512,512]{1,0:T(8,128)(2,1)}, u32[]{:S(2)}, u32[]{:S(2)}) collective-permute-start(bf16[512,512]{1,0:T(8,128)(2,1)S(1)} %copy-done.20), channel_id=1, source_target_pairs={{0,16},{8,24},{16,0},{24,8},{1,17},{9,25},{17,1},{25,9},{2,18},{10... | collective-permute-start | bytes 1572872 | tf_op jit(solution)/shard_map/ppermute | solution.py:374
  331.0 34.1 %collective-permute-start.47 = (bf16[512,512]{1,0:T(8,128)(2,1)S(1)}, bf16[512,512]{1,0:T(8,128)(2,1)}, u32[]{:S(2)}, u32[]{:S(2)}) collective-permute-start(bf16[512,512]{1,0:T(8,128)(2,1)S(1)} %copy-done.20), channel_id=1, source_target_pairs={{0,24},{8,16},{16,8},{24,0},{1,25},{9,17},{17,9},{25,1},{2,26},{10... | collective-permute-start | bytes 1572872 | tf_op jit(solution)/shard_map/ppermute | solution.py:374
  372.9 151.7 %reduce-scatter.5.cloned.1.call-start = ((), (), s32[]{:S(2)}) async-start(), calls=%async_computation.8 | async-start | bytes 2359296 | tf_op jit(solution)/shard_map/reduce_scatter | solution.py:433
  385.1 9.7 %collective-permute-start.29 = (bf16[128,640]{1,0:T(8,128)(2,1)}, bf16[128,640]{1,0:T(8,128)(2,1)S(1)}, u32[]{:S(2)}, u32[]{:S(2)}) collective-permute-start(bf16[128,640]{1,0:T(8,128)(2,1)} %get-tuple-element.73), channel_id=1, source_target_pairs={{0,24},{8,16},{16,8},{24,0},{1,25},{9,17},{17,9},{25,1},{2,26},{10... | collective-permute-start | bytes 491528 | tf_op jit(solution)/shard_map/ppermute | solution.py:374
  386.4 12.3 %collective-permute-start.28 = (bf16[128,640]{1,0:T(8,128)(2,1)}, bf16[128,640]{1,0:T(8,128)(2,1)S(1)}, u32[]{:S(2)}, u32[]{:S(2)}) collective-permute-start(bf16[128,640]{1,0:T(8,128)(2,1)} %get-tuple-element.72), channel_id=1, source_target_pairs={{0,16},{8,24},{16,0},{24,8},{1,17},{9,25},{17,1},{25,9},{2,18},{10... | collective-permute-start | bytes 491528 | tf_op jit(solution)/shard_map/ppermute | solution.py:374
  387.9 10.8 %collective-permute-start.27 = (bf16[128,640]{1,0:T(8,128)(2,1)}, bf16[128,640]{1,0:T(8,128)(2,1)S(1)}, u32[]{:S(2)}, u32[]{:S(2)}) collective-permute-start(bf16[128,640]{1,0:T(8,128)(2,1)} %get-tuple-element.71), channel_id=1, source_target_pairs={{0,8},{8,0},{16,24},{24,16},{1,9},{9,1},{17,25},{25,17},{2,10},{10... | collective-permute-start | bytes 491528 | tf_op jit(solution)/shard_map/ppermute | solution.py:374
  391.9 11.4 %collective-permute-start.38 = (bf16[4,128,256]{2,0,1:T(4,128)(2,1)S(1)}, bf16[4,128,256]{2,0,1:T(4,128)(2,1)S(1)}, u32[]{:S(2)}, u32[]{:S(2)}) collective-permute-start(bf16[4,128,256]{2,0,1:T(4,128)(2,1)S(1)} %get-tuple-element.123), channel_id=1, source_target_pairs={{0,24},{8,16},{16,8},{24,0},{1,25},{9,17},{17,9},{25,1},{2,26},{10... | collective-permute-start | bytes 786440 | tf_op jit(solution)/shard_map/ppermute | solution.py:374
  393.3 13.0 %collective-permute-start.37 = (bf16[4,128,256]{2,0,1:T(4,128)(2,1)S(1)}, bf16[4,128,256]{2,0,1:T(4,128)(2,1)S(1)}, u32[]{:S(2)}, u32[]{:S(2)}) collective-permute-start(bf16[4,128,256]{2,0,1:T(4,128)(2,1)S(1)} %get-tuple-element.124), channel_id=1, source_target_pairs={{0,16},{8,24},{16,0},{24,8},{1,17},{9,25},{17,1},{25,9},{2,18},{10... | collective-permute-start | bytes 786440 | tf_op jit(solution)/shard_map/ppermute | solution.py:374
  394.8 12.9 %collective-permute-start.36 = (bf16[4,128,256]{2,0,1:T(4,128)(2,1)S(1)}, bf16[4,128,256]{2,0,1:T(4,128)(2,1)S(1)}, u32[]{:S(2)}, u32[]{:S(2)}) collective-permute-start(bf16[4,128,256]{2,0,1:T(4,128)(2,1)S(1)} %get-tuple-element.125), channel_id=1, source_target_pairs={{0,8},{8,0},{16,24},{24,16},{1,9},{9,1},{17,25},{25,17},{2,10},{10... | collective-permute-start | bytes 786440 | tf_op jit(solution)/shard_map/ppermute | solution.py:374
  401.3 9.1 %collective-permute-start.30 = (bf16[128,576]{1,0:T(8,128)(2,1)S(1)}, bf16[128,576]{1,0:T(8,128)(2,1)S(1)}, u32[]{:S(2)}, u32[]{:S(2)}) collective-permute-start(bf16[128,576]{1,0:T(8,128)(2,1)S(1)} %pad_maximum_fusion.11), channel_id=1, source_target_pairs={{0,8},{8,0},{16,24},{24,16},{1,9},{9,1},{17,25},{25,17},{2,10},{10... | collective-permute-start | bytes 442376 | tf_op jit(solution)/shard_map/ppermute | solution.py:374
  402.7 7.7 %collective-permute-start.31 = (bf16[128,576]{1,0:T(8,128)(2,1)S(1)}, bf16[128,576]{1,0:T(8,128)(2,1)S(1)}, u32[]{:S(2)}, u32[]{:S(2)}) collective-permute-start(bf16[128,576]{1,0:T(8,128)(2,1)S(1)} %pad_maximum_fusion.11), channel_id=1, source_target_pairs={{0,16},{8,24},{16,0},{24,8},{1,17},{9,25},{17,1},{25,9},{2,18},{10... | collective-permute-start | bytes 442376 | tf_op jit(solution)/shard_map/ppermute | solution.py:374
  403.3 8.7 %collective-permute-start.32 = (bf16[128,576]{1,0:T(8,128)(2,1)S(1)}, bf16[128,576]{1,0:T(8,128)(2,1)S(1)}, u32[]{:S(2)}, u32[]{:S(2)}) collective-permute-start(bf16[128,576]{1,0:T(8,128)(2,1)S(1)} %pad_maximum_fusion.11), channel_id=1, source_target_pairs={{0,24},{8,16},{16,8},{24,0},{1,25},{9,17},{17,9},{25,1},{2,26},{10... | collective-permute-start | bytes 442376 | tf_op jit(solution)/shard_map/ppermute | solution.py:374
  431.8 102.5 %reduce-scatter.11.cloned.1.call-start = ((), (), s32[]{:S(2)}) async-start(), calls=%async_computation.11 | async-start | bytes 3538944 | tf_op jit(solution)/shard_map/reduce_scatter | solution.py:433
  449.4 15.0 %collective-permute-start.18 = (bf16[128,2048]{1,0:T(8,128)(2,1)}, bf16[128,2048]{1,0:T(8,128)(2,1)S(1)}, u32[]{:S(2)}, u32[]{:S(2)}) collective-permute-start(bf16[128,2048]{1,0:T(8,128)(2,1)} %get-tuple-element.58), channel_id=1, source_target_pairs={{0,8},{8,0},{16,24},{24,16},{1,9},{9,1},{17,25},{25,17},{2,10},{10... | collective-permute-start | bytes 1572872 | tf_op jit(solution)/shard_map/ppermute | solution.py:374
  449.9 26.3 %collective-permute-start.19 = (bf16[128,2048]{1,0:T(8,128)(2,1)}, bf16[128,2048]{1,0:T(8,128)(2,1)}, u32[]{:S(2)}, u32[]{:S(2)}) collective-permute-start(bf16[128,2048]{1,0:T(8,128)(2,1)} %get-tuple-element.59), channel_id=1, source_target_pairs={{0,16},{8,24},{16,0},{24,8},{1,17},{9,25},{17,1},{25,9},{2,18},{10... | collective-permute-start | bytes 1572872 | tf_op jit(solution)/shard_map/ppermute | solution.py:374
  451.5 26.3 %collective-permute-start.20 = (bf16[128,2048]{1,0:T(8,128)(2,1)}, bf16[128,2048]{1,0:T(8,128)(2,1)}, u32[]{:S(2)}, u32[]{:S(2)}) collective-permute-start(bf16[128,2048]{1,0:T(8,128)(2,1)} %get-tuple-element.60), channel_id=1, source_target_pairs={{0,24},{8,16},{16,8},{24,0},{1,25},{9,17},{17,9},{25,1},{2,26},{10... | collective-permute-start | bytes 1572872 | tf_op jit(solution)/shard_map/ppermute | solution.py:374
  455.3 79.0 %collective-permute-start.55 = (bf16[256,2464]{0,1:T(8,128)(2,1)}, bf16[256,2464]{0,1:T(8,128)(2,1)}, u32[]{:S(2)}, u32[]{:S(2)}) collective-permute-start(bf16[256,2464]{0,1:T(8,128)(2,1)} %copy.227), channel_id=1, source_target_pairs={{0,8},{8,0},{16,24},{24,16},{1,9},{9,1},{17,25},{25,17},{2,10},{10... | collective-permute-start | bytes 3784712 | tf_op jit(solution)/shard_map/ppermute | solution.py:374
  455.9 79.9 %collective-permute-start.56 = (bf16[256,2464]{0,1:T(8,128)(2,1)}, bf16[256,2464]{0,1:T(8,128)(2,1)}, u32[]{:S(2)}, u32[]{:S(2)}) collective-permute-start(bf16[256,2464]{0,1:T(8,128)(2,1)} %copy.227), channel_id=1, source_target_pairs={{0,16},{8,24},{16,0},{24,8},{1,17},{9,25},{17,1},{25,9},{2,18},{10... | collective-permute-start | bytes 3784712 | tf_op jit(solution)/shard_map/ppermute | solution.py:374
  464.4 49.5 %collective-permute-start.35 = (bf16[128,2048]{1,0:T(8,128)(2,1)}, bf16[128,2048]{1,0:T(8,128)(2,1)S(1)}, u32[]{:S(2)}, u32[]{:S(2)}) collective-permute-start(bf16[128,2048]{1,0:T(8,128)(2,1)} %get-tuple-element.112), channel_id=1, source_target_pairs={{0,24},{8,16},{16,8},{24,0},{1,25},{9,17},{17,9},{25,1},{2,26},{10... | collective-permute-start | bytes 1572872 | tf_op jit(solution)/shard_map/ppermute | solution.py:374
  476.3 44.4 %collective-permute-start.34 = (bf16[128,2048]{1,0:T(8,128)(2,1)}, bf16[128,2048]{1,0:T(8,128)(2,1)S(1)}, u32[]{:S(2)}, u32[]{:S(2)}) collective-permute-start(bf16[128,2048]{1,0:T(8,128)(2,1)} %get-tuple-element.113), channel_id=1, source_target_pairs={{0,16},{8,24},{16,0},{24,8},{1,17},{9,25},{17,1},{25,9},{2,18},{10... | collective-permute-start | bytes 1572872 | tf_op jit(solution)/shard_map/ppermute | solution.py:374
  477.9 42.8 %collective-permute-start.33 = (bf16[128,2048]{1,0:T(8,128)(2,1)}, bf16[128,2048]{1,0:T(8,128)(2,1)S(1)}, u32[]{:S(2)}, u32[]{:S(2)}) collective-permute-start(bf16[128,2048]{1,0:T(8,128)(2,1)} %get-tuple-element.111), channel_id=1, source_target_pairs={{0,8},{8,0},{16,24},{24,16},{1,9},{9,1},{17,25},{25,17},{2,10},{10... | collective-permute-start | bytes 1572872 | tf_op jit(solution)/shard_map/ppermute | solution.py:374
  522.4 25.2 %collective-permute-start.48 = (bf16[256,1280]{1,0:T(8,128)(2,1)}, bf16[256,1280]{1,0:T(8,128)(2,1)}, u32[]{:S(2)}, u32[]{:S(2)}) collective-permute-start(bf16[256,1280]{1,0:T(8,128)(2,1)} %reduce-scatter.7.cloned.1.call-done.refs_0_), channel_id=1, source_target_pairs={{0,8},{8,0},{16,24},{24,16},{1,9},{9,1},{17,25},{25,17},{2,10},{10... | collective-permute-start | bytes 1966088 | tf_op jit(solution)/shard_map/ppermute | solution.py:374
  524.1 24.6 %collective-permute-start.49 = (bf16[256,1280]{1,0:T(8,128)(2,1)}, bf16[256,1280]{1,0:T(8,128)(2,1)}, u32[]{:S(2)}, u32[]{:S(2)}) collective-permute-start(bf16[256,1280]{1,0:T(8,128)(2,1)} %reduce-scatter.7.cloned.1.call-done.refs_0_), channel_id=1, source_target_pairs={{0,16},{8,24},{16,0},{24,8},{1,17},{9,25},{17,1},{25,9},{2,18},{10... | collective-permute-start | bytes 1966088 | tf_op jit(solution)/shard_map/ppermute | solution.py:374
  524.6 20.4 %collective-permute-start.52 = (bf16[256,416]{1,0:T(8,128)(2,1)}, bf16[256,416]{1,0:T(8,128)(2,1)}, u32[]{:S(2)}, u32[]{:S(2)}) collective-permute-start(bf16[256,416]{1,0:T(8,128)(2,1)} %bitcast.176), channel_id=1, source_target_pairs={{0,8},{8,0},{16,24},{24,16},{1,9},{9,1},{17,25},{25,17},{2,10},{10... | collective-permute-start | bytes 638984 | tf_op jit(solution)/shard_map/ppermute | solution.py:374
  534.3 25.8 %collective-permute-start.59 = (bf16[256,704]{1,0:T(8,128)(2,1)}, bf16[256,704]{1,0:T(8,128)(2,1)}, u32[]{:S(2)}, u32[]{:S(2)}) collective-permute-start(bf16[256,704]{1,0:T(8,128)(2,1)} %reduce-scatter.11.cloned.1.call-done.refs_0_), channel_id=1, source_target_pairs={{0,8},{8,0},{16,24},{24,16},{1,9},{9,1},{17,25},{25,17},{2,10},{10... | collective-permute-start | bytes 1081352 | tf_op jit(solution)/shard_map/ppermute | solution.py:374
  535.8 10.6 %collective-permute-start.60 = (bf16[256,704]{1,0:T(8,128)(2,1)}, bf16[256,704]{1,0:T(8,128)(2,1)}, u32[]{:S(2)}, u32[]{:S(2)}) collective-permute-start(bf16[256,704]{1,0:T(8,128)(2,1)} %reduce-scatter.11.cloned.1.call-done.refs_0_), channel_id=1, source_target_pairs={{0,16},{8,24},{16,0},{24,8},{1,17},{9,25},{17,1},{25,9},{2,18},{10... | collective-permute-start | bytes 1081352 | tf_op jit(solution)/shard_map/ppermute | solution.py:374
  545.0 13.0 %collective-permute-start.53 = (bf16[256,416]{1,0:T(8,128)(2,1)}, bf16[256,416]{1,0:T(8,128)(2,1)S(1)}, u32[]{:S(2)}, u32[]{:S(2)}) collective-permute-start(bf16[256,416]{1,0:T(8,128)(2,1)} %bitcast.177), channel_id=1, source_target_pairs={{0,16},{8,24},{16,0},{24,8},{1,17},{9,25},{17,1},{25,9},{2,18},{10... | collective-permute-start | bytes 638984 | tf_op jit(solution)/shard_map/ppermute | solution.py:374
  546.4 13.0 %collective-permute-start.54 = (bf16[256,416]{1,0:T(8,128)(2,1)}, bf16[256,416]{1,0:T(8,128)(2,1)S(1)}, u32[]{:S(2)}, u32[]{:S(2)}) collective-permute-start(bf16[256,416]{1,0:T(8,128)(2,1)} %bitcast.178), channel_id=1, source_target_pairs={{0,24},{8,16},{16,8},{24,0},{1,25},{9,17},{17,9},{25,1},{2,26},{10... | collective-permute-start | bytes 638984 | tf_op jit(solution)/shard_map/ppermute | solution.py:374
  547.6 44.6 %collective-permute-start.57 = (bf16[128,2464]{0,1:T(8,128)(2,1)}, bf16[128,2464]{0,1:T(8,128)(2,1)S(1)}, u32[]{:S(2)}, u32[]{:S(2)}) collective-permute-start(bf16[128,2464]{0,1:T(8,128)(2,1)} %copy.231), channel_id=1, source_target_pairs={{0,8},{8,0},{16,24},{24,16},{1,9},{9,1},{17,25},{25,17},{2,10},{10... | collective-permute-start | bytes 1892360 | tf_op jit(solution)/shard_map/ppermute | solution.py:374
  548.6 44.7 %collective-permute-start.58 = (bf16[128,2464]{0,1:T(8,128)(2,1)S(1)}, bf16[128,2464]{0,1:T(8,128)(2,1)S(1)}, u32[]{:S(2)}, u32[]{:S(2)}) collective-permute-start(bf16[128,2464]{0,1:T(8,128)(2,1)S(1)} %copy.233), channel_id=1, source_target_pairs={{0,16},{8,24},{16,0},{24,8},{1,17},{9,25},{17,1},{25,9},{2,18},{10... | collective-permute-start | bytes 1892360 | tf_op jit(solution)/shard_map/ppermute | solution.py:374
  558.0 17.0 %collective-permute-start.61 = (bf16[128,704]{1,0:T(8,128)(2,1)}, bf16[128,704]{1,0:T(8,128)(2,1)S(1)}, u32[]{:S(2)}, u32[]{:S(2)}) collective-permute-start(bf16[128,704]{1,0:T(8,128)(2,1)} %slice.378), channel_id=1, source_target_pairs={{0,8},{8,0},{16,24},{24,16},{1,9},{9,1},{17,25},{25,17},{2,10},{10... | collective-permute-start | bytes 540680 | tf_op jit(solution)/shard_map/ppermute | solution.py:374
  559.4 26.3 %collective-permute-start.50 = (bf16[128,1280]{1,0:T(8,128)(2,1)}, bf16[128,1280]{1,0:T(8,128)(2,1)S(1)}, u32[]{:S(2)}, u32[]{:S(2)}) collective-permute-start(bf16[128,1280]{1,0:T(8,128)(2,1)} %slice.371), channel_id=1, source_target_pairs={{0,8},{8,0},{16,24},{24,16},{1,9},{9,1},{17,25},{25,17},{2,10},{10... | collective-permute-start | bytes 983048 | tf_op jit(solution)/shard_map/ppermute | solution.py:374
  560.1 25.6 %collective-permute-start.51 = (bf16[128,1280]{1,0:T(8,128)(2,1)S(1)}, bf16[128,1280]{1,0:T(8,128)(2,1)S(1)}, u32[]{:S(2)}, u32[]{:S(2)}) collective-permute-start(bf16[128,1280]{1,0:T(8,128)(2,1)S(1)} %slice.372), channel_id=1, source_target_pairs={{0,16},{8,24},{16,0},{24,8},{1,17},{9,25},{17,1},{25,9},{2,18},{10... | collective-permute-start | bytes 983048 | tf_op jit(solution)/shard_map/ppermute | solution.py:374
  (81 other events, 1005.8 us)
Sparse Core Ops, SparseCore 0:
  10.4 40.9 all-gather.6
  53.6 63.5 all-gather.4
  119.5 85.0 all-gather.8
  206.6 49.6 all-gather.10
  286.3 108.0 reduce-scatter.8
  396.6 58.2 reduce-scatter.6
  457.8 34.7 reduce-scatter.4
  495.4 38.8 reduce-scatter.10

commit v2 on v1

--- a/solution.py
+++ b/solution.py
@@ -2,7 +2,6 @@
 import jax.numpy as jnp
 from jax import lax
 from jax.experimental import pallas as pl
-from jax.experimental.layout import Layout, with_layout_constraint
 from jax.experimental.pallas import tpu as pltpu
 from jax.sharding import PartitionSpec as P
 
@@ -50,10 +49,6 @@
     return (pre_act * sigmoid_val, sigmoid_val * (1.0 + pre_act * (1.0 - sigmoid_val)))
 
 
-def by_rows(values):
-    return with_layout_constraint(values, Layout(major_to_minor=(0, 1)))
-
-
 def fold(values, rows):
     n, c = values.shape
     f = rows // n
@@ -79,9 +74,23 @@
     return lax.broadcasted_iota(jnp.int32, (TOK, 128), 1)
 
 
-def attention_kernel(R, HR, q_ref, rope_ref, kv_ref, cos_ref, sin_ref, bias_ref, out_w_ref,
-                     att_ref, probs_ref, qb_ref, krb_ref, *part_refs):
-    HN = HR * DN
+def block_at(R, r_ref, k, width):
+    if R != 4:
+        return slice(k * width, (k + 1) * width)
+    return pl.ds(pl.multiple_of((r_ref[0] ^ k) * width, width), width)
+
+
+def attention_kernel(R, HR, r_ref, q_ref, rope_ref, lat_ref, cos_ref, sin_ref, bias_ref, *refs):
+    out_w_refs, kvu_refs = refs[:R], refs[R : 2 * R]
+    att_ref, probs_ref, qb_ref, krb_ref, kv_ref = refs[2 * R : 2 * R + 5]
+    part_refs, sum_ref = refs[2 * R + 5 : 3 * R + 5], refs[-1]
+    HN, KR, W = HR * DN, KVR // R, DN + DV
+    lats = [lat_ref[:, block_at(R, r_ref, k, KR)] for k in range(R)]
+    for h in range(HR):
+        total = dot(lats[0], kvu_refs[0][h * KR : (h + 1) * KR, :])
+        for k in range(1, R):
+            total = total + dot(lats[k], kvu_refs[k][h * KR : (h + 1) * KR, :])
+        kv_ref[:, h * W : (h + 1) * W] = total.astype(BF)
     lane = lane_index()
     cos, sin = cos_ref[...], sin_ref[...]
     rope = rope_ref[...]
@@ -102,7 +111,7 @@
     for h in range(HR):
         head = (lane >= 32 * h) & (lane < 32 * h + 32)
         scores = (
-            dot_t(q_n[:, h * DN : (h + 1) * DN], kv_ref[:, h * DN : (h + 1) * DN])
+            dot_t(q_n[:, h * DN : (h + 1) * DN], kv_ref[:, h * W : h * W + DN])
             + dot_t(jnp.where(head, qr_1, 0.0).astype(BF), kr_1)
             + dot_t(jnp.where(head, qr_2, 0.0).astype(BF), kr_2)
             + bias
@@ -110,23 +119,25 @@
         expd = jnp.exp(scores - jnp.max(scores, axis=-1, keepdims=True))
         probs = expd / jnp.sum(expd, axis=-1, keepdims=True)
         probs_ref[h] = probs
-        value = kv_ref[:, HN + h * DV : HN + (h + 1) * DV]
+        value = kv_ref[:, h * W + DN : (h + 1) * W]
         att_ref[:, h * DV : (h + 1) * DV] = dot(probs.astype(BF), value).astype(BF)
-    part = dot(att_ref[...], out_w_ref[...]).astype(BF)
+    att = att_ref[...]
+    for k in range(R):
+        sum_ref[:, block_at(R, r_ref, k, D // R)] = dot(att, out_w_refs[k][...]).astype(BF)
     for k in range(R):
 
         @pl.when(pl.program_id(0) == k)
         def _():
-            part_refs[k][...] = part
-
-
-def attention_grad_kernel(R, HR, *refs):
-    grad_refs = refs[:R]
-    (att_ref, probs_ref, kv_ref, qb_ref, krb_ref, cos_ref, sin_ref, out_w_ref, kvu_ref,
-     gq_ref, gkv_ref) = refs[R : R + 11]
-    glat_refs = refs[R + 11 : 2 * R + 11]
-    ghb_ref = refs[2 * R + 11]
-    HN = HR * DN
+            part_refs[k][...] = sum_ref[...]
+
+
+def attention_grad_kernel(R, HR, r_ref, *refs):
+    grad_refs, out_w_refs, kvu_refs = refs[:R], refs[R : 2 * R], refs[2 * R : 3 * R]
+    (att_ref, probs_ref, kv_ref, qb_ref, krb_ref, cos_ref, sin_ref,
+     gq_ref, gkv_ref) = refs[3 * R : 3 * R + 9]
+    glat_refs = refs[3 * R + 9 : 4 * R + 9]
+    ghb_ref, lat_ref = refs[4 * R + 9 :]
+    HN, KR, W = HR * DN, KVR // R, DN + DV
     step = pl.program_id(0)
     for k in range(R):
 
@@ -134,8 +145,10 @@
         def _():
             ghb_ref[...] = grad_refs[k][...]
 
-    ghb = ghb_ref[...]
-    g_att = dot_t(ghb, out_w_ref[...]).astype(BF)
+    g_att = dot_t(ghb_ref[:, block_at(R, r_ref, 0, D // R)], out_w_refs[0][...])
+    for k in range(1, R):
+        g_att = g_att + dot_t(ghb_ref[:, block_at(R, r_ref, k, D // R)], out_w_refs[k][...])
+    g_att = g_att.astype(BF)
     lane = lane_index()
     cos, sin = cos_ref[...], sin_ref[...]
     kr_1, kr_2 = krb_ref[:, :128], krb_ref[:, 128:]
@@ -145,17 +158,17 @@
     gq_1, gq_2, gk_1, gk_2 = zero, zero, zero, zero
     for h in range(HR):
         cut = slice(h * DN, (h + 1) * DN)
-        cut_v = slice(HN + h * DV, HN + (h + 1) * DV)
+        key, value = slice(h * W, h * W + DN), slice(h * W + DN, (h + 1) * W)
         head = (lane >= 32 * h) & (lane < 32 * h + 32)
         ga = g_att[:, cut]
         probs = probs_ref[h]
-        gkv_ref[:, cut_v] = t_dot(probs.astype(BF), ga).astype(BF)
+        gkv_ref[:, value] = t_dot(probs.astype(BF), ga).astype(BF)
         delta = jnp.sum(ga.astype(F32) * att_ref[:, cut].astype(F32), axis=-1, keepdims=True)
-        gs = (probs * (dot_t(ga, kv_ref[:, cut_v]) - delta)).astype(BF)
-        gq_ref[:, cut] = (dot(gs, kv_ref[:, cut]) * SCALE).astype(BF)
+        gs = (probs * (dot_t(ga, kv_ref[:, value]) - delta)).astype(BF)
+        gq_ref[:, cut] = (dot(gs, kv_ref[:, key]) * SCALE).astype(BF)
         gq_1 = gq_1 + jnp.where(head, dot(gs, kr_1), 0.0)
         gq_2 = gq_2 + jnp.where(head, dot(gs, kr_2), 0.0)
-        gkv_ref[:, cut] = t_dot(gs, qb_ref[:, cut]).astype(BF)
+        gkv_ref[:, key] = t_dot(gs, qb_ref[:, cut]).astype(BF)
         gk_1 = gk_1 + t_dot(gs, jnp.where(head, qr_1, 0.0).astype(BF))
         gk_2 = gk_2 + t_dot(gs, jnp.where(head, qr_2, 0.0).astype(BF))
     gq_ref[:, HN : HN + 128] = ((gq_1 * cos + gq_2 * sin) * SCALE).astype(BF)
@@ -163,17 +176,25 @@
     u_1, u_2 = roll_sum(gk_1), roll_sum(gk_2)
     r_1, r_2 = u_1 * cos + u_2 * sin, u_2 * cos - u_1 * sin
     g_rope = jnp.where(lane < 32, r_1, jnp.where(lane < 64, r_2, 0.0)).astype(BF)
-    g_lat = dot_t(gkv_ref[...], kvu_ref[...]).astype(BF)
+    lat_ref[:, KVR:] = g_rope
+    for k in range(R):
+        total = dot_t(gkv_ref[:, :W], kvu_refs[k][:KR, :])
+        for h in range(1, HR):
+            total = total + dot_t(
+                gkv_ref[:, h * W : (h + 1) * W], kvu_refs[k][h * KR : (h + 1) * KR, :]
+            )
+        lat_ref[:, block_at(R, r_ref, k, KR)] = total.astype(BF)
     for k in range(R):
 
         @pl.when(step == k)
         def _():
-            glat_refs[k][:, :KVR] = g_lat
-            glat_refs[k][:, KVR:] = g_rope
-
-
-def exact_dot(left, right):
-    return jnp.dot(left, right, precision=lax.Precision.HIGHEST, preferred_element_type=F32)
+            glat_refs[k][...] = lat_ref[...]
+
+
+def scatter_rows(spread, rows):
+    high = rows.astype(BF)
+    low = (rows - high.astype(F32)).astype(BF)
+    return dot(spread, jnp.concatenate([high, low], axis=0))
 
 
 REP, SHD = "replica", "shard"
@@ -220,34 +241,29 @@
         e_gh = e_acc_ref[...]
         e_geg_ref[:, :FR] = (e_gh * e_slope_ref[...]).astype(BF)
         e_geg_ref[:, FR:] = (e_gh * e_act_ref[...]).astype(BF)
-        for k in range(R):
-            tok, row = slice(k * TOK, (k + 1) * TOK), slice(k * CAP, (k + 1) * CAP)
-            gc = exact_dot(spread_ref[tok, :], gc_acc_ref[row, :])
-            gc_ref[tok, :] = gc
-            p = (gc * chosen_ref[tok, :])[:, :NE]
-            probs = probs_ref[tok, :]
-            first = lax.broadcasted_iota(jnp.int32, (TOK, NE), 1) == 0
-            lg = probs * (jnp.where(first, p, 0.0) - probs[:, :1] * p)
-            lg_ref[tok, :] = lg.astype(BF)
+        gc = scatter_rows(spread_ref[...], gc_acc_ref[...])
+        gc_ref[...] = gc
+        p = (gc * chosen_ref[...])[:, :NE]
+        probs = probs_ref[...]
+        first = lax.broadcasted_iota(jnp.int32, probs.shape, 1) == 0
+        lg = probs * (jnp.where(first, p, 0.0) - probs[:, :1] * p)
+        lg_ref[...] = lg.astype(BF)
 
     @pl.when(step >= STEPS)
     def _():
         g_n2 = dot_t(geg_ref[...], in_ref[:, : 2 * SR]) + dot_t(lg_ref[...], router_ref[...])
         rows_back = dot_t(e_geg_ref[...], in_ref[:, 2 * SR :])
+        total = g_n2 + scatter_rows(spread_ref[...], rows_back)
         for k in range(R):
-            tok, row = slice(k * TOK, (k + 1) * TOK), slice(k * CAP, (k + 1) * CAP)
-            part = g_n2[tok] + exact_dot(spread_ref[tok, :], rows_back[row])
-            part_refs[k][...] = part.astype(BF)
+            part_refs[k][...] = total[k * TOK : (k + 1) * TOK].astype(BF)
 
 
 def ffn_out_kernel(R, SR, s_hid_ref, rest_ref, spread_ref, rows_w_ref, rows_out_ref, *part_refs):
-    w_sdt = rest_ref[:, :SR]
+    total = dot_t(s_hid_ref[...], rest_ref[:, :SR]) + scatter_rows(
+        spread_ref[...], rows_w_ref[...] * rows_out_ref[...]
+    )
     for k in range(R):
-        tok, row = slice(k * TOK, (k + 1) * TOK), slice(k * CAP, (k + 1) * CAP)
-        part = dot_t(s_hid_ref[tok, :], w_sdt) + exact_dot(
-            spread_ref[tok, :], rows_w_ref[row, :] * rows_out_ref[row, :]
-        )
-        part_refs[k][...] = part.astype(BF)
+        part_refs[k][...] = total[k * TOK : (k + 1) * TOK].astype(BF)
 
 
 def add_kernel(hidden_ref, *refs):
@@ -261,7 +277,9 @@
     cut = 2 * SR + 2 * FR
     out_ref[:, : 2 * SR] = t_dot(n2_ref[...], geg_ref[...]).astype(BF)
     out_ref[:, 2 * SR : cut] = t_dot(rows_in_ref[...], e_geg_ref[...]).astype(BF)
-    out_ref[:, cut:] = t_dot(rows_geo_ref[...], e_hid_ref[...]).astype(BF)
+    out_ref[:, cut : cut + FR] = t_dot(rows_geo_ref[...], e_hid_ref[...]).astype(BF)
+    if out_ref.shape[1] > cut + FR:
+        out_ref[:, cut + FR :] = jnp.zeros((CHUNK, out_ref.shape[1] - cut - FR), BF)
 
 
 def product_kernel(left_ref, right_ref, out_ref):
@@ -289,6 +307,24 @@
 
     out_ref[:, :QW] = t_dot(n1_ref[...], gq_ref[...]).astype(BF)
     out_ref[:, QW:] = t_dot(att_ref[...], ghb_ref[...]).astype(BF)
+
+
+def tail_kernel(R, HS, HR, KR, LR, NR, r_ref, n1_ref, n2_ref, gd_ref, lg_ref, gains_ref, *refs):
+    out_ref = refs[R]
+    W, n = DN + DV, HR // HS
+    step = pl.program_id(0)
+    out_ref[...] = jnp.zeros(out_ref.shape, BF)
+    for k in range(R):
+
+        @pl.when((r_ref[0] ^ (step // n)) == k)
+        def _():
+            for h in range(HS):
+                out_ref[h * KR : (h + 1) * KR, :W] = refs[k][(step % n) * HS + h]
+
+    out_ref[:, W : W + LR] = t_dot(n1_ref[...], gd_ref[...]).astype(BF)
+    out_ref[:, W + LR : W + LR + NR] = t_dot(n2_ref[...], lg_ref[...]).astype(BF)
+    cut = W + LR + NR
+    out_ref[: gains_ref.shape[1], cut : cut + 64] = gains_ref[0].astype(BF)
 
 
 def whole_block(shape):
@@ -302,7 +338,8 @@
         up_ref[:, j * SR : (j + 1) * SR] = blocks[j, :, SR:cut].astype(F32)
         e_gate_ref[:, j * FR : (j + 1) * FR] = blocks[j, :, cut : cut + FR].astype(F32)
         e_up_ref[:, j * FR : (j + 1) * FR] = blocks[j, :, cut + FR : cut + 2 * FR].astype(F32)
-        e_down_ref[j * FR : (j + 1) * FR, :] = blocks[j, :, cut + 2 * FR :].astype(F32).T
+        e_down = blocks[j, :, cut + 2 * FR : cut + 3 * FR].astype(F32)
+        e_down_ref[j * FR : (j + 1) * FR, :] = e_down.T
 
 
 def join_down_kernel(R, SR, blocks, down_ref):
@@ -331,7 +368,7 @@
                 j, h * KR : (h + 1) * KR, :W
             ].astype(F32)
         down_ref[j * LR : (j + 1) * LR, :] = blocks[j, :, W : W + LR].astype(F32).T
-        router_ref[j * NR : (j + 1) * NR, :] = blocks[j, :, W + LR :].astype(F32).T
+        router_ref[j * NR : (j + 1) * NR, :] = blocks[j, :, W + LR : W + LR + NR].astype(F32).T
 
 
 def join_blocks(kernel, R, r, pieces, outs):
@@ -421,9 +458,8 @@
             if R != 4:
                 return [(k, 0, block) for k, block in enumerate(gather(values))]
             mid = values.shape[0] // 2
-            values = by_rows(values)
-            side, other = by_rows(send(values, 1)), by_rows(send(values, 2))
-            top, low = by_rows(send(other[:mid], 1)), by_rows(send(side[mid:], 2))
+            side, other = send(values, 1), send(values, 2)
+            top, low = send(other[:mid], 1), send(side[mid:], 2)
             return [(0, 0, values), (1, 0, side), (2, 0, other), (3, 0, top), (3, mid, low)]
 
         def shard_gather(values):
@@ -447,40 +483,11 @@
         x_all = jnp.concatenate(gather(hidden_in))
         cot_all = jnp.concatenate(gather(cotangent))
 
+        CD, CR, CG = QW, QW + KVR + DR, QW + KVR + DR + NE
+        CH = -(-(CG + 64) // 128) * 128
+        KW = HS * KR * (DN + DV) // DL
         kv_piece = (
             part(kv_up, KR, 0).reshape(KR, HS, DN + DV).transpose(1, 0, 2).reshape(HS * KR, DN + DV)
-        )
-        head_own = jnp.concatenate([part(out_weight, DC), fold(kv_piece, DL)], axis=1)
-        head_all = shard_gather(head_own)
-        kvu_all = unfold_all(head_all[:, DC:], S, DL, HS * KR).reshape(H, KR, DN + DV)
-        out_all = head_all[:, :DC]
-        head_blocks = []
-        for k in range(R):
-            rk = r ^ k
-            piece = jnp.concatenate(
-                [
-                    lax.dynamic_slice_in_dim(out_all, rk * HR * DV, HR * DV, 0),
-                    fold(
-                        lax.dynamic_slice_in_dim(kvu_all, rk * HR, HR, 0).reshape(
-                            HR * KR, DN + DV
-                        ),
-                        HR * DV,
-                    ),
-                ],
-                axis=1,
-            )
-            head_blocks.append(send(piece, k) if k else piece)
-        head_nat = natural(head_blocks)
-        out_w = jnp.concatenate([b[:, :DC] for b in head_nat], axis=1)
-        kvu = jnp.concatenate(
-            [unfold(b[:, DC:], HR * KR).reshape(HR, KR, DN + DV) for b in head_nat], axis=1
-        )
-        kvu2 = jnp.concatenate(
-            [
-                kvu[:, :, :DN].transpose(1, 0, 2).reshape(KVR, HR * DN),
-                kvu[:, :, DN:].transpose(1, 0, 2).reshape(KVR, HR * DV),
-            ],
-            axis=1,
         )
 
         def gain_rows(one, two, kv):
@@ -506,15 +513,31 @@
                 kv_down,
                 router_weight,
                 gain_rows(norm_gain, mixer_gain, kv_gain),
+                jnp.zeros((DL, CH - CG - 64), BF),
+                part(out_weight, DC),
+                fold(kv_piece, DL),
             ],
             axis=1,
         )
         attn_all = shard_gather(attn_own)
-        CD, CR, CG = QW, QW + KVR + DR, QW + KVR + DR + NE
+        head_blocks = []
+        for k in range(R):
+            piece = lax.dynamic_slice_in_dim(attn_all, (r ^ k) * HR * DV, HR * DV, 0)[:, CH:]
+            head_blocks.append(send(piece, k) if k else piece)
+        if R == 4:
+            out_ws = kvus = head_blocks
+            kvu_spec = pl.BlockSpec((HR * KR, DN + DV), lambda i, r_ref: (0, DC // KW))
+        else:
+            head_nat = natural(head_blocks)
+            out_ws = [b[:, :DC] for b in head_nat]
+            kvus = [unfold_all(b[:, DC:], S // R, DL, HS * KR) for b in head_nat]
+            kvu_spec = whole_block((HR * KR, DN + DV))
+        out_w_spec = pl.BlockSpec((HR * DV, DC), lambda i, r_ref: (0, 0))
+        r_one = r.reshape(1)
         w_q = attn_all[:, :QW]
         w_down = attn_all[:, CD:CR]
         w_router = attn_all[:, CR:CG]
-        gain_all = attn_all[:, CG:].reshape(S, DL, 64).astype(F32)
+        gain_all = attn_all[:, CG : CG + 64].reshape(S, DL, 64).astype(F32)
         gain_one = gain_all[:, :GR].reshape(D)
         gain_two = gain_all[:, GR : 2 * GR].reshape(D)
         gain_kv = gain_all[:, 2 * GR, : KVR // S].reshape(KVR)
@@ -538,11 +561,10 @@
         xf = x_all.astype(F32)
         scale_one = inv_rms(xf)
         n1 = (xf * scale_one * gain_one).astype(BF)
-        qlat = dot(n1, attn_all)
+        qlat = dot(n1, attn_all[:, :CH])
         latent = qlat[:, CD : CD + KVR]
         scale_kv = inv_rms(latent)
         lat_n = (latent * scale_kv * gain_kv).astype(BF)
-        kv = dot(lat_n, kvu2).astype(BF)
 
         start = meta[:, 0].astype(F32)
         position = index.astype(F32)[None] - start
@@ -553,41 +575,40 @@
         bias = jnp.where(allowed, 0.0, NEGATIVE).astype(F32)
 
         def rows(width, column=0):
-            return pl.BlockSpec((TOK, width), lambda i: (i, column))
-
-        def whole(*shape):
-            return pl.BlockSpec(shape, lambda i: (0,) * len(shape))
+            return pl.BlockSpec((TOK, width), lambda i, r_ref: (i, column))
 
         HN = HR * DN
+        probs_spec = pl.BlockSpec((HR, TOK, TOK), lambda i, r_ref: (i, 0, 0))
         forward = pl.pallas_call(
             lambda *refs: attention_kernel(R, HR, *refs),
-            grid=(R,),
-            in_specs=[
-                rows(QW),
-                rows(128, (CD + KVR) // 128),
-                rows(2 * HN),
-                rows(128),
-                rows(128),
-                pl.BlockSpec((1, TOK, TOK), lambda i: (i, 0, 0)),
-                whole(HN, D),
-            ],
-            out_specs=[
-                rows(HN),
-                pl.BlockSpec((HR, TOK, TOK), lambda i: (i, 0, 0)),
-                rows(QW),
-                rows(256),
-            ]
-            + [whole(TOK, D)] * R,
+            grid_spec=pltpu.PrefetchScalarGridSpec(
+                num_scalar_prefetch=1,
+                grid=(R,),
+                in_specs=[
+                    rows(QW),
+                    rows(128, (CD + KVR) // 128),
+                    rows(KVR),
+                    rows(128),
+                    rows(128),
+                    pl.BlockSpec((1, TOK, TOK), lambda i, r_ref: (i, 0, 0)),
+                ]
+                + [out_w_spec] * R
+                + [kvu_spec] * R,
+                out_specs=[rows(HN), probs_spec, rows(QW), rows(256), rows(2 * HN)]
+                + [whole_block((TOK, D))] * R,
+                scratch_shapes=[pltpu.VMEM((TOK, D), BF)],
+            ),
             out_shape=[
                 jax.ShapeDtypeStruct((T, HN), BF),
                 jax.ShapeDtypeStruct((R * HR, TOK, TOK), F32),
                 jax.ShapeDtypeStruct((T, QW), BF),
                 jax.ShapeDtypeStruct((T, 256), BF),
+                jax.ShapeDtypeStruct((T, 2 * HN), BF),
             ]
             + [jax.ShapeDtypeStruct((TOK, D), BF)] * R,
         )
-        att, probs, q_b, kr_b, *out_parts = forward(
-            qlat, qlat, kv, cosine, sine, bias, out_w
+        att, probs, q_b, kr_b, kv, *out_parts = forward(
+            r_one, qlat, qlat, lat_n, cosine, sine, bias, *out_ws, *kvus
         )
         x_own = hidden_in.astype(F32)
         hidden = x_own + reduce_parts(out_parts)
@@ -628,7 +649,9 @@
         e_act, e_slope = silu_parts(e_g)
         e_hid = (e_act * e_u).astype(BF)
         rows_geo = (rows_w * rows_g).astype(BF)
-        spread = dispatch.transpose(0, 2, 1).reshape(T, CAP)
+        slot = (place + CAP * jnp.arange(R)[:, None]).reshape(T, 1)
+        spread = (slot == jnp.arange(2 * R * CAP)[None] % (R * CAP)) & (chosen.reshape(T, 1) > 0.5)
+        spread = (spread & (place.reshape(T, 1) < CAP)).astype(BF)
         chosen_wide = jnp.broadcast_to(chosen.reshape(T, 1), (T, 128))
         operands = (
             cot_all,
@@ -699,7 +722,7 @@
         def columns(values):
             return pl.BlockSpec((values.shape[0], CHUNK), lambda i: (0, i))
 
-        GW = 2 * SR + 3 * FR
+        GW = -(-(2 * SR + 3 * FR) // 128) * 128
         gu_part = pl.pallas_call(
             lambda *refs: ffn_weight_kernel(SR, FR, *refs),
             grid=(STEPS,),
@@ -716,10 +739,15 @@
         )(n2, s_geg, rows_in, e_geg, rows_geo, e_hid)
         gu_red = shard_reduce(gu_part)
         operands = (s_hid, rest_all, spread, rows_w, rows_out)
+        specs = {
+            1: pl.BlockSpec((CHUNK, SR + FR), lambda i: (i, 0)),
+            4: pl.BlockSpec((RC, CHUNK), lambda i: (0, i)),
+        }
         out_ffn = pl.pallas_call(
             lambda *refs: ffn_out_kernel(R, SR, *refs),
-            in_specs=[whole_block(v.shape) for v in operands],
-            out_specs=[whole_block((TOK, D))] * R,
+            grid=(STEPS,),
+            in_specs=[specs.get(n, whole_block(v.shape)) for n, v in enumerate(operands)],
+            out_specs=[pl.BlockSpec((TOK, CHUNK), lambda i: (0, i))] * R,
             out_shape=[jax.ShapeDtypeStruct((TOK, D), BF)] * R,
         )(*operands)
         out_ffn = [out_ffn[0]] + [send(out_ffn[k], k) for k in range(1, R)]
@@ -741,30 +769,33 @@
 
         backward = pl.pallas_call(
             lambda *refs: attention_grad_kernel(R, HR, *refs),
-            grid=(R,),
-            in_specs=[whole(TOK, D)] * R
-            + [
-                rows(HN),
-                pl.BlockSpec((HR, TOK, TOK), lambda i: (i, 0, 0)),
-                rows(2 * HN),
-                rows(QW),
-                rows(256),
-                rows(128),
-                rows(128),
-                whole(HN, D),
-                whole(KVR, 2 * HN),
-            ],
-            out_specs=[rows(QW), rows(2 * HN)] + [whole(TOK, KVR + 128)] * R,
+            grid_spec=pltpu.PrefetchScalarGridSpec(
+                num_scalar_prefetch=1,
+                grid=(R,),
+                in_specs=[whole_block((TOK, D))] * R
+                + [out_w_spec] * R
+                + [kvu_spec] * R
+                + [
+                    rows(HN),
+                    probs_spec,
+                    rows(2 * HN),
+                    rows(QW),
+                    rows(256),
+                    rows(128),
+                    rows(128),
+                ],
+                out_specs=[rows(QW), rows(2 * HN)] + [whole_block((TOK, KVR + 128))] * R,
+                scratch_shapes=[pltpu.VMEM((TOK, D), BF), pltpu.VMEM((TOK, KVR + 128), BF)],
+            ),
             out_shape=[
                 jax.ShapeDtypeStruct((T, QW), BF),
                 jax.ShapeDtypeStruct((T, 2 * HN), BF),
             ]
             + [jax.ShapeDtypeStruct((TOK, KVR + 128), BF)] * R,
-            scratch_shapes=[pltpu.VMEM((TOK, D), BF)],
         )
         ghb = gather(grad_hidden.astype(BF))
         gq, g_kv, *glat_parts = backward(
-            *ghb, att, probs, kv, q_b, kr_b, cosine, sine, out_w, kvu2
+            r_one, *ghb, *out_ws, *kvus, att, probs, kv, q_b, kr_b, cosine, sine
         )
         attn_part = pl.pallas_call(
             lambda *refs: attention_weight_kernel(R, QW, *refs),
@@ -803,46 +834,53 @@
         )
         g_norm = jnp.sum(gn1_part * xf * scale_one, axis=0)
 
-        g_kvu2 = t_dot(lat_n, g_kv).astype(BF)
-        g_kvu = jnp.concatenate(
-            [
-                g_kvu2[:, :HN].reshape(KVR, HR, DN),
-                g_kvu2[:, HN:].reshape(KVR, HR, DV),
-            ],
-            axis=2,
-        ).transpose(1, 0, 2)
+        g_kvu = t_dot(lat_n, g_kv).astype(BF).reshape(KVR, HR, DN + DV).transpose(1, 0, 2)
         kvu_blocks = []
         for k in range(R):
             b = lax.dynamic_slice_in_dim(g_kvu, (r ^ k) * KR, KR, 1)
             kvu_blocks.append(send(b, k) if k else b)
-        g_kvu_all = jnp.concatenate(natural(kvu_blocks))
-        g_kvu_all = fold_all(g_kvu_all.reshape(H * KR, DN + DV), S, DL)
-
-        g_router = t_dot(n2, part(logits_grad(gc_total), NR))
-        g_down = t_dot(n1, gd)
+        lg = part(logits_grad(gc_total), NR)
         vectors = jnp.concatenate([g_norm, g_mixer, g_kvgain])
         summed = sum(gather(vectors))
         g_gains = gain_rows(
             summed[:D].reshape(S, DL),
             summed[D : 2 * D].reshape(S, DL),
             summed[2 * D :].reshape(S, KVR // S),
-        ).reshape(D, 64)
+        )
         attn_red = shard_reduce(attn_part)
-        pad = (-(LR + NR + 64)) % 128
-        tail_red = shard_reduce(
-            jnp.concatenate(
+        TW = -(-(KW + LR + NR + 64) // 128) * 128
+        if KW == DN + DV:
+            tail_part = pl.pallas_call(
+                lambda *refs: tail_kernel(R, HS, HR, KR, LR, NR, *refs),
+                grid_spec=pltpu.PrefetchScalarGridSpec(
+                    num_scalar_prefetch=1,
+                    grid=(S,),
+                    in_specs=[
+                        pl.BlockSpec((T, DL), lambda i, r_ref: (0, i)),
+                        pl.BlockSpec((T, DL), lambda i, r_ref: (0, i)),
+                        whole_block(gd.shape),
+                        whole_block(lg.shape),
+                        pl.BlockSpec((1, 16, 64), lambda i, r_ref: (i, 0, 0)),
+                    ]
+                    + [whole_block((HR, KR, DN + DV))] * R,
+                    out_specs=pl.BlockSpec((DL, TW), lambda i, r_ref: (i, 0)),
+                ),
+                out_shape=jax.ShapeDtypeStruct((D, TW), BF),
+            )(r_one, n1, n2, gd, lg, g_gains[:, :16], *kvu_blocks)
+        else:
+            g_kvu_all = jnp.concatenate(natural(kvu_blocks))
+            tail_part = jnp.concatenate(
                 [
-                    g_kvu_all,
-                    g_down.astype(BF),
-                    g_router.astype(BF),
-                    g_gains.astype(BF),
-                    jnp.zeros((D, pad), BF),
+                    fold_all(g_kvu_all.reshape(H * KR, DN + DV), S, DL),
+                    t_dot(n1, gd).astype(BF),
+                    t_dot(n2, lg).astype(BF),
+                    g_gains.reshape(D, 64).astype(BF),
+                    jnp.zeros((D, TW - KW - LR - NR - 64), BF),
                 ],
                 axis=1,
-            ),
-        )
-
-        KW = HS * KR * (DN + DV) // DL
+            )
+        tail_red = shard_reduce(tail_part)
+
         (own_sd,) = join_blocks(
             lambda *refs: join_down_kernel(R, SR, *refs), R, r, gather_pieces(down_red), [(SH, DL)]
         )
@@ -860,7 +898,7 @@
             gather_pieces(attn_red),
             [(DL, H * (DN + DR)), (DL, D)],
         )
-        tail_pieces = gather(tail_red[:, : KW + LR + NR])
+        tail_pieces = gather(tail_red)
         gains_red = tail_red[:, KW + LR + NR : KW + LR + NR + 64].astype(F32)
         if KW == DN + DV:
             own_ku, own_kd, own_rw = join_blocks(
@@ -883,7 +921,7 @@
                 ]
             ).astype(F32)
             own_kd = jnp.concatenate([b[:, KW : KW + LR] for b in tail_nat], axis=1).astype(F32)
-            own_rw = jnp.concatenate([b[:, KW + LR :] for b in tail_nat], axis=1).astype(F32)
+            own_rw = jnp.concatenate([b[:, KW + LR : KW + LR + NR] for b in tail_nat], axis=1).astype(F32)
         return (
             result,
             grad_input,

time: 614 us -> 643 us (1.047)
  waiting for transfers between devices: 269 us -> 316 us
  local copies, waits for them, and re-layouts: 68.4 us -> 52.9 us
  starting transfers between devices: 84 us -> 76.7 us
    all_gather x4 -> x3, waiting for transfers between devices: 33 us -> 55.6 us  [shard_gather(): return lax.all_gather(values, SHD, axis=0, tiled=True)]
    ppermute x63, waiting for transfers between devices: 227 us -> 245 us  [send(): return lax.ppermute(values, REP, links[k])]
    reduce_scatter x4, waiting for transfers between devices: 8.05 us -> 16.1 us  [shard_reduce(): return lax.psum_scatter(values, SHD, scatter_dimension=0, tiled=True)]
    concatenate x4 -> x0, local copies, waits for them, and re-layouts: 7.06 us -> none  [the longest x1 5.62 us: local(): jnp.concatenate([g_kvu_all, g_down.astype(BF), g_router.astype(BF), g_gai...]
    ppermute x63, starting transfers between devices: 83.1 us -> 76.1 us  [send(): return lax.ppermute(values, REP, links[k])]
    unnamed x154 -> x171, local copies, waits for them, and re-layouts: 13.3 us -> 18.6 us
    dot_general x5 -> x4, matrix products: 20.4 us -> 15.2 us  [dot(): return jnp.dot(left, right, preferred_element_type=F32)]
    pallas_call x3 -> x4, Pallas kernels: 37.9 us -> 41.9 us  [the longest x1 14.3 us: local(): forward(r_one, qlat, qlat, lat_n, cosine, sine, bias, *out_ws, *kvus)]
  transfers between devices with their start and end apart: 71 -> 70, of which waited for: 39 -> 33; matrix products, arithmetic and copies ran while one was open for 20% -> 16% of each run, Pallas kernels for 11% -> 11%
where the time goes in v2:
time: 643 us; the launch traced here: 633 us
  waiting for transfers between devices  316 us (49%)
  Pallas kernels  104 us (16%)
  starting transfers between devices  76.7 us (12%)
  local copies, waits for them, and re-layouts  52.9 us (8%)
  other arithmetic  40.4 us (6%)
  matrix products  26.8 us (4%)
  between operations  15.5 us (2%)
    ppermute x63, waiting for transfers between devices, send(): return lax.ppermute(values, REP, links[k])  245 us
    ppermute x63, starting transfers between devices, send(): return lax.ppermute(values, REP, links[k])  76.1 us
    all_gather x3, waiting for transfers between devices, shard_gather(): return lax.all_gather(values, SHD, axis=0, tiled=True)  55.6 us
    pallas_call x4, Pallas kernels, join_blocks(): pl.pallas_call(body, in_specs=[pl.BlockSpec(memory_space=pltpu.SMEM)] + [...  19.3 us
    unnamed x171, local copies, waits for them, and re-layouts  18.6 us
    pallas_call x1, Pallas kernels, local(): pl.pallas_call(lambda *refs: ffn_grad_kernel(R, SR, FR, *refs), grid=(2 *...  17.1 us
    reduce_scatter x4, waiting for transfers between devices, shard_reduce(): return lax.psum_scatter(values, SHD, scatter_dimension=0, tiled=True)  16.1 us
    dot_general x4, matrix products, dot(): return jnp.dot(left, right, preferred_element_type=F32)  15.2 us
  transfers between devices with their start and end apart: 70, of which 33 were waited for; matrix products, arithmetic and copies ran while one was open for 16% of the time, Pallas kernels for 11%

profile of v2, /device:TPU:0, one launch (start us, length us, event | category | flops | bytes accessed | tf_op | source)
XLA Modules:
  0.0 632.6 jit_solution(13927058121522169733)
XLA Ops:
  12.0 2.2 concatenate.39
  17.2 2.1 concatenate.42
  19.4 3.9 collective-permute-start.2
  25.9 1.9 collective-permute-start.3
  32.3 3.1 collective-permute-done.5
  37.2 9.4 %collective-permute-done.4 = bf16[8,128]{1,0:T(8,128)(2,1)S(1)} collective-permute-done((bf16[8,128]{1,0:T(8,128)(2,1)S(1)}, bf16[8,128]{1,0:T(8,128)(2,1)S(1)}, u32[]{:S(2)}, u32[]{:S(2)}) %collective-permute-start.4) | collective-permute-done | bytes 2080 | tf_op jit(solution)/shard_map/ppermute | solution.py:411
  52.2 55.6 %all-gather.4.cloned.1.call-done = bf16[2048,2304]{1,0:T(8,128)(2,1)} async-done(((bf16[256,2304]{1,0:T(8,128)(2,1)}), bf16[2048,2304]{1,0:T(8,128)(2,1)}) %all-gather.4.cloned.1.call-update) | async-done | bytes 9437200 | tf_op jit(solution)/shard_map/all_gather | solution.py:466
  107.8 2.2 fusion.56
  111.2 3.8 fusion.57
  118.4 3.4 fusion.6.refs_1_
  121.8 3.4 fusion.refs_1_.refs_2_
  127.3 8.4 %collective-permute-done.6.refs_8_.refs_12_.refs_6_.refs_10_ = bf16[512,768]{1,0:T(8,128)(2,1)} collective-permute-done((bf16[512,768]{1,0:T(8,128)(2,1)}, bf16[512,768]{1,0:T(8,128)(2,1)}, u32[]{:S(2)}, u32[]{:S(2)}) %collective-permute-start.6) | collective-permute-done | bytes 786464 | tf_op jit(solution)/shard_map/ppermute | solution.py:411
  135.7 17.3 %collective-permute-done.7.refs_9_.refs_13_.refs_7_.refs_11_ = bf16[512,768]{1,0:T(8,128)(2,1)} collective-permute-done((bf16[512,768]{1,0:T(8,128)(2,1)}, bf16[512,768]{1,0:T(8,128)(2,1)}, u32[]{:S(2)}, u32[]{:S(2)}) %collective-permute-start.7) | collective-permute-done | bytes 786464 | tf_op jit(solution)/shard_map/ppermute | solution.py:411
  153.0 14.3 %shard_map.297 = (bf16[512,512]{1,0:T(8,128)(2,1)}, f32[16,128,128]{2,1,0:T(8,128)}, bf16[512,768]{1,0:T(8,128)(2,1)}, bf16[512,256]{1,0:T(8,128)(2,1)}, bf16[51...) custom-call(s32[1]{0:T(128)} %bitcast.refs_0_.r_ref, ...), custom_call_target="tpu_custom_call" | custom-call | tf_op jit(solution)/shard_map/pallas_call | solution.py:610
  173.1 10.2 %collective-permute-done.11 = bf16[128,2048]{1,0:T(8,128)(2,1)S(1)} collective-permute-done((bf16[128,2048]{1,0:T(8,128)(2,1)}, bf16[128,2048]{1,0:T(8,128)(2,1)S(1)}, u32[]{:S(2)}, u32[]{:S(2)}) %collective-permute-start.11) | collective-permute-done | bytes 524320 | tf_op jit(solution)/shard_map/ppermute | solution.py:411
  184.9 9.6 %collective-permute-done.10 = bf16[128,2048]{1,0:T(8,128)(2,1)S(1)} collective-permute-done((bf16[128,2048]{1,0:T(8,128)(2,1)}, bf16[128,2048]{1,0:T(8,128)(2,1)S(1)}, u32[]{:S(2)}, u32[]{:S(2)}) %collective-permute-start.10) | collective-permute-done | bytes 524320 | tf_op jit(solution)/shard_map/ppermute | solution.py:411
  195.3 2.2 multiply_reduce_fusion.2
  206.0 11.1 %collective-permute-done.14 = bf16[128,2048]{1,0:T(8,128)(2,1)S(1)} collective-permute-done((bf16[128,2048]{1,0:T(8,128)(2,1)S(1)}, bf16[128,2048]{1,0:T(8,128)(2,1)S(1)}, u32[]{:S(2)}, u32[]{:S(2)}) %collective-permute-start.14) | collective-permute-done | bytes 524320 | tf_op jit(solution)/shard_map/ppermute | solution.py:411
  217.1 9.4 %collective-permute-done.13 = bf16[128,2048]{1,0:T(8,128)(2,1)S(1)} collective-permute-done((bf16[128,2048]{1,0:T(8,128)(2,1)S(1)}, bf16[128,2048]{1,0:T(8,128)(2,1)S(1)}, u32[]{:S(2)}, u32[]{:S(2)}) %collective-permute-start.13) | collective-permute-done | bytes 524320 | tf_op jit(solution)/shard_map/ppermute | solution.py:411
  226.7 3.0 fusion.67
  238.6 2.8 fusion.11
  242.6 6.0 fusion.2
  248.5 2.7 multiply_multiply_fusion
  252.9 17.1 %shard_map.298 = (bf16[512,1408]{1,0:T(8,128)(2,1)}, bf16[64,704]{1,0:T(8,128)(2,1)}, f32[64,2048]{1,0:T(8,128)}, f32[512,128]{1,0:T(8,128)}, bf16[128,2048]{1,0...) custom-call(bf16[512,2048]{1,0:T(8,128)(2,1)} %copy-done.5, ...), custom_call_target="tpu_custom_call" | custom-call | tf_op jit(solution)/shard_map/pallas_call | solution.py:694
  270.0 9.3 %shard_map.306 = bf16[2048,2560]{1,0:T(8,128)(2,1)} custom-call(bf16[512,2048]{1,0:T(8,128)(2,1)} %copy-done.2, bf16[512,1408]{1,0:T(8,128)(2,1)} %get-tuple-element.83.refs_1_, bf16[64,2048]{1,0:T(8,128)(2,1)} %bitcast.95, bf16[64,704]{1,0:T(8,128)(2,1)} %get-tuple-element.84.refs_3_, bf16[64,2048]{1,0:T(8,128)(2,1)} %multiply_convert_fusion.3.refs_8_.refs_4_, ...), custom_call_target="tpu_custom_call" | custom-call | tf_op jit(solution)/shard_map/pallas_call | solution.py:726
  287.9 12.2 %collective-permute-done.23 = bf16[128,2048]{1,0:T(8,128)(2,1)S(1)} collective-permute-done((bf16[128,2048]{1,0:T(8,128)(2,1)S(1)}, bf16[128,2048]{1,0:T(8,128)(2,1)S(1)}, u32[]{:S(2)}, u32[]{:S(2)}) %collective-permute-start.23) | collective-permute-done | bytes 524320 | tf_op jit(solution)/shard_map/ppermute | solution.py:411
  300.1 9.5 %collective-permute-done.22 = bf16[128,2048]{1,0:T(8,128)(2,1)S(1)} collective-permute-done((bf16[128,2048]{1,0:T(8,128)(2,1)S(1)}, bf16[128,2048]{1,0:T(8,128)(2,1)S(1)}, u32[]{:S(2)}, u32[]{:S(2)}) %collective-permute-start.22) | collective-permute-done | bytes 524320 | tf_op jit(solution)/shard_map/ppermute | solution.py:411
  310.2 2.6 fusion.54
  318.0 9.6 %collective-permute-done.24.refs_2_.refs_4_ = bf16[128,2048]{1,0:T(8,128)(2,1)S(1)} collective-permute-done((bf16[128,2048]{1,0:T(8,128)(2,1)S(1)}, bf16[128,2048]{1,0:T(8,128)(2,1)S(1)}, u32[]{:S(2)}, u32[]{:S(2)}) %collective-permute-start.24) | collective-permute-done | bytes 524320 | tf_op jit(solution)/shard_map/ppermute | solution.py:411
  327.6 11.5 %collective-permute-done.25.refs_3_.refs_5_ = bf16[128,2048]{1,0:T(8,128)(2,1)S(1)} collective-permute-done((bf16[128,2048]{1,0:T(8,128)(2,1)S(1)}, bf16[128,2048]{1,0:T(8,128)(2,1)S(1)}, u32[]{:S(2)}, u32[]{:S(2)}) %collective-permute-start.25) | collective-permute-done | bytes 524320 | tf_op jit(solution)/shard_map/ppermute | solution.py:411
  340.2 13.3 %shard_map.301 = (bf16[512,768]{1,0:T(8,128)(2,1)}, bf16[512,1024]{1,0:T(8,128)(2,1)}, bf16[128,640]{1,0:T(8,128)(2,1)}, bf16[128,640]{1,0:T(8,128)(2,1)}, bf16[...) custom-call(s32[1]{0:T(128)} %bitcast.refs_0_.r_ref, bf16[128,2048]{1,0:T(8,128)(2,1)} %copy-done.13, ...), custom_call_target="tpu_custom_call" | custom-call | tf_op jit(solution)/shard_map/pallas_call | solution.py:797
  358.0 3.4 collective-permute-done.29
  371.8 2.3 copy.126
  374.0 2.2 collective-permute-done.31
  380.1 7.0 %fusion.8 = (f32[2048]{0:T(1024)S(1)}, bf16[512,2048]{1,0:T(8,128)(2,1)}, f32[512,2048]{1,0:T(8,128)}) fusion(f32[512]{0:T(512)S(1)} %copy-done.63, bf16[128,2048]{1,0:T(8,128)(2,1)S(1)} %copy-done.27, bf16[128,2048]{1,0:T(8,128)(2,1)S(1)} %copy-done.29, bf16[128,2048]{1,0:T(8,128)(2,1)S(1)} %copy-done.31, bf16[128,2048]{1,0:T(8,128)(2,1)S(1)} %copy-done.9, ...), kind=kOutput, calls=%fused_computation.11 | convolution fusion | flops 1624242176 | bytes 16525312 | tf_op jit(solution)/shard_map/dot_general | solution.py:32
  387.7 2.2 collective-permute-start.40
  393.7 2.1 collective-permute-start.44
  396.7 3.7 collective-permute-done.42.refs_7_
  400.4 3.8 collective-permute-done.43.refs_8_
  404.9 8.2 %shard_map.302 = bf16[2048,512]{1,0:T(8,128)(2,1)} custom-call(s32[1]{0:T(128)} %bitcast.refs_0_.r_ref, bf16[512,2048]{1,0:T(8,128)(2,1)} %copy-done.7, bf16[512,2048]{1,0:T(8,128)(2,1)} %copy-done.2, bf16[512,144]{1,0:T(8,128)(2,1)} %copy-done.17, bf16[512,16]{1,0:T(8,128)(2,1)} %fusion.29.refs_4_, f32[8,16,64]{2,1,0:T(8,128)} %fusion.38.refs_5_, ...), custom_call_target="tpu_custom_call" | custom-call | tf_op jit(solution)/shard_map/pallas_call | solution.py:853
  413.2 5.5 shard_map.308
  423.3 11.3 %collective-permute-done.45.refs_8_ = bf16[512,512]{1,0:T(8,128)(2,1)S(1)} collective-permute-done((bf16[512,512]{1,0:T(8,128)(2,1)S(1)}, bf16[512,512]{1,0:T(8,128)(2,1)S(1)}, u32[]{:S(2)}, u32[]{:S(2)}) %collective-permute-start.45) | collective-permute-done | bytes 524320 | tf_op jit(solution)/shard_map/ppermute | solution.py:411
  434.6 7.0 %collective-permute-done.46.refs_9_ = bf16[512,512]{1,0:T(8,128)(2,1)S(1)} collective-permute-done((bf16[512,512]{1,0:T(8,128)(2,1)S(1)}, bf16[512,512]{1,0:T(8,128)(2,1)S(1)}, u32[]{:S(2)}, u32[]{:S(2)}) %collective-permute-start.46) | collective-permute-done | bytes 524320 | tf_op jit(solution)/shard_map/ppermute | solution.py:411
  443.2 7.7 %shard_map.303 = bf16[2048,1280]{1,0:T(8,128)(2,1)} custom-call(s32[1]{0:T(128)} %bitcast.refs_0_.r_ref, bf16[512,2048]{1,0:T(8,128)(2,1)} %copy-done.7, bf16[512,768]{1,0:T(8,128)(2,1)} %get-tuple-element.71.refs_2_, bf16[128,2048]{1,0:T(8,128)(2,1)} %copy-done.13, bf16[128,2048]{1,0:T(8,128)(2,1)} %copy-done.22, bf16[128,2048]{1,0:T(8,128)(2,1)} %copy-done.23, ...), custom_call_target="tpu_custom_call" | custom-call | tf_op jit(solution)/shard_map/pallas_call | solution.py:800
  451.6 6.1 shard_map.299
  458.7 2.5 collective-permute-start.20
  462.2 2.5 fusion.58
  464.7 8.0 %collective-permute-done.18.refs_1_ = bf16[128,2048]{1,0:T(8,128)(2,1)S(1)} collective-permute-done((bf16[128,2048]{1,0:T(8,128)(2,1)}, bf16[128,2048]{1,0:T(8,128)(2,1)S(1)}, u32[]{:S(2)}, u32[]{:S(2)}) %collective-permute-start.18) | collective-permute-done | bytes 524320 | tf_op jit(solution)/shard_map/ppermute | solution.py:411
  473.1 7.6 %collective-permute-done.19.refs_2_ = bf16[128,2048]{1,0:T(8,128)(2,1)S(1)} collective-permute-done((bf16[128,2048]{1,0:T(8,128)(2,1)}, bf16[128,2048]{1,0:T(8,128)(2,1)S(1)}, u32[]{:S(2)}, u32[]{:S(2)}) %collective-permute-start.19) | collective-permute-done | bytes 524320 | tf_op jit(solution)/shard_map/ppermute | solution.py:411
  485.5 38.1 %collective-permute-done.35 = bf16[128,2048]{1,0:T(8,128)(2,1)S(1)} collective-permute-done((bf16[128,2048]{1,0:T(8,128)(2,1)S(1)}, bf16[128,2048]{1,0:T(8,128)(2,1)S(1)}, u32[]{:S(2)}, u32[]{:S(2)}) %collective-permute-start.35) | collective-permute-done | bytes 524320 | tf_op jit(solution)/shard_map/ppermute | solution.py:411
  523.7 3.0 shard_map.300
  526.7 4.2 collective-permute-done.34
  532.1 2.0 fusion.19
  534.1 16.1 %reduce-scatter.7.cloned.1.call-done.refs_0_ = bf16[256,1280]{1,0:T(8,128)(2,1)} async-done(((bf16[2048,1280]{1,0:T(8,128)(2,1)}), bf16[256,1280]{1,0:T(8,128)(2,1)}) %reduce-scatter.7.cloned.1.call-update) | async-done | bytes 655376 | tf_op jit(solution)/shard_map/reduce_scatter | solution.py:469
  556.6 3.0 fusion.18
  559.6 2.0 slice.322
  561.6 6.3 %collective-permute-done.48.refs_1_ = bf16[256,1280]{1,0:T(8,128)(2,1)S(1)} collective-permute-done((bf16[256,1280]{1,0:T(8,128)(2,1)}, bf16[256,1280]{1,0:T(8,128)(2,1)S(1)}, u32[]{:S(2)}, u32[]{:S(2)}) %collective-permute-start.48) | collective-permute-done | bytes 655392 | tf_op jit(solution)/shard_map/ppermute | solution.py:411
  569.5 5.6 collective-permute-done.49.refs_2_
  578.6 2.1 collective-permute-done.53.refs_2_
  586.5 13.8 %collective-permute-done.61.refs_3_ = bf16[128,704]{1,0:T(8,128)(2,1)S(1)} collective-permute-done((bf16[128,704]{1,0:T(8,128)(2,1)S(1)}, bf16[128,704]{1,0:T(8,128)(2,1)S(1)}, u32[]{:S(2)}, u32[]{:S(2)}) %collective-permute-start.61) | collective-permute-done | bytes 180256 | tf_op jit(solution)/shard_map/ppermute | solution.py:411
  603.0 2.9 shard_map.305
  606.6 3.5 shard_map.309
  610.9 5.2 shard_map.304
  617.8 7.7 %shard_map.307 = (f32[256,2816]{1,0:T(8,128)}, f32[256,2816]{1,0:T(8,128)}, f32[256,1408]{1,0:T(8,128)}, f32[256,1408]{1,0:T(8,128)}, f32[1408,256]{1,0:T(8,128)}) custom-call(s32[1]{0:T(128)} %bitcast.refs_0_.r_ref, bf16[256,2560]{1,0:T(8,128)(2,1)} %reduce-scatter.9.cloned.1.call-done.refs_0_, bf16[256,2560]{1,0:T(8,128)(2,1)} %copy-done.18, ...), custom_call_target="tpu_custom_call" | custom-call | tf_op jit(solution)/shard_map/pallas_call | solution.py:383
  (409 shorter events, 135.0 us)
Async XLA Ops:
  7.2 100.6 %all-gather.4.cloned.1.call-start = ((), (), s32[]{:S(2)}) async-start(), calls=%async_computation.4 | async-start | bytes 10616832 | tf_op jit(solution)/shard_map/all_gather | solution.py:466
  14.2 224.4 %all-gather.6.cloned.1.call-start = ((), (), s32[]{:S(2)}) async-start(), calls=%async_computation.5 | async-start | bytes 10027008 | tf_op jit(solution)/shard_map/all_gather | solution.py:466
  19.4 232.7 %all-gather.8.cloned.1.call-start = ((), (), s32[]{:S(2)}) async-start(), calls=%async_computation.6 | async-start | bytes 5308416 | tf_op jit(solution)/shard_map/all_gather | solution.py:466
  19.4 32.2 %collective-permute-start.2 = (bf16[128,2048]{1,0:T(8,128)(2,1)S(1)}, bf16[128,2048]{1,0:T(8,128)(2,1)S(1)}, u32[]{:S(2)}, u32[]{:S(2)}) collective-permute-start(bf16[128,2048]{1,0:T(8,128)(2,1)S(1)} %copy-done.8), channel_id=1, source_target_pairs={{0,24},{8,16},{16,8},{24,0},{1,25},{9,17},{17,9},{25,1},{2,26},{10... | collective-permute-start | bytes 1572872 | tf_op jit(solution)/shard_map/ppermute | solution.py:411
  23.4 28.3 %collective-permute-start.1 = (bf16[128,2048]{1,0:T(8,128)(2,1)S(1)}, bf16[128,2048]{1,0:T(8,128)(2,1)S(1)}, u32[]{:S(2)}, u32[]{:S(2)}) collective-permute-start(bf16[128,2048]{1,0:T(8,128)(2,1)S(1)} %copy-done.8), channel_id=1, source_target_pairs={{0,16},{8,24},{16,0},{24,8},{1,17},{9,25},{17,1},{25,9},{2,18},{10... | collective-permute-start | bytes 1572872 | tf_op jit(solution)/shard_map/ppermute | solution.py:411
  24.3 11.1 %collective-permute-start.5 = (bf16[8,128]{1,0:T(8,128)(2,1)S(1)}, bf16[8,128]{1,0:T(8,128)(2,1)S(1)}, u32[]{:S(2)}, u32[]{:S(2)}) collective-permute-start(bf16[8,128]{1,0:T(8,128)(2,1)S(1)} %get-tuple-element.148), channel_id=1, source_target_pairs={{0,24},{8,16},{16,8},{24,0},{1,25},{9,17},{17,9},{25,1},{2,26},{10... | collective-permute-start | bytes 6152 | tf_op jit(solution)/shard_map/ppermute | solution.py:411
  25.8 20.8 %collective-permute-start.4 = (bf16[8,128]{1,0:T(8,128)(2,1)S(1)}, bf16[8,128]{1,0:T(8,128)(2,1)S(1)}, u32[]{:S(2)}, u32[]{:S(2)}) collective-permute-start(bf16[8,128]{1,0:T(8,128)(2,1)S(1)} %get-tuple-element.148), channel_id=1, source_target_pairs={{0,16},{8,24},{16,0},{24,8},{1,17},{9,25},{17,1},{25,9},{2,18},{10... | collective-permute-start | bytes 6152 | tf_op jit(solution)/shard_map/ppermute | solution.py:411
  25.9 22.5 %collective-permute-start.3 = (bf16[8,128]{1,0:T(8,128)(2,1)S(1)}, bf16[8,128]{1,0:T(8,128)(2,1)S(1)}, u32[]{:S(2)}, u32[]{:S(2)}) collective-permute-start(bf16[8,128]{1,0:T(8,128)(2,1)S(1)} %get-tuple-element.148), channel_id=1, source_target_pairs={{0,8},{8,0},{16,24},{24,16},{1,9},{9,1},{17,25},{25,17},{2,10},{10... | collective-permute-start | bytes 6152 | tf_op jit(solution)/shard_map/ppermute | solution.py:411
  31.1 430.0 %reduce-scatter.9.cloned.1.call-start = ((), (), s32[]{:S(2)}) async-start(), calls=%async_computation.9 | async-start | bytes 11796480 | tf_op jit(solution)/shard_map/reduce_scatter | solution.py:469
  35.5 16.2 %collective-permute-start = (bf16[128,2048]{1,0:T(8,128)(2,1)S(1)}, bf16[128,2048]{1,0:T(8,128)(2,1)S(1)}, u32[]{:S(2)}, u32[]{:S(2)}) collective-permute-start(bf16[128,2048]{1,0:T(8,128)(2,1)S(1)} %copy-done.8), channel_id=1, source_target_pairs={{0,8},{8,0},{16,24},{24,16},{1,9},{9,1},{17,25},{25,17},{2,10},{10... | collective-permute-start | bytes 1572872 | tf_op jit(solution)/shard_map/ppermute | solution.py:411
  46.6 154.4 %collective-permute-start.15 = (bf16[128,2048]{1,0:T(8,128)(2,1)}, bf16[128,2048]{1,0:T(8,128)(2,1)}, u32[]{:S(2)}, u32[]{:S(2)}) collective-permute-start(bf16[128,2048]{1,0:T(8,128)(2,1)} %param.35), channel_id=1, source_target_pairs={{0,8},{8,0},{16,24},{24,16},{1,9},{9,1},{17,25},{25,17},{2,10},{10... | collective-permute-start | bytes 1572872 | tf_op jit(solution)/shard_map/ppermute | solution.py:411
  48.4 154.6 %collective-permute-start.16 = (bf16[128,2048]{1,0:T(8,128)(2,1)}, bf16[128,2048]{1,0:T(8,128)(2,1)}, u32[]{:S(2)}, u32[]{:S(2)}) collective-permute-start(bf16[128,2048]{1,0:T(8,128)(2,1)} %param.35), channel_id=1, source_target_pairs={{0,16},{8,24},{16,0},{24,8},{1,17},{9,25},{17,1},{25,9},{2,18},{10... | collective-permute-start | bytes 1572872 | tf_op jit(solution)/shard_map/ppermute | solution.py:411
  114.9 20.7 %collective-permute-start.6 = (bf16[512,768]{1,0:T(8,128)(2,1)}, bf16[512,768]{1,0:T(8,128)(2,1)}, u32[]{:S(2)}, u32[]{:S(2)}) collective-permute-start(bf16[512,768]{1,0:T(8,128)(2,1)} %get-tuple-element.106), channel_id=1, source_target_pairs={{0,8},{8,0},{16,24},{24,16},{1,9},{9,1},{17,25},{25,17},{2,10},{10... | collective-permute-start | bytes 2359304 | tf_op jit(solution)/shard_map/ppermute | solution.py:411
  116.4 36.6 %collective-permute-start.7 = (bf16[512,768]{1,0:T(8,128)(2,1)}, bf16[512,768]{1,0:T(8,128)(2,1)}, u32[]{:S(2)}, u32[]{:S(2)}) collective-permute-start(bf16[512,768]{1,0:T(8,128)(2,1)} %get-tuple-element.105), channel_id=1, source_target_pairs={{0,16},{8,24},{16,0},{24,8},{1,17},{9,25},{17,1},{25,9},{2,18},{10... | collective-permute-start | bytes 2359304 | tf_op jit(solution)/shard_map/ppermute | solution.py:411
  117.9 35.1 %collective-permute-start.8 = (bf16[512,768]{1,0:T(8,128)(2,1)}, bf16[512,768]{1,0:T(8,128)(2,1)}, u32[]{:S(2)}, u32[]{:S(2)}) collective-permute-start(bf16[512,768]{1,0:T(8,128)(2,1)} %get-tuple-element.104), channel_id=1, source_target_pairs={{0,24},{8,16},{16,8},{24,0},{1,25},{9,17},{17,9},{25,1},{2,26},{10... | collective-permute-start | bytes 2359304 | tf_op jit(solution)/shard_map/ppermute | solution.py:411
  167.3 16.0 %collective-permute-start.11 = (bf16[128,2048]{1,0:T(8,128)(2,1)}, bf16[128,2048]{1,0:T(8,128)(2,1)S(1)}, u32[]{:S(2)}, u32[]{:S(2)}) collective-permute-start(bf16[128,2048]{1,0:T(8,128)(2,1)} %get-tuple-element.56), channel_id=1, source_target_pairs={{0,24},{8,16},{16,8},{24,0},{1,25},{9,17},{17,9},{25,1},{2,26},{10... | collective-permute-start | bytes 1572872 | tf_op jit(solution)/shard_map/ppermute | solution.py:411
  169.0 25.5 %collective-permute-start.10 = (bf16[128,2048]{1,0:T(8,128)(2,1)}, bf16[128,2048]{1,0:T(8,128)(2,1)S(1)}, u32[]{:S(2)}, u32[]{:S(2)}) collective-permute-start(bf16[128,2048]{1,0:T(8,128)(2,1)} %get-tuple-element.55), channel_id=1, source_target_pairs={{0,16},{8,24},{16,0},{24,8},{1,17},{9,25},{17,1},{25,9},{2,18},{10... | collective-permute-start | bytes 1572872 | tf_op jit(solution)/shard_map/ppermute | solution.py:411
  170.1 24.6 %collective-permute-start.9 = (bf16[128,2048]{1,0:T(8,128)(2,1)}, bf16[128,2048]{1,0:T(8,128)(2,1)}, u32[]{:S(2)}, u32[]{:S(2)}) collective-permute-start(bf16[128,2048]{1,0:T(8,128)(2,1)} %get-tuple-element.54), channel_id=1, source_target_pairs={{0,8},{8,0},{16,24},{24,16},{1,9},{9,1},{17,25},{25,17},{2,10},{10... | collective-permute-start | bytes 1572872 | tf_op jit(solution)/shard_map/ppermute | solution.py:411
  183.3 22.6 %collective-permute-start.17 = (bf16[128,2048]{1,0:T(8,128)(2,1)}, bf16[128,2048]{1,0:T(8,128)(2,1)S(1)}, u32[]{:S(2)}, u32[]{:S(2)}) collective-permute-start(bf16[128,2048]{1,0:T(8,128)(2,1)} %param.35), channel_id=1, source_target_pairs={{0,24},{8,16},{16,8},{24,0},{1,25},{9,17},{17,9},{25,1},{2,26},{10... | collective-permute-start | bytes 1572872 | tf_op jit(solution)/shard_map/ppermute | solution.py:411
  198.3 18.8 %collective-permute-start.14 = (bf16[128,2048]{1,0:T(8,128)(2,1)S(1)}, bf16[128,2048]{1,0:T(8,128)(2,1)S(1)}, u32[]{:S(2)}, u32[]{:S(2)}) collective-permute-start(bf16[128,2048]{1,0:T(8,128)(2,1)S(1)} %multiply_convert_fusion.1), channel_id=1, source_target_pairs={{0,24},{8,16},{16,8},{24,0},{1,25},{9,17},{17,9},{25,1},{2,26},{10... | collective-permute-start | bytes 1572872 | tf_op jit(solution)/shard_map/ppermute | solution.py:411
  199.9 26.6 %collective-permute-start.13 = (bf16[128,2048]{1,0:T(8,128)(2,1)S(1)}, bf16[128,2048]{1,0:T(8,128)(2,1)S(1)}, u32[]{:S(2)}, u32[]{:S(2)}) collective-permute-start(bf16[128,2048]{1,0:T(8,128)(2,1)S(1)} %multiply_convert_fusion.1), channel_id=1, source_target_pairs={{0,16},{8,24},{16,0},{24,8},{1,17},{9,25},{17,1},{25,9},{2,18},{10... | collective-permute-start | bytes 1572872 | tf_op jit(solution)/shard_map/ppermute | solution.py:411
  201.0 25.5 %collective-permute-start.12 = (bf16[128,2048]{1,0:T(8,128)(2,1)S(1)}, bf16[128,2048]{1,0:T(8,128)(2,1)S(1)}, u32[]{:S(2)}, u32[]{:S(2)}) collective-permute-start(bf16[128,2048]{1,0:T(8,128)(2,1)S(1)} %multiply_convert_fusion.1), channel_id=1, source_target_pairs={{0,8},{8,0},{16,24},{24,16},{1,9},{9,1},{17,25},{25,17},{2,10},{10... | collective-permute-start | bytes 1572872 | tf_op jit(solution)/shard_map/ppermute | solution.py:411
  279.4 244.2 %reduce-scatter.5.cloned.1.call-start = ((), (), s32[]{:S(2)}) async-start(), calls=%async_computation.7 | async-start | bytes 2359296 | tf_op jit(solution)/shard_map/reduce_scatter | solution.py:469
  283.8 32.8 %collective-permute-start.36 = (f32[4,128]{1,0:T(4,128)S(1)}, f32[4,128]{1,0:T(4,128)S(1)}, u32[]{:S(2)}, u32[]{:S(2)}) collective-permute-start(f32[4,128]{1,0:T(4,128)S(1)} %bitcast.128), channel_id=1, source_target_pairs={{0,8},{8,0},{16,24},{24,16},{1,9},{9,1},{17,25},{25,17},{2,10},{10... | collective-permute-start | bytes 6152 | tf_op jit(solution)/shard_map/ppermute | solution.py:411
  284.4 15.7 %collective-permute-start.23 = (bf16[128,2048]{1,0:T(8,128)(2,1)S(1)}, bf16[128,2048]{1,0:T(8,128)(2,1)S(1)}, u32[]{:S(2)}, u32[]{:S(2)}) collective-permute-start(bf16[128,2048]{1,0:T(8,128)(2,1)S(1)} %copy-done.75), channel_id=1, source_target_pairs={{0,24},{8,16},{16,8},{24,0},{1,25},{9,17},{17,9},{25,1},{2,26},{10... | collective-permute-start | bytes 1572872 | tf_op jit(solution)/shard_map/ppermute | solution.py:411
  285.8 23.7 %collective-permute-start.22 = (bf16[128,2048]{1,0:T(8,128)(2,1)S(1)}, bf16[128,2048]{1,0:T(8,128)(2,1)S(1)}, u32[]{:S(2)}, u32[]{:S(2)}) collective-permute-start(bf16[128,2048]{1,0:T(8,128)(2,1)S(1)} %copy-done.74), channel_id=1, source_target_pairs={{0,16},{8,24},{16,0},{24,8},{1,17},{9,25},{17,1},{25,9},{2,18},{10... | collective-permute-start | bytes 1572872 | tf_op jit(solution)/shard_map/ppermute | solution.py:411
  287.3 22.3 %collective-permute-start.21 = (bf16[128,2048]{1,0:T(8,128)(2,1)S(1)}, bf16[128,2048]{1,0:T(8,128)(2,1)S(1)}, u32[]{:S(2)}, u32[]{:S(2)}) collective-permute-start(bf16[128,2048]{1,0:T(8,128)(2,1)S(1)} %copy-done.73), channel_id=1, source_target_pairs={{0,8},{8,0},{16,24},{24,16},{1,9},{9,1},{17,25},{25,17},{2,10},{10... | collective-permute-start | bytes 1572872 | tf_op jit(solution)/shard_map/ppermute | solution.py:411
  312.8 14.8 %collective-permute-start.24 = (bf16[128,2048]{1,0:T(8,128)(2,1)S(1)}, bf16[128,2048]{1,0:T(8,128)(2,1)S(1)}, u32[]{:S(2)}, u32[]{:S(2)}) collective-permute-start(bf16[128,2048]{1,0:T(8,128)(2,1)S(1)} %get-tuple-element.96.refs_1_.refs_3_), channel_id=1, source_target_pairs={{0,8},{8,0},{16,24},{24,16},{1,9},{9,1},{17,25},{25,17},{2,10},{10... | collective-permute-start | bytes 1572872 | tf_op jit(solution)/shard_map/ppermute | solution.py:411
  314.3 24.9 %collective-permute-start.25 = (bf16[128,2048]{1,0:T(8,128)(2,1)S(1)}, bf16[128,2048]{1,0:T(8,128)(2,1)S(1)}, u32[]{:S(2)}, u32[]{:S(2)}) collective-permute-start(bf16[128,2048]{1,0:T(8,128)(2,1)S(1)} %get-tuple-element.96.refs_1_.refs_3_), channel_id=1, source_target_pairs={{0,16},{8,24},{16,0},{24,8},{1,17},{9,25},{17,1},{25,9},{2,18},{10... | collective-permute-start | bytes 1572872 | tf_op jit(solution)/shard_map/ppermute | solution.py:411
  314.9 24.2 %collective-permute-start.26 = (bf16[128,2048]{1,0:T(8,128)(2,1)S(1)}, bf16[128,2048]{1,0:T(8,128)(2,1)S(1)}, u32[]{:S(2)}, u32[]{:S(2)}) collective-permute-start(bf16[128,2048]{1,0:T(8,128)(2,1)S(1)} %get-tuple-element.96.refs_1_.refs_3_), channel_id=1, source_target_pairs={{0,24},{8,16},{16,8},{24,0},{1,25},{9,17},{17,9},{25,1},{2,26},{10... | collective-permute-start | bytes 1572872 | tf_op jit(solution)/shard_map/ppermute | solution.py:411
  353.6 7.9 %collective-permute-start.29 = (bf16[128,640]{1,0:T(8,128)(2,1)}, bf16[128,640]{1,0:T(8,128)(2,1)S(1)}, u32[]{:S(2)}, u32[]{:S(2)}) collective-permute-start(bf16[128,640]{1,0:T(8,128)(2,1)} %get-tuple-element.75), channel_id=1, source_target_pairs={{0,24},{8,16},{16,8},{24,0},{1,25},{9,17},{17,9},{25,1},{2,26},{10... | collective-permute-start | bytes 491528 | tf_op jit(solution)/shard_map/ppermute | solution.py:411
  355.1 8.1 %collective-permute-start.28 = (bf16[128,640]{1,0:T(8,128)(2,1)}, bf16[128,640]{1,0:T(8,128)(2,1)S(1)}, u32[]{:S(2)}, u32[]{:S(2)}) collective-permute-start(bf16[128,640]{1,0:T(8,128)(2,1)} %get-tuple-element.74), channel_id=1, source_target_pairs={{0,16},{8,24},{16,0},{24,8},{1,17},{9,25},{17,1},{25,9},{2,18},{10... | collective-permute-start | bytes 491528 | tf_op jit(solution)/shard_map/ppermute | solution.py:411
  355.7 7.5 %collective-permute-start.27 = (bf16[128,640]{1,0:T(8,128)(2,1)}, bf16[128,640]{1,0:T(8,128)(2,1)S(1)}, u32[]{:S(2)}, u32[]{:S(2)}) collective-permute-start(bf16[128,640]{1,0:T(8,128)(2,1)} %get-tuple-element.73), channel_id=1, source_target_pairs={{0,8},{8,0},{16,24},{24,16},{1,9},{9,1},{17,25},{25,17},{2,10},{10... | collective-permute-start | bytes 491528 | tf_op jit(solution)/shard_map/ppermute | solution.py:411
  367.3 9.0 %collective-permute-start.31 = (bf16[128,576]{1,0:T(8,128)(2,1)S(1)}, bf16[128,576]{1,0:T(8,128)(2,1)S(1)}, u32[]{:S(2)}, u32[]{:S(2)}) collective-permute-start(bf16[128,576]{1,0:T(8,128)(2,1)S(1)} %pad_maximum_fusion.3), channel_id=1, source_target_pairs={{0,16},{8,24},{16,0},{24,8},{1,17},{9,25},{17,1},{25,9},{2,18},{10... | collective-permute-start | bytes 442376 | tf_op jit(solution)/shard_map/ppermute | solution.py:411
  368.6 8.3 %collective-permute-start.32 = (bf16[128,576]{1,0:T(8,128)(2,1)S(1)}, bf16[128,576]{1,0:T(8,128)(2,1)}, u32[]{:S(2)}, u32[]{:S(2)}) collective-permute-start(bf16[128,576]{1,0:T(8,128)(2,1)S(1)} %pad_maximum_fusion.3), channel_id=1, source_target_pairs={{0,24},{8,16},{16,8},{24,0},{1,25},{9,17},{17,9},{25,1},{2,26},{10... | collective-permute-start | bytes 442376 | tf_op jit(solution)/shard_map/ppermute | solution.py:411
  387.7 8.1 %collective-permute-start.40 = (f32[4608]{0:T(1024)S(1)}, f32[4608]{0:T(1024)S(1)}, u32[]{:S(2)}, u32[]{:S(2)}) collective-permute-start(f32[4608]{0:T(1024)S(1)} %pad_maximum_fusion.4), channel_id=1, source_target_pairs={{0,16},{8,24},{16,0},{24,8},{1,17},{9,25},{17,1},{25,9},{2,18},{10... | collective-permute-start | bytes 55304 | tf_op jit(solution)/shard_map/ppermute | solution.py:411
  391.8 8.6 %collective-permute-start.42 = (bf16[4,128,256]{2,1,0:T(8,128)(2,1)S(1)}, bf16[4,128,256]{2,1,0:T(8,128)(2,1)S(1)}, u32[]{:S(2)}, u32[]{:S(2)}) collective-permute-start(bf16[4,128,256]{2,1,0:T(8,128)(2,1)S(1)} %bitcast.101), channel_id=1, source_target_pairs={{0,8},{8,0},{16,24},{24,16},{1,9},{9,1},{17,25},{25,17},{2,10},{10... | collective-permute-start | bytes 786440 | tf_op jit(solution)/shard_map/ppermute | solution.py:411
  393.3 10.8 %collective-permute-start.43 = (bf16[4,128,256]{2,1,0:T(8,128)(2,1)S(1)}, bf16[4,128,256]{2,1,0:T(8,128)(2,1)S(1)}, u32[]{:S(2)}, u32[]{:S(2)}) collective-permute-start(bf16[4,128,256]{2,1,0:T(8,128)(2,1)S(1)} %bitcast.102), channel_id=1, source_target_pairs={{0,16},{8,24},{16,0},{24,8},{1,17},{9,25},{17,1},{25,9},{2,18},{10... | collective-permute-start | bytes 786440 | tf_op jit(solution)/shard_map/ppermute | solution.py:411
  393.7 10.5 %collective-permute-start.44 = (bf16[4,128,256]{2,1,0:T(8,128)(2,1)S(1)}, bf16[4,128,256]{2,1,0:T(8,128)(2,1)S(1)}, u32[]{:S(2)}, u32[]{:S(2)}) collective-permute-start(bf16[4,128,256]{2,1,0:T(8,128)(2,1)S(1)} %bitcast.103), channel_id=1, source_target_pairs={{0,24},{8,16},{16,8},{24,0},{1,25},{9,17},{17,9},{25,1},{2,26},{10... | collective-permute-start | bytes 786440 | tf_op jit(solution)/shard_map/ppermute | solution.py:411
  413.2 117.7 %reduce-scatter.11.cloned.1.call-start = ((), (), s32[]{:S(2)}) async-start(), calls=%async_computation.10 | async-start | bytes 3538944 | tf_op jit(solution)/shard_map/reduce_scatter | solution.py:469
  418.8 131.4 %reduce-scatter.7.cloned.1.call-start = ((), (), s32[]{:S(2)}) async-start(), calls=%async_computation.8 | async-start | bytes 5898240 | tf_op jit(solution)/shard_map/reduce_scatter | solution.py:469
  419.8 14.8 %collective-permute-start.45 = (bf16[512,512]{1,0:T(8,128)(2,1)S(1)}, bf16[512,512]{1,0:T(8,128)(2,1)S(1)}, u32[]{:S(2)}, u32[]{:S(2)}) collective-permute-start(bf16[512,512]{1,0:T(8,128)(2,1)S(1)} %copy-done.20), channel_id=1, source_target_pairs={{0,8},{8,0},{16,24},{24,16},{1,9},{9,1},{17,25},{25,17},{2,10},{10... | collective-permute-start | bytes 1572872 | tf_op jit(solution)/shard_map/ppermute | solution.py:411
  420.8 20.8 %collective-permute-start.46 = (bf16[512,512]{1,0:T(8,128)(2,1)S(1)}, bf16[512,512]{1,0:T(8,128)(2,1)S(1)}, u32[]{:S(2)}, u32[]{:S(2)}) collective-permute-start(bf16[512,512]{1,0:T(8,128)(2,1)S(1)} %copy-done.20), channel_id=1, source_target_pairs={{0,16},{8,24},{16,0},{24,8},{1,17},{9,25},{17,1},{25,9},{2,18},{10... | collective-permute-start | bytes 1572872 | tf_op jit(solution)/shard_map/ppermute | solution.py:411
  421.9 19.7 %collective-permute-start.47 = (bf16[512,512]{1,0:T(8,128)(2,1)S(1)}, bf16[512,512]{1,0:T(8,128)(2,1)S(1)}, u32[]{:S(2)}, u32[]{:S(2)}) collective-permute-start(bf16[512,512]{1,0:T(8,128)(2,1)S(1)} %copy-done.20), channel_id=1, source_target_pairs={{0,24},{8,16},{16,8},{24,0},{1,25},{9,17},{17,9},{25,1},{2,26},{10... | collective-permute-start | bytes 1572872 | tf_op jit(solution)/shard_map/ppermute | solution.py:411
  457.7 15.0 %collective-permute-start.18 = (bf16[128,2048]{1,0:T(8,128)(2,1)}, bf16[128,2048]{1,0:T(8,128)(2,1)S(1)}, u32[]{:S(2)}, u32[]{:S(2)}) collective-permute-start(bf16[128,2048]{1,0:T(8,128)(2,1)} %get-tuple-element.59), channel_id=1, source_target_pairs={{0,8},{8,0},{16,24},{24,16},{1,9},{9,1},{17,25},{25,17},{2,10},{10... | collective-permute-start | bytes 1572872 | tf_op jit(solution)/shard_map/ppermute | solution.py:411
  457.7 23.0 %collective-permute-start.19 = (bf16[128,2048]{1,0:T(8,128)(2,1)}, bf16[128,2048]{1,0:T(8,128)(2,1)S(1)}, u32[]{:S(2)}, u32[]{:S(2)}) collective-permute-start(bf16[128,2048]{1,0:T(8,128)(2,1)} %get-tuple-element.60), channel_id=1, source_target_pairs={{0,16},{8,24},{16,0},{24,8},{1,17},{9,25},{17,1},{25,9},{2,18},{10... | collective-permute-start | bytes 1572872 | tf_op jit(solution)/shard_map/ppermute | solution.py:411
  458.7 25.7 %collective-permute-start.20 = (bf16[128,2048]{1,0:T(8,128)(2,1)}, bf16[128,2048]{1,0:T(8,128)(2,1)}, u32[]{:S(2)}, u32[]{:S(2)}) collective-permute-start(bf16[128,2048]{1,0:T(8,128)(2,1)} %get-tuple-element.61), channel_id=1, source_target_pairs={{0,24},{8,16},{16,8},{24,0},{1,25},{9,17},{17,9},{25,1},{2,26},{10... | collective-permute-start | bytes 1572872 | tf_op jit(solution)/shard_map/ppermute | solution.py:411
  461.2 92.5 %collective-permute-start.55 = (bf16[256,2560]{1,0:T(8,128)(2,1)}, bf16[256,2560]{1,0:T(8,128)(2,1)S(1)}, u32[]{:S(2)}, u32[]{:S(2)}) collective-permute-start(bf16[256,2560]{1,0:T(8,128)(2,1)} %reduce-scatter.9.cloned.1.call-done.refs_0_), channel_id=1, source_target_pairs={{0,8},{8,0},{16,24},{24,16},{1,9},{9,1},{17,25},{25,17},{2,10},{10... | collective-permute-start | bytes 3932168 | tf_op jit(solution)/shard_map/ppermute | solution.py:411
  461.2 93.9 %collective-permute-start.56 = (bf16[256,2560]{1,0:T(8,128)(2,1)}, bf16[256,2560]{1,0:T(8,128)(2,1)}, u32[]{:S(2)}, u32[]{:S(2)}) collective-permute-start(bf16[256,2560]{1,0:T(8,128)(2,1)} %reduce-scatter.9.cloned.1.call-done.refs_0_), channel_id=1, source_target_pairs={{0,16},{8,24},{16,0},{24,8},{1,17},{9,25},{17,1},{25,9},{2,18},{10... | collective-permute-start | bytes 3932168 | tf_op jit(solution)/shard_map/ppermute | solution.py:411
  472.7 50.9 %collective-permute-start.35 = (bf16[128,2048]{1,0:T(8,128)(2,1)S(1)}, bf16[128,2048]{1,0:T(8,128)(2,1)S(1)}, u32[]{:S(2)}, u32[]{:S(2)}) collective-permute-start(bf16[128,2048]{1,0:T(8,128)(2,1)S(1)} %get-tuple-element.114), channel_id=1, source_target_pairs={{0,24},{8,16},{16,8},{24,0},{1,25},{9,17},{17,9},{25,1},{2,26},{10... | collective-permute-start | bytes 1572872 | tf_op jit(solution)/shard_map/ppermute | solution.py:411
  480.7 50.2 %collective-permute-start.34 = (bf16[128,2048]{1,0:T(8,128)(2,1)}, bf16[128,2048]{1,0:T(8,128)(2,1)}, u32[]{:S(2)}, u32[]{:S(2)}) collective-permute-start(bf16[128,2048]{1,0:T(8,128)(2,1)} %get-tuple-element.115), channel_id=1, source_target_pairs={{0,16},{8,24},{16,0},{24,8},{1,17},{9,25},{17,1},{25,9},{2,18},{10... | collective-permute-start | bytes 1572872 | tf_op jit(solution)/shard_map/ppermute | solution.py:411
  484.4 47.7 %collective-permute-start.33 = (bf16[128,2048]{1,0:T(8,128)(2,1)}, bf16[128,2048]{1,0:T(8,128)(2,1)}, u32[]{:S(2)}, u32[]{:S(2)}) collective-permute-start(bf16[128,2048]{1,0:T(8,128)(2,1)} %get-tuple-element.113), channel_id=1, source_target_pairs={{0,8},{8,0},{16,24},{24,16},{1,9},{9,1},{17,25},{25,17},{2,10},{10... | collective-permute-start | bytes 1572872 | tf_op jit(solution)/shard_map/ppermute | solution.py:411
  523.6 28.1 %collective-permute-start.52 = (bf16[256,512]{1,0:T(8,128)(2,1)}, bf16[256,512]{1,0:T(8,128)(2,1)}, u32[]{:S(2)}, u32[]{:S(2)}) collective-permute-start(bf16[256,512]{1,0:T(8,128)(2,1)} %reduce-scatter.5.cloned.1.call-done.refs_0_), channel_id=1, source_target_pairs={{0,8},{8,0},{16,24},{24,16},{1,9},{9,1},{17,25},{25,17},{2,10},{10... | collective-permute-start | bytes 786440 | tf_op jit(solution)/shard_map/ppermute | solution.py:411
  530.9 22.2 %collective-permute-start.60 = (bf16[256,704]{1,0:T(8,128)(2,1)}, bf16[256,704]{1,0:T(8,128)(2,1)}, u32[]{:S(2)}, u32[]{:S(2)}) collective-permute-start(bf16[256,704]{1,0:T(8,128)(2,1)} %reduce-scatter.11.cloned.1.call-done.refs_0_), channel_id=1, source_target_pairs={{0,16},{8,24},{16,0},{24,8},{1,17},{9,25},{17,1},{25,9},{2,18},{10... | collective-permute-start | bytes 1081352 | tf_op jit(solution)/shard_map/ppermute | solution.py:411
  550.2 17.8 %collective-permute-start.48 = (bf16[256,1280]{1,0:T(8,128)(2,1)}, bf16[256,1280]{1,0:T(8,128)(2,1)S(1)}, u32[]{:S(2)}, u32[]{:S(2)}) collective-permute-start(bf16[256,1280]{1,0:T(8,128)(2,1)} %reduce-scatter.7.cloned.1.call-done.refs_0_), channel_id=1, source_target_pairs={{0,8},{8,0},{16,24},{24,16},{1,9},{9,1},{17,25},{25,17},{2,10},{10... | collective-permute-start | bytes 1966088 | tf_op jit(solution)/shard_map/ppermute | solution.py:411
  551.7 23.4 %collective-permute-start.49 = (bf16[256,1280]{1,0:T(8,128)(2,1)}, bf16[256,1280]{1,0:T(8,128)(2,1)S(1)}, u32[]{:S(2)}, u32[]{:S(2)}) collective-permute-start(bf16[256,1280]{1,0:T(8,128)(2,1)} %reduce-scatter.7.cloned.1.call-done.refs_0_), channel_id=1, source_target_pairs={{0,16},{8,24},{16,0},{24,8},{1,17},{9,25},{17,1},{25,9},{2,18},{10... | collective-permute-start | bytes 1966088 | tf_op jit(solution)/shard_map/ppermute | solution.py:411
  553.1 27.6 %collective-permute-start.53 = (bf16[256,512]{1,0:T(8,128)(2,1)}, bf16[256,512]{1,0:T(8,128)(2,1)S(1)}, u32[]{:S(2)}, u32[]{:S(2)}) collective-permute-start(bf16[256,512]{1,0:T(8,128)(2,1)} %reduce-scatter.5.cloned.1.call-done.refs_0_), channel_id=1, source_target_pairs={{0,16},{8,24},{16,0},{24,8},{1,17},{9,25},{17,1},{25,9},{2,18},{10... | collective-permute-start | bytes 786440 | tf_op jit(solution)/shard_map/ppermute | solution.py:411
  553.7 27.6 %collective-permute-start.54 = (bf16[256,512]{1,0:T(8,128)(2,1)}, bf16[256,512]{1,0:T(8,128)(2,1)S(1)}, u32[]{:S(2)}, u32[]{:S(2)}) collective-permute-start(bf16[256,512]{1,0:T(8,128)(2,1)} %reduce-scatter.5.cloned.1.call-done.refs_0_), channel_id=1, source_target_pairs={{0,24},{8,16},{16,8},{24,0},{1,25},{9,17},{17,9},{25,1},{2,26},{10... | collective-permute-start | bytes 786440 | tf_op jit(solution)/shard_map/ppermute | solution.py:411
  555.2 27.6 %collective-permute-start.59 = (bf16[256,704]{1,0:T(8,128)(2,1)}, bf16[256,704]{1,0:T(8,128)(2,1)}, u32[]{:S(2)}, u32[]{:S(2)}) collective-permute-start(bf16[256,704]{1,0:T(8,128)(2,1)} %reduce-scatter.11.cloned.1.call-done.refs_0_), channel_id=1, source_target_pairs={{0,8},{8,0},{16,24},{24,16},{1,9},{9,1},{17,25},{25,17},{2,10},{10... | collective-permute-start | bytes 1081352 | tf_op jit(solution)/shard_map/ppermute | solution.py:411
  568.0 48.1 %collective-permute-start.57 = (bf16[128,2560]{1,0:T(8,128)(2,1)}, bf16[128,2560]{1,0:T(8,128)(2,1)S(1)}, u32[]{:S(2)}, u32[]{:S(2)}) collective-permute-start(bf16[128,2560]{1,0:T(8,128)(2,1)} %slice.322), channel_id=1, source_target_pairs={{0,8},{8,0},{16,24},{24,16},{1,9},{9,1},{17,25},{25,17},{2,10},{10... | collective-permute-start | bytes 1966088 | tf_op jit(solution)/shard_map/ppermute | solution.py:411
  575.1 41.0 %collective-permute-start.58 = (bf16[128,2560]{1,0:T(8,128)(2,1)S(1)}, bf16[128,2560]{1,0:T(8,128)(2,1)S(1)}, u32[]{:S(2)}, u32[]{:S(2)}) collective-permute-start(bf16[128,2560]{1,0:T(8,128)(2,1)S(1)} %slice.323), channel_id=1, source_target_pairs={{0,16},{8,24},{16,0},{24,8},{1,17},{9,25},{17,1},{25,9},{2,18},{10... | collective-permute-start | bytes 1966088 | tf_op jit(solution)/shard_map/ppermute | solution.py:411
  580.7 19.6 %collective-permute-start.61 = (bf16[128,704]{1,0:T(8,128)(2,1)S(1)}, bf16[128,704]{1,0:T(8,128)(2,1)S(1)}, u32[]{:S(2)}, u32[]{:S(2)}) collective-permute-start(bf16[128,704]{1,0:T(8,128)(2,1)S(1)} %slice.324), channel_id=1, source_target_pairs={{0,8},{8,0},{16,24},{24,16},{1,9},{9,1},{17,25},{25,17},{2,10},{10... | collective-permute-start | bytes 540680 | tf_op jit(solution)/shard_map/ppermute | solution.py:411
  581.3 28.9 %collective-permute-start.50 = (bf16[128,1280]{1,0:T(8,128)(2,1)S(1)}, bf16[128,1280]{1,0:T(8,128)(2,1)S(1)}, u32[]{:S(2)}, u32[]{:S(2)}) collective-permute-start(bf16[128,1280]{1,0:T(8,128)(2,1)S(1)} %slice.318), channel_id=1, source_target_pairs={{0,8},{8,0},{16,24},{24,16},{1,9},{9,1},{17,25},{25,17},{2,10},{10... | collective-permute-start | bytes 983048 | tf_op jit(solution)/shard_map/ppermute | solution.py:411
  582.7 28.2 %collective-permute-start.51 = (bf16[128,1280]{1,0:T(8,128)(2,1)S(1)}, bf16[128,1280]{1,0:T(8,128)(2,1)}, u32[]{:S(2)}, u32[]{:S(2)}) collective-permute-start(bf16[128,1280]{1,0:T(8,128)(2,1)S(1)} %slice.319), channel_id=1, source_target_pairs={{0,16},{8,24},{16,0},{24,8},{1,17},{9,25},{17,1},{25,9},{2,18},{10... | collective-permute-start | bytes 983048 | tf_op jit(solution)/shard_map/ppermute | solution.py:411
  (87 other events, 1176.0 us)
Sparse Core Ops, SparseCore 0:
  14.4 93.4 all-gather.3
  110.0 84.7 all-gather.5
  197.1 49.6 all-gather.7
  279.5 106.8 reduce-scatter.8
  413.3 33.8 reduce-scatter.4
  449.9 38.8 reduce-scatter.10
  491.0 59.1 reduce-scatter.6

commit v3 on v2

--- a/solution.py
+++ b/solution.py
@@ -34,10 +34,6 @@
 
 def t_dot(left, right):
     return lax.dot_general(left, right, (((0,), (0,)), ((), ())), preferred_element_type=F32)
-
-
-def ein(form, left, right):
-    return jnp.einsum(form, left, right, preferred_element_type=F32)
 
 
 def inv_rms(values):
@@ -204,34 +200,69 @@
 CHUNK = D // STEPS
 
 
-def ffn_grad_kernel(R, SR, FR, cot_ref, rest_ref, in_ref, act_ref, slope_ref, e_hid_ref, e_act_ref,
+def add_step(step, ref, value):
+    @pl.when(step == 0)
+    def _():
+        ref[...] = value
+
+    @pl.when(step > 0)
+    def _():
+        ref[...] += value
+
+
+def ffn_in_kernel(R, SR, FR, *refs):
+    (in_ref, router_ref, pick_ref, chosen_ref, rows_g_ref, n2_ref, rows_in_ref, act_ref, slope_ref,
+     s_hid_ref, e_act_ref, e_slope_ref, e_hid_ref, probs_ref, rows_w_ref, rows_geo_ref, acc_ref,
+     e_acc_ref, logits_ref) = refs[R:]
+    step = pl.program_id(0)
+    for k in range(R):
+        n2_ref[k * TOK : (k + 1) * TOK, :] = refs[k][...]
+    n2 = n2_ref[...]
+    rows_in = dot(pick_ref[...], n2).astype(BF)
+    rows_in_ref[...] = rows_in
+    add_step(step, acc_ref, dot(n2, in_ref[:, : 2 * SR]))
+    add_step(step, e_acc_ref, dot(rows_in, in_ref[:, 2 * SR : 2 * SR + 2 * FR]))
+    add_step(step, logits_ref, dot(n2, router_ref[:, 128 - NE :]))
+
+    @pl.when(step == STEPS - 1)
+    def _():
+        up = acc_ref[:, SR:]
+        act, slope = silu_parts(acc_ref[:, :SR])
+        act_ref[...] = act
+        slope_ref[...] = slope * up
+        s_hid_ref[...] = (act * up).astype(BF)
+        e_up = e_acc_ref[:, FR:]
+        e_act, e_slope = silu_parts(e_acc_ref[:, :FR])
+        e_act_ref[...] = e_act
+        e_slope_ref[...] = e_slope * e_up
+        e_hid_ref[...] = (e_act * e_up).astype(BF)
+        logits = logits_ref[...]
+        expd = jnp.exp(logits - jnp.max(logits, axis=-1, keepdims=True))
+        probs = expd / jnp.sum(expd, axis=-1, keepdims=True)
+        probs_ref[...] = probs
+        combine = probs[:, :1] * chosen_ref[...]
+        high = combine.astype(BF)
+        low = (combine - high.astype(F32)).astype(BF)
+        rows_w = dot(pick_ref[...], high) + dot(pick_ref[...], low)
+        rows_w_ref[...] = rows_w
+        rows_geo_ref[...] = (rows_w[:, :1] * rows_g_ref[...]).astype(BF)
+
+
+def ffn_grad_kernel(SR, FR, EX, cot_ref, rest_ref, more_ref, act_ref, slope_ref, e_hid_ref, e_act_ref,
                     e_slope_ref, rows_geo_ref, rows_g_ref, spread_ref, probs_ref, chosen_ref,
-                    router_ref, geg_ref, e_geg_ref, rows_out_ref, gc_ref, *refs):
-    part_refs = refs[:R]
-    acc_ref, e_acc_ref, gc_acc_ref, lg_ref = refs[R:]
+                    geg_ref, e_geg_ref, rows_out_ref, gc_ref, lg_ref, acc_ref, e_acc_ref,
+                    gc_acc_ref):
     step = pl.program_id(0)
-
-    @pl.when(step < STEPS)
-    def _():
-        w_edt = rest_ref[:, SR:]
-        s_gh = dot(cot_ref[...], rest_ref[:, :SR])
-        e_gh = dot(rows_geo_ref[...], w_edt)
-        rows_out = dot_t(e_hid_ref[...], w_edt)
-        rows_out_ref[...] = rows_out
-        gc_rows = jnp.sum(rows_g_ref[...] * rows_out, axis=-1, keepdims=True)
-        gc_rows = jnp.broadcast_to(gc_rows, gc_acc_ref.shape)
-
-        @pl.when(step == 0)
-        def _():
-            acc_ref[...] = s_gh
-            e_acc_ref[...] = e_gh
-            gc_acc_ref[...] = gc_rows
-
-        @pl.when(step > 0)
-        def _():
-            acc_ref[...] += s_gh
-            e_acc_ref[...] += e_gh
-            gc_acc_ref[...] += gc_rows
+    FM, at = FR - EX, (2 * SR + 2 * FR) % 128
+    w_edt, w_more = rest_ref[:, SR:], more_ref[:, at : at + EX]
+    geo = rows_geo_ref[...]
+    add_step(step, acc_ref, dot(cot_ref[...], rest_ref[:, :SR]))
+    add_step(step, e_acc_ref.at[:, :FM], dot(geo, w_edt))
+    add_step(step, e_acc_ref.at[:, FM:], dot(geo, w_more))
+    rows_out = dot_t(e_hid_ref[:, :FM], w_edt) + dot_t(e_hid_ref[:, FM:], w_more)
+    rows_out_ref[...] = rows_out
+    gc_rows = jnp.sum(rows_g_ref[...] * rows_out, axis=-1, keepdims=True)
+    add_step(step, gc_acc_ref, jnp.broadcast_to(gc_rows, gc_acc_ref.shape))
 
     @pl.when(step == STEPS - 1)
     def _():
@@ -249,18 +280,18 @@
         lg = probs * (jnp.where(first, p, 0.0) - probs[:, :1] * p)
         lg_ref[...] = lg.astype(BF)
 
-    @pl.when(step >= STEPS)
-    def _():
-        g_n2 = dot_t(geg_ref[...], in_ref[:, : 2 * SR]) + dot_t(lg_ref[...], router_ref[...])
-        rows_back = dot_t(e_geg_ref[...], in_ref[:, 2 * SR :])
-        total = g_n2 + scatter_rows(spread_ref[...], rows_back)
-        for k in range(R):
-            part_refs[k][...] = total[k * TOK : (k + 1) * TOK].astype(BF)
+
+def ffn_n2_kernel(R, SR, geg_ref, e_geg_ref, lg_ref, spread_ref, in_ref, router_ref, *part_refs):
+    total = dot_t(geg_ref[...], in_ref[:, : 2 * SR]) + dot_t(lg_ref[...], router_ref[:, 128 - NE :])
+    rows_back = dot_t(e_geg_ref[...], in_ref[:, 2 * SR : 2 * SR + e_geg_ref.shape[1]])
+    total = total + scatter_rows(spread_ref[...], rows_back)
+    for k in range(R):
+        part_refs[k][...] = total[k * TOK : (k + 1) * TOK].astype(BF)
 
 
 def ffn_out_kernel(R, SR, s_hid_ref, rest_ref, spread_ref, rows_w_ref, rows_out_ref, *part_refs):
     total = dot_t(s_hid_ref[...], rest_ref[:, :SR]) + scatter_rows(
-        spread_ref[...], rows_w_ref[...] * rows_out_ref[...]
+        spread_ref[...], rows_w_ref[:, :1] * rows_out_ref[...]
     )
     for k in range(R):
         part_refs[k][...] = total[k * TOK : (k + 1) * TOK].astype(BF)
@@ -484,7 +515,7 @@
         cot_all = jnp.concatenate(gather(cotangent))
 
         CD, CR, CG = QW, QW + KVR + DR, QW + KVR + DR + NE
-        CH = -(-(CG + 64) // 128) * 128
+        CH = -(-CG // 128) * 128
         KW = HS * KR * (DN + DV) // DL
         kv_piece = (
             part(kv_up, KR, 0).reshape(KR, HS, DN + DV).transpose(1, 0, 2).reshape(HS * KR, DN + DV)
@@ -512,8 +543,7 @@
                 jnp.pad(q_own[..., DN + half :].reshape(DL, HL), rope_pad),
                 kv_down,
                 router_weight,
-                gain_rows(norm_gain, mixer_gain, kv_gain),
-                jnp.zeros((DL, CH - CG - 64), BF),
+                *([jnp.zeros((DL, CH - CG), BF)] if CH > CG else []),
                 part(out_weight, DC),
                 fold(kv_piece, DL),
             ],
@@ -535,13 +565,21 @@
         out_w_spec = pl.BlockSpec((HR * DV, DC), lambda i, r_ref: (0, 0))
         r_one = r.reshape(1)
         w_q = attn_all[:, :QW]
-        w_down = attn_all[:, CD:CR]
-        w_router = attn_all[:, CR:CG]
-        gain_all = attn_all[:, CG : CG + 64].reshape(S, DL, 64).astype(F32)
-        gain_one = gain_all[:, :GR].reshape(D)
-        gain_two = gain_all[:, GR : 2 * GR].reshape(D)
-        gain_kv = gain_all[:, 2 * GR, : KVR // S].reshape(KVR)
-
+        gain_own = jnp.concatenate([norm_gain, mixer_gain, kv_gain])
+        shard = lax.axis_index(SHD)
+        gain_got = [gain_own] + [
+            lax.ppermute(gain_own, SHD, [(i, i ^ j) for i in range(S)]) for j in range(1, S)
+        ]
+        gain_got = jnp.stack(gain_got).astype(F32)
+        gain_all = jnp.concatenate(
+            [lax.dynamic_index_in_dim(gain_got, shard ^ j, 0) for j in range(S)]
+        )
+        gain_one = gain_all[:, :DL].reshape(D)
+        gain_two = gain_all[:, DL : 2 * DL].reshape(D)
+        gain_kv = gain_all[:, 2 * DL :].reshape(KVR)
+
+        EX = (SR + FR) % 128
+        down_t = jnp.concatenate([part(shared_down, SR, 0).T, part(expert_down[0], FR, 0).T], axis=1)
         in_all = shard_gather(
             jnp.concatenate(
                 [
@@ -549,14 +587,12 @@
                     part(shared_up, SR),
                     part(expert_gate[0], FR),
                     part(expert_up[0], FR),
+                    down_t[:, SR + FR - EX :],
                 ],
                 axis=1,
             ),
         )
-        w_gu, w_egu = in_all[:, : 2 * SR], in_all[:, 2 * SR :]
-        rest_all = shard_gather(
-            jnp.concatenate([part(shared_down, SR, 0).T, part(expert_down[0], FR, 0).T], axis=1),
-        )
+        rest_all = shard_gather(down_t[:, : SR + FR - EX])
 
         xf = x_all.astype(F32)
         scale_one = inv_rms(xf)
@@ -615,101 +651,85 @@
 
         scale_two = inv_rms(hidden)
         n2_own = (hidden * scale_two * gain_two).astype(BF)
-        n2 = jnp.concatenate(gather(n2_own))
+        n2_blocks = gather(n2_own)
         att_all = gather(att)
-        probs_r = jax.nn.softmax(dot(n2, w_router), axis=-1)
+        RC = R * CAP
         chosen = meta[:, 1].astype(F32)
-        combine = probs_r[:, 0].reshape(R, TOK) * chosen
         place = jnp.cumsum(chosen.astype(jnp.int32), axis=1) - 1
-        slots = jnp.arange(CAP, dtype=jnp.int32)
-        dispatch = (
-            (place[:, None, :] == slots[None, :, None]) & (chosen[:, None, :] > 0.5)
-        ).astype(F32)
-        dispatch_b = dispatch.astype(BF)
-        n2_b = n2.reshape(R, TOK, D)
-        cot_b = cot_all.reshape(R, TOK, D)
-        rows_in = ein("bct,btd->bcd", dispatch_b, n2_b).astype(BF).reshape(R * CAP, D)
-        rows_g = ein("bct,btd->bcd", dispatch_b, cot_b).reshape(R * CAP, D)
-        rows_w = jnp.sum(dispatch * combine[:, None, :], axis=-1).reshape(R * CAP, 1)
-
-        pre = dot(n2, w_gu)
-        g_pre, u_pre = pre[:, :SR], pre[:, SR:]
-        act, slope = silu_parts(g_pre)
-        s_hid = (act * u_pre).astype(BF)
+        slot = place + CAP * jnp.arange(R)[:, None]
+        slot = jnp.where((chosen > 0.5) & (place < CAP), slot, -1).reshape(T)
+        pick = (jnp.arange(RC)[:, None] == slot[None]).astype(BF)
+        spread = (slot[:, None] == jnp.arange(2 * RC)[None] % RC).astype(BF)
+        chosen_wide = jnp.broadcast_to(chosen.reshape(T, 1), (T, 128))
+        rows_g = dot(pick, cot_all)
+
+        def call(kernel, operands, specs, outs, scratch=()):
+            return pl.pallas_call(
+                kernel,
+                grid=(STEPS,),
+                in_specs=[specs.get(n, whole_block(v.shape)) for n, v in enumerate(operands)],
+                out_specs=[
+                    pl.BlockSpec((h, CHUNK), lambda i: (0, i))
+                    if w == D
+                    else whole_block((h, abs(w)))
+                    for h, w, _ in outs
+                ],
+                out_shape=[jax.ShapeDtypeStruct((h, abs(w)), t) for h, w, t in outs],
+                scratch_shapes=[pltpu.VMEM(shape, F32) for shape in scratch],
+            )(*operands)
+
+        def columns(values):
+            return pl.BlockSpec((values.shape[0], CHUNK), lambda i: (0, i))
+
+        def chunk_rows(width, column=0):
+            return pl.BlockSpec((CHUNK, width), lambda i: (i, column))
+
+        w_in_spec, router_spec = chunk_rows(2 * SR + 2 * FR + EX), chunk_rows(128, CR // 128)
+        more_spec = chunk_rows(128, (2 * SR + 2 * FR) // 128)
+        (
+            n2, rows_in, act, slope_up, s_hid, e_act, e_slope_up, e_hid, probs_r, rows_w, rows_geo
+        ) = call(
+            lambda *refs: ffn_in_kernel(R, SR, FR, *refs),
+            (*n2_blocks, in_all, attn_all, pick, chosen_wide, rows_g),
+            {**{k: columns(n2_own) for k in range(R)}, R: w_in_spec, R + 1: router_spec},
+            [
+                (T, D, BF), (RC, D, BF), (T, SR, F32), (T, SR, F32), (T, SR, BF), (RC, FR, F32),
+                (RC, FR, F32), (RC, FR, BF), (T, NE, F32), (RC, 128, F32), (RC, -D, BF),
+            ],
+            [(T, 2 * SR), (RC, 2 * FR), (T, NE)],
+        )
+
         down_part = pl.pallas_call(
             product_kernel,
             grid=(STEPS,),
-            in_specs=[pl.BlockSpec((T, CHUNK), lambda i: (0, i)), whole_block((T, SR))],
+            in_specs=[columns(cot_all), whole_block((T, SR))],
             out_specs=pl.BlockSpec((CHUNK, SR), lambda i: (i, 0)),
             out_shape=jax.ShapeDtypeStruct((D, SR), BF),
         )(cot_all, s_hid)
         down_red = shard_reduce(down_part)
-        e_pre = dot(rows_in, w_egu)
-        e_g, e_u = e_pre[:, :FR], e_pre[:, FR:]
-        e_act, e_slope = silu_parts(e_g)
-        e_hid = (e_act * e_u).astype(BF)
-        rows_geo = (rows_w * rows_g).astype(BF)
-        slot = (place + CAP * jnp.arange(R)[:, None]).reshape(T, 1)
-        spread = (slot == jnp.arange(2 * R * CAP)[None] % (R * CAP)) & (chosen.reshape(T, 1) > 0.5)
-        spread = (spread & (place.reshape(T, 1) < CAP)).astype(BF)
-        chosen_wide = jnp.broadcast_to(chosen.reshape(T, 1), (T, 128))
-        operands = (
-            cot_all,
-            rest_all,
-            in_all,
-            act,
-            u_pre * slope,
-            e_hid,
-            e_act,
-            e_u * e_slope,
-            rows_geo,
-            rows_g,
-            spread,
-            probs_r,
-            chosen_wide,
-            w_router,
-        )
-        RC = R * CAP
-
-        def early(i):
-            return jnp.minimum(i, STEPS - 1)
-
-        def late(i):
-            return jnp.maximum(i - STEPS, 0)
-
-        specs = {
-            0: pl.BlockSpec((T, CHUNK), lambda i: (0, early(i))),
-            1: pl.BlockSpec((CHUNK, SR + FR), lambda i: (early(i), 0)),
-            2: pl.BlockSpec((CHUNK, 2 * SR + 2 * FR), lambda i: (late(i), 0)),
-            8: pl.BlockSpec((RC, CHUNK), lambda i: (0, early(i))),
-            9: pl.BlockSpec((RC, CHUNK), lambda i: (0, early(i))),
-            13: pl.BlockSpec((CHUNK, NE), lambda i: (late(i), 0)),
-        }
-        shapes = [
-            ((T, 2 * SR), BF),
-            ((RC, 2 * FR), BF),
-            ((RC, D), F32),
-            ((T, 128), F32),
-        ] + [((TOK, D), BF)] * R
-        s_geg, e_geg, rows_out, gc_wide, *gn2_parts = pl.pallas_call(
-            lambda *refs: ffn_grad_kernel(R, SR, FR, *refs),
-            grid=(2 * STEPS,),
-            in_specs=[specs.get(n, whole_block(v.shape)) for n, v in enumerate(operands)],
-            out_specs=[
-                whole_block(shapes[0][0]),
-                whole_block(shapes[1][0]),
-                pl.BlockSpec((RC, CHUNK), lambda i: (0, early(i))),
-                whole_block(shapes[3][0]),
-            ]
-            + [pl.BlockSpec((TOK, CHUNK), lambda i: (0, late(i)))] * R,
-            out_shape=[jax.ShapeDtypeStruct(s, t) for s, t in shapes],
-            scratch_shapes=[
-                pltpu.VMEM((T, SR), F32),
-                pltpu.VMEM((RC, FR), F32),
-                pltpu.VMEM((RC, 128), F32),
-                pltpu.VMEM((T, NE), BF),
-            ],
-        )(*operands)
+
+        s_geg, e_geg, rows_out, gc_wide, lg_part = call(
+            lambda *refs: ffn_grad_kernel(SR, FR, EX, *refs),
+            (
+                cot_all, rest_all, in_all, act, slope_up, e_hid, e_act, e_slope_up, rows_geo, rows_g,
+                spread, probs_r, chosen_wide,
+            ),
+            {
+                0: columns(cot_all),
+                1: chunk_rows(SR + FR - EX),
+                2: more_spec,
+                8: columns(rows_geo),
+                9: columns(rows_g),
+            },
+            [(T, 2 * SR, BF), (RC, 2 * FR, BF), (RC, D, F32), (T, 128, F32), (T, NE, BF)],
+            [(T, SR), (RC, FR), (RC, 128)],
+        )
+        gn2_parts = call(
+            lambda *refs: ffn_n2_kernel(R, SR, *refs),
+            (s_geg, e_geg, lg_part, spread, in_all, attn_all),
+            {4: w_in_spec, 5: router_spec},
+            [(TOK, D, BF)] * R,
+        )
         gc_part = gc_wide[:, 0].reshape(R, TOK)
 
         def logits_grad(gc):
@@ -718,9 +738,6 @@
             return (probs_r * (p * first - probs_r[:, :1] * p)).astype(BF)
 
         gn2 = reduce_parts(gn2_parts)
-
-        def columns(values):
-            return pl.BlockSpec((values.shape[0], CHUNK), lambda i: (0, i))
 
         GW = -(-(2 * SR + 3 * FR) // 128) * 128
         gu_part = pl.pallas_call(
@@ -740,7 +757,7 @@
         gu_red = shard_reduce(gu_part)
         operands = (s_hid, rest_all, spread, rows_w, rows_out)
         specs = {
-            1: pl.BlockSpec((CHUNK, SR + FR), lambda i: (i, 0)),
+            1: pl.BlockSpec((CHUNK, SR + FR - EX), lambda i: (i, 0)),
             4: pl.BlockSpec((RC, CHUNK), lambda i: (0, i)),
         }
         out_ffn = pl.pallas_call(
@@ -823,7 +840,7 @@
         )
         gd_own = jnp.concatenate([g_latent, glat[:, KVR : KVR + DR]], axis=1).astype(BF)
         gd = part(jnp.concatenate(gather(gd_own)), LR)
-        gn1_part = dot_t(gq, w_q) + dot_t(gd, part(w_down, LR))
+        gn1_part = dot_t(gq, w_q) + dot_t(gd, lax.dynamic_slice(attn_all, (0, CD + r * LR), (D, LR)))
         gn1 = reduce_blocks(gn1_part)
         scale_own = scale_one[:TOK]
         scaled_one = gn1 * gain_one
@@ -841,7 +858,8 @@
             kvu_blocks.append(send(b, k) if k else b)
         lg = part(logits_grad(gc_total), NR)
         vectors = jnp.concatenate([g_norm, g_mixer, g_kvgain])
-        summed = sum(gather(vectors))
+        gathered = gather(vectors)
+        summed = sum(gathered)
         g_gains = gain_rows(
             summed[:D].reshape(S, DL),
             summed[D : 2 * D].reshape(S, DL),

time: 643 us -> 628 us (0.977)
  Pallas kernels: 104 us -> 124 us
  waiting for transfers between devices: 316 us -> 296 us
  other arithmetic: 40.4 us -> 30.1 us
  starting transfers between devices: 76.7 us -> 85.4 us
  matrix products: 26.8 us -> 18.4 us
    all_gather x3, waiting for transfers between devices: 55.6 us -> 33.6 us  [shard_gather(): return lax.all_gather(values, SHD, axis=0, tiled=True)]
    pallas_call x2 -> x4, Pallas kernels: 22.7 us -> 43.1 us  [the longest x3 37.6 us: call(): pl.pallas_call(kernel, grid=(STEPS,), in_specs=[specs.get(n, whole_block(...]
    ppermute x0 -> x7, starting transfers between devices: none -> 9.69 us  [local(): lax.ppermute(gain_own, SHD, [(i, i ^ j) for i in range(S)])]
    dot_general x4 -> x2, matrix products: 15.2 us -> 7.33 us  [dot(): return jnp.dot(left, right, preferred_element_type=F32)]
    unnamed x171 -> x129, local copies, waits for them, and re-layouts: 18.6 us -> 22.3 us
  transfers between devices with their start and end apart: 70 -> 77, of which waited for: 33 -> 36; matrix products, arithmetic and copies ran while one was open for 16% -> 13% of each run, Pallas kernels for 11% -> 15%
where the time goes in v3:
time: 628 us; the launch traced here: 622 us
  waiting for transfers between devices  296 us (47%)
  Pallas kernels  124 us (20%)
  starting transfers between devices  85.4 us (14%)
  local copies, waits for them, and re-layouts  52.5 us (8%)
  other arithmetic  30.1 us (5%)
  matrix products  18.4 us (3%)
  between operations  15.4 us (2%)
    ppermute x63, waiting for transfers between devices, send(): return lax.ppermute(values, REP, links[k])  244 us
    ppermute x63, starting transfers between devices, send(): return lax.ppermute(values, REP, links[k])  75.4 us
    pallas_call x3, Pallas kernels, call(): pl.pallas_call(kernel, grid=(STEPS,), in_specs=[specs.get(n, whole_block(...  37.6 us
    all_gather x3, waiting for transfers between devices, shard_gather(): return lax.all_gather(values, SHD, axis=0, tiled=True)  33.6 us
    unnamed x129, local copies, waits for them, and re-layouts  22.3 us
    pallas_call x4, Pallas kernels, join_blocks(): pl.pallas_call(body, in_specs=[pl.BlockSpec(memory_space=pltpu.SMEM)] + [...  19.5 us
    reduce_scatter x4, waiting for transfers between devices, shard_reduce(): return lax.psum_scatter(values, SHD, scatter_dimension=0, tiled=True)  18 us
    pallas_call x1, Pallas kernels, local(): forward(r_one, qlat, qlat, lat_n, cosine, sine, bias, *out_ws, *kvus)  13.8 us
  transfers between devices with their start and end apart: 77, of which 36 were waited for; matrix products, arithmetic and copies ran while one was open for 13% of the time, Pallas kernels for 15%

profile of v3, /device:TPU:0, one launch (start us, length us, event | category | flops | bytes accessed | tf_op | source)
XLA Modules:
  0.0 621.6 jit_solution(5405853526707210698)
XLA Ops:
  11.7 2.0 concatenate.40
  18.0 2.2 concatenate.42
  21.4 2.6 collective-permute-start.4
  24.1 2.8 collective-permute-start.6
  31.6 3.6 collective-permute-start.8
  35.3 2.5 collective-permute-start.2
  42.4 8.1 %collective-permute-done.12 = bf16[8,128]{1,0:T(8,128)(2,1)S(1)} collective-permute-done((bf16[8,128]{1,0:T(8,128)(2,1)S(1)}, bf16[8,128]{1,0:T(8,128)(2,1)S(1)}, u32[]{:S(2)}, u32[]{:S(2)}) %collective-permute-start.12) | collective-permute-done | bytes 2080 | tf_op jit(solution)/shard_map/ppermute | solution.py:442
  52.0 9.7 %collective-permute-done.11 = bf16[8,128]{1,0:T(8,128)(2,1)S(1)} collective-permute-done((bf16[8,128]{1,0:T(8,128)(2,1)S(1)}, bf16[8,128]{1,0:T(8,128)(2,1)S(1)}, u32[]{:S(2)}, u32[]{:S(2)}) %collective-permute-start.11) | collective-permute-done | bytes 2080 | tf_op jit(solution)/shard_map/ppermute | solution.py:442
  66.1 2.2 multiply_sine_fusion
  68.9 4.2 fusion.4.refs_1_
  73.1 30.2 %all-gather.4.cloned.1.call-done.refs_5_ = bf16[2048,2176]{1,0:T(8,128)(2,1)} async-done(((bf16[256,2176]{1,0:T(8,128)(2,1)}), bf16[2048,2176]{1,0:T(8,128)(2,1)}) %all-gather.4.cloned.1.call-update) | async-done | bytes 8912912 | tf_op jit(solution)/shard_map/all_gather | solution.py:497
  103.3 3.1 fusion.39
  109.9 6.0 fusion.refs_1_.refs_2_
  118.5 8.4 %collective-permute-done.13.refs_8_.refs_12_.refs_6_.refs_10_ = bf16[512,768]{1,0:T(8,128)(2,1)S(1)} collective-permute-done((bf16[512,768]{1,0:T(8,128)(2,1)S(1)}, bf16[512,768]{1,0:T(8,128)(2,1)S(1)}, u32[]{:S(2)}, u32[]{:S(2)}) %collective-permute-start.13) | collective-permute-done | bytes 786464 | tf_op jit(solution)/shard_map/ppermute | solution.py:442
  126.8 17.3 %collective-permute-done.14.refs_9_.refs_13_.refs_7_.refs_11_ = bf16[512,768]{1,0:T(8,128)(2,1)S(1)} collective-permute-done((bf16[512,768]{1,0:T(8,128)(2,1)S(1)}, bf16[512,768]{1,0:T(8,128)(2,1)S(1)}, u32[]{:S(2)}, u32[]{:S(2)}) %collective-permute-start.14) | collective-permute-done | bytes 786464 | tf_op jit(solution)/shard_map/ppermute | solution.py:442
  145.3 13.8 %shard_map.297 = (bf16[512,512]{1,0:T(8,128)(2,1)}, f32[16,128,128]{2,1,0:T(8,128)}, bf16[512,768]{1,0:T(8,128)(2,1)}, bf16[512,256]{1,0:T(8,128)(2,1)}, bf16[51...) custom-call(s32[1]{0:T(128)} %bitcast.refs_0_.r_ref, ...), custom_call_target="tpu_custom_call" | custom-call | tf_op jit(solution)/shard_map/pallas_call | solution.py:646
  166.7 1.9 constant_dynamic-update-slice_fusion.1
  168.7 6.4 %collective-permute-done.18 = bf16[128,2048]{1,0:T(8,128)(2,1)S(1)} collective-permute-done((bf16[128,2048]{1,0:T(8,128)(2,1)}, bf16[128,2048]{1,0:T(8,128)(2,1)S(1)}, u32[]{:S(2)}, u32[]{:S(2)}) %collective-permute-start.18) | collective-permute-done | bytes 524320 | tf_op jit(solution)/shard_map/ppermute | solution.py:442
  175.1 11.1 %collective-permute-done.17 = bf16[128,2048]{1,0:T(8,128)(2,1)S(1)} collective-permute-done((bf16[128,2048]{1,0:T(8,128)(2,1)}, bf16[128,2048]{1,0:T(8,128)(2,1)S(1)}, u32[]{:S(2)}, u32[]{:S(2)}) %collective-permute-start.17) | collective-permute-done | bytes 524320 | tf_op jit(solution)/shard_map/ppermute | solution.py:442
  191.6 6.0 collective-permute-done.24
  200.3 8.6 %collective-permute-done.19.refs_1_ = bf16[128,2048]{1,0:T(8,128)(2,1)S(1)} collective-permute-done((bf16[128,2048]{1,0:T(8,128)(2,1)S(1)}, bf16[128,2048]{1,0:T(8,128)(2,1)S(1)}, u32[]{:S(2)}, u32[]{:S(2)}) %collective-permute-start.19) | collective-permute-done | bytes 524320 | tf_op jit(solution)/shard_map/ppermute | solution.py:442
  208.9 9.4 %collective-permute-done.21.refs_3_ = bf16[128,2048]{1,0:T(8,128)(2,1)} collective-permute-done((bf16[128,2048]{1,0:T(8,128)(2,1)S(1)}, bf16[128,2048]{1,0:T(8,128)(2,1)}, u32[]{:S(2)}, u32[]{:S(2)}) %collective-permute-start.21) | collective-permute-done | bytes 524320 | tf_op jit(solution)/shard_map/ppermute | solution.py:442
  219.1 14.8 %shard_map.298 = (bf16[512,2048]{1,0:T(8,128)(2,1)}, bf16[64,2048]{1,0:T(8,128)(2,1)}, f32[512,704]{1,0:T(8,128)}, f32[512,704]{1,0:T(8,128)}, bf16[512,704]{1,0...) custom-call(bf16[128,2048]{1,0:T(8,128)(2,1)} %copy-done.17, ...), custom_call_target="tpu_custom_call" | custom-call | tf_op jit(solution)/shard_map/pallas_call | solution.py:667
  233.9 3.4 all-gather.8.cloned.1.call-done.refs_1_
  237.3 12.8 %shard_map.299 = (bf16[512,1408]{1,0:T(8,128)(2,1)}, bf16[64,704]{1,0:T(8,128)(2,1)}, f32[64,2048]{1,0:T(8,128)}, f32[512,128]{1,0:T(8,128)}, bf16[512,64]{1,0:T(8,128)(2,1)}) custom-call(bf16[512,2048]{1,0:T(8,128)(2,1)} %copy-done.5, bf16[2048,1024]{1,0:T(8,128)(2,1)} %all-gather.8.cloned.1.call-done.refs_1_, ...), custom_call_target="tpu_custom_call" | custom-call | tf_op jit(solution)/shard_map/pallas_call | solution.py:667
  250.1 9.2 %shard_map.308 = bf16[2048,2560]{1,0:T(8,128)(2,1)} custom-call(bf16[512,2048]{1,0:T(8,128)(2,1)} %get-tuple-element.100.refs_2_.refs_0_, bf16[512,1408]{1,0:T(8,128)(2,1)} %get-tuple-element.83.refs_0_.refs_1_, bf16[64,2048]{1,0:T(8,128)(2,1)} %get-tuple-element.108.refs_2_, bf16[64,704]{1,0:T(8,128)(2,1)} %get-tuple-element.84.refs_1_.refs_3_, ...), custom_call_target="tpu_custom_call" | custom-call | tf_op jit(solution)/shard_map/pallas_call | solution.py:743
  264.1 10.0 %shard_map.302 = (bf16[128,2048]{1,0:T(8,128)(2,1)}, bf16[128,2048]{1,0:T(8,128)(2,1)}, bf16[128,2048]{1,0:T(8,128)(2,1)}, bf16[128,2048]{1,0:T(8,128)(2,1)}) custom-call(bf16[512,1408]{1,0:T(8,128)(2,1)} %get-tuple-element.83.refs_0_.refs_1_, bf16[64,704]{1,0:T(8,128)(2,1)} %get-tuple-element.84.refs_1_.refs_3_, bf16[512,64]{1,0:T(8,128)(2,1)} %get-tuple-element.85.refs_2_, ...), custom_call_target="tpu_custom_call" | custom-call | tf_op jit(solution)/shard_map/pallas_call | solution.py:667
  274.1 2.6 collective-permute-start.30
  277.6 12.4 %collective-permute-done.30 = bf16[128,2048]{1,0:T(8,128)(2,1)S(1)} collective-permute-done((bf16[128,2048]{1,0:T(8,128)(2,1)}, bf16[128,2048]{1,0:T(8,128)(2,1)S(1)}, u32[]{:S(2)}, u32[]{:S(2)}) %collective-permute-start.30) | collective-permute-done | bytes 524320 | tf_op jit(solution)/shard_map/ppermute | solution.py:442
  290.1 10.3 %collective-permute-done.29 = bf16[128,2048]{1,0:T(8,128)(2,1)S(1)} collective-permute-done((bf16[128,2048]{1,0:T(8,128)(2,1)}, bf16[128,2048]{1,0:T(8,128)(2,1)S(1)}, u32[]{:S(2)}, u32[]{:S(2)}) %collective-permute-start.29) | collective-permute-done | bytes 524320 | tf_op jit(solution)/shard_map/ppermute | solution.py:442
  311.4 7.2 %collective-permute-done.31.refs_2_.refs_4_ = bf16[128,2048]{1,0:T(8,128)(2,1)S(1)} collective-permute-done((bf16[128,2048]{1,0:T(8,128)(2,1)S(1)}, bf16[128,2048]{1,0:T(8,128)(2,1)S(1)}, u32[]{:S(2)}, u32[]{:S(2)}) %collective-permute-start.31) | collective-permute-done | bytes 524320 | tf_op jit(solution)/shard_map/ppermute | solution.py:442
  318.6 11.5 %collective-permute-done.32.refs_3_.refs_5_ = bf16[128,2048]{1,0:T(8,128)(2,1)S(1)} collective-permute-done((bf16[128,2048]{1,0:T(8,128)(2,1)S(1)}, bf16[128,2048]{1,0:T(8,128)(2,1)S(1)}, u32[]{:S(2)}, u32[]{:S(2)}) %collective-permute-start.32) | collective-permute-done | bytes 524320 | tf_op jit(solution)/shard_map/ppermute | solution.py:442
  330.9 13.4 %shard_map.303 = (bf16[512,768]{1,0:T(8,128)(2,1)}, bf16[512,1024]{1,0:T(8,128)(2,1)}, bf16[128,640]{1,0:T(8,128)(2,1)}, bf16[128,640]{1,0:T(8,128)(2,1)}, bf16[...) custom-call(s32[1]{0:T(128)} %bitcast.refs_0_.r_ref, bf16[128,2048]{1,0:T(8,128)(2,1)} %copy-done.11, ...), custom_call_target="tpu_custom_call" | custom-call | tf_op jit(solution)/shard_map/pallas_call | solution.py:814
  348.8 3.0 collective-permute-done.36
  363.7 2.3 collective-permute-done.38
  366.4 2.5 fusion.18
  369.0 6.9 %fusion.6 = (f32[2048]{0:T(1024)S(1)}, bf16[512,2048]{1,0:T(8,128)(2,1)}, f32[512,2048]{1,0:T(8,128)}) fusion(f32[512]{0:T(512)S(1)} %add_rsqrt_fusion.1, bf16[128,2048]{1,0:T(8,128)(2,1)S(1)} %copy-done.20, bf16[128,2048]{1,0:T(8,128)(2,1)S(1)} %copy-done.22, bf16[128,2048]{1,0:T(8,128)(2,1)S(1)} %copy-done.24, bf16[128,2048]{1,0:T(8,128)(2,1)S(1)} %copy-done.7, ...), kind=kOutput, calls=%fused_computation.9 | convolution fusion | flops 1624242176 | bytes 16525312 | tf_op jit(solution)/shard_map/dot_general | solution.py:32
  387.1 3.6 collective-permute-done.49.refs_7_
  390.7 3.6 collective-permute-done.50.refs_8_
  395.1 8.2 %shard_map.304 = bf16[2048,512]{1,0:T(8,128)(2,1)} custom-call(s32[1]{0:T(128)} %bitcast.refs_0_.r_ref, bf16[512,2048]{1,0:T(8,128)(2,1)} %fusion.4.refs_1_, bf16[512,2048]{1,0:T(8,128)(2,1)} %get-tuple-element.100.refs_2_.refs_0_, bf16[512,144]{1,0:T(8,128)(2,1)} %copy-done.12, bf16[512,16]{1,0:T(8,128)(2,1)} %fusion.24.refs_4_, ...), custom_call_target="tpu_custom_call" | custom-call | tf_op jit(solution)/shard_map/pallas_call | solution.py:871
  403.4 5.5 shard_map.310
  413.4 11.3 %collective-permute-done.52.refs_8_ = bf16[512,512]{1,0:T(8,128)(2,1)S(1)} collective-permute-done((bf16[512,512]{1,0:T(8,128)(2,1)S(1)}, bf16[512,512]{1,0:T(8,128)(2,1)S(1)}, u32[]{:S(2)}, u32[]{:S(2)}) %collective-permute-start.52) | collective-permute-done | bytes 524320 | tf_op jit(solution)/shard_map/ppermute | solution.py:442
  424.8 7.2 %collective-permute-done.53.refs_9_ = bf16[512,512]{1,0:T(8,128)(2,1)S(1)} collective-permute-done((bf16[512,512]{1,0:T(8,128)(2,1)S(1)}, bf16[512,512]{1,0:T(8,128)(2,1)S(1)}, u32[]{:S(2)}, u32[]{:S(2)}) %collective-permute-start.53) | collective-permute-done | bytes 524320 | tf_op jit(solution)/shard_map/ppermute | solution.py:442
  432.8 7.9 %shard_map.305 = bf16[2048,1280]{1,0:T(8,128)(2,1)} custom-call(s32[1]{0:T(128)} %bitcast.refs_0_.r_ref, bf16[512,2048]{1,0:T(8,128)(2,1)} %fusion.4.refs_1_, bf16[512,768]{1,0:T(8,128)(2,1)} %get-tuple-element.95.refs_2_, bf16[128,2048]{1,0:T(8,128)(2,1)} %copy-done.11, bf16[128,2048]{1,0:T(8,128)(2,1)} %copy-done.15, bf16[128,2048]{1,0:T(8,128)(2,1)} %copy-done.16, ...), custom_call_target="tpu_custom_call" | custom-call | tf_op jit(solution)/shard_map/pallas_call | solution.py:817
  440.7 6.1 shard_map.300
  447.9 2.4 collective-permute-start.27
  451.4 2.5 fusion.40
  453.9 7.9 %collective-permute-done.25.refs_1_ = bf16[128,2048]{1,0:T(8,128)(2,1)S(1)} collective-permute-done((bf16[128,2048]{1,0:T(8,128)(2,1)}, bf16[128,2048]{1,0:T(8,128)(2,1)S(1)}, u32[]{:S(2)}, u32[]{:S(2)}) %collective-permute-start.25) | collective-permute-done | bytes 524320 | tf_op jit(solution)/shard_map/ppermute | solution.py:442
  463.1 7.9 %collective-permute-done.26.refs_2_ = bf16[128,2048]{1,0:T(8,128)(2,1)S(1)} collective-permute-done((bf16[128,2048]{1,0:T(8,128)(2,1)}, bf16[128,2048]{1,0:T(8,128)(2,1)S(1)}, u32[]{:S(2)}, u32[]{:S(2)}) %collective-permute-start.26) | collective-permute-done | bytes 524320 | tf_op jit(solution)/shard_map/ppermute | solution.py:442
  473.5 2.2 collective-permute-start.40
  475.7 36.4 %collective-permute-done.42 = bf16[128,2048]{1,0:T(8,128)(2,1)S(1)} collective-permute-done((bf16[128,2048]{1,0:T(8,128)(2,1)S(1)}, bf16[128,2048]{1,0:T(8,128)(2,1)S(1)}, u32[]{:S(2)}, u32[]{:S(2)}) %collective-permute-start.42) | collective-permute-done | bytes 524320 | tf_op jit(solution)/shard_map/ppermute | solution.py:442
  512.9 3.0 shard_map.301
  515.9 2.3 collective-permute-done.41
  519.9 2.2 fusion.14
  522.1 17.9 %reduce-scatter.7.cloned.1.call-done.refs_0_ = bf16[256,1280]{1,0:T(8,128)(2,1)} async-done(((bf16[2048,1280]{1,0:T(8,128)(2,1)}), bf16[256,1280]{1,0:T(8,128)(2,1)}) %reduce-scatter.7.cloned.1.call-update) | async-done | bytes 655376 | tf_op jit(solution)/shard_map/reduce_scatter | solution.py:500
  547.2 2.7 fusion.13
  552.1 5.8 collective-permute-done.55.refs_1_
  559.4 5.6 collective-permute-done.56.refs_2_
  567.5 3.1 collective-permute-done.60.refs_2_
  576.4 13.8 %collective-permute-done.68.refs_3_ = bf16[128,704]{1,0:T(8,128)(2,1)S(1)} collective-permute-done((bf16[128,704]{1,0:T(8,128)(2,1)S(1)}, bf16[128,704]{1,0:T(8,128)(2,1)S(1)}, u32[]{:S(2)}, u32[]{:S(2)}) %collective-permute-start.68) | collective-permute-done | bytes 180256 | tf_op jit(solution)/shard_map/ppermute | solution.py:442
  592.2 2.9 shard_map.307
  596.6 3.5 shard_map.311
  601.5 5.2 shard_map.306
  606.7 7.8 %shard_map.309 = (f32[256,2816]{1,0:T(8,128)}, f32[256,2816]{1,0:T(8,128)}, f32[256,1408]{1,0:T(8,128)}, f32[256,1408]{1,0:T(8,128)}, f32[1408,256]{1,0:T(8,128)}) custom-call(s32[1]{0:T(128)} %bitcast.refs_0_.r_ref, bf16[256,2560]{1,0:T(8,128)(2,1)} %reduce-scatter.9.cloned.1.call-done.refs_0_, bf16[256,2560]{1,0:T(8,128)(2,1)} %collective-permute-done.62.refs_1_, ...), custom_call_target="tpu_custom_call" | custom-call | tf_op jit(solution)/shard_map/pallas_call | solution.py:414
  (369 shorter events, 133.2 us)
Async XLA Ops:
  7.2 96.1 %all-gather.4.cloned.1.call-start = ((), (), s32[]{:S(2)}) async-start(), calls=%async_computation.4 | async-start | bytes 10027008 | tf_op jit(solution)/shard_map/all_gather | solution.py:497
  13.8 186.5 %all-gather.6.cloned.1.call-start = ((), (), s32[]{:S(2)}) async-start(), calls=%async_computation.5 | async-start | bytes 10027008 | tf_op jit(solution)/shard_map/all_gather | solution.py:497
  20.2 217.1 %all-gather.8.cloned.1.call-start = ((), (), s32[]{:S(2)}) async-start(), calls=%async_computation.6 | async-start | bytes 4718592 | tf_op jit(solution)/shard_map/all_gather | solution.py:497
  20.9 10.7 %collective-permute-start.3 = (bf16[576]{0:T(1024)(128)(2,1)S(1)}, bf16[576]{0:T(1024)(128)(2,1)S(1)}, u32[]{:S(2)}, u32[]{:S(2)}) collective-permute-start(bf16[576]{0:T(1024)(128)(2,1)S(1)} %dynamic-update-slice.6), channel_id=1, source_target_pairs={{0,1},{1,0},{2,3},{3,2},{4,5},{5,4},{6,7},{7,6},{8,9},{9,8},{10,11... | collective-permute-start | bytes 3464 | tf_op jit(solution)/shard_map/ppermute | solution.py:571
  21.4 13.8 %collective-permute-start.4 = (bf16[576]{0:T(1024)(128)(2,1)S(1)}, bf16[576]{0:T(1024)(128)(2,1)S(1)}, u32[]{:S(2)}, u32[]{:S(2)}) collective-permute-start(bf16[576]{0:T(1024)(128)(2,1)S(1)} %dynamic-update-slice.6), channel_id=1, source_target_pairs={{0,2},{1,3},{2,0},{3,1},{4,6},{5,7},{6,4},{7,5},{8,10},{9,11},{10,... | collective-permute-start | bytes 3464 | tf_op jit(solution)/shard_map/ppermute | solution.py:571
  24.1 11.3 %collective-permute-start.5 = (bf16[576]{0:T(1024)(128)(2,1)S(1)}, bf16[576]{0:T(1024)(128)(2,1)S(1)}, u32[]{:S(2)}, u32[]{:S(2)}) collective-permute-start(bf16[576]{0:T(1024)(128)(2,1)S(1)} %dynamic-update-slice.6), channel_id=1, source_target_pairs={{0,3},{1,2},{2,1},{3,0},{4,7},{5,6},{6,5},{7,4},{8,11},{9,10},{10,... | collective-permute-start | bytes 3464 | tf_op jit(solution)/shard_map/ppermute | solution.py:571
  24.1 13.7 %collective-permute-start.6 = (bf16[576]{0:T(1024)(128)(2,1)S(1)}, bf16[576]{0:T(1024)(128)(2,1)S(1)}, u32[]{:S(2)}, u32[]{:S(2)}) collective-permute-start(bf16[576]{0:T(1024)(128)(2,1)S(1)} %dynamic-update-slice.6), channel_id=1, source_target_pairs={{0,4},{1,5},{2,6},{3,7},{4,0},{5,1},{6,2},{7,3},{8,12},{9,13},{10,... | collective-permute-start | bytes 3464 | tf_op jit(solution)/shard_map/ppermute | solution.py:571
  26.9 11.6 %collective-permute-start.7 = (bf16[576]{0:T(1024)(128)(2,1)S(1)}, bf16[576]{0:T(1024)(128)(2,1)S(1)}, u32[]{:S(2)}, u32[]{:S(2)}) collective-permute-start(bf16[576]{0:T(1024)(128)(2,1)S(1)} %dynamic-update-slice.6), channel_id=1, source_target_pairs={{0,5},{1,4},{2,7},{3,6},{4,1},{5,0},{6,3},{7,2},{8,13},{9,12},{10,... | collective-permute-start | bytes 3464 | tf_op jit(solution)/shard_map/ppermute | solution.py:571
  29.0 421.3 %reduce-scatter.9.cloned.1.call-start = ((), (), s32[]{:S(2)}) async-start(), calls=%async_computation.9 | async-start | bytes 11796480 | tf_op jit(solution)/shard_map/reduce_scatter | solution.py:500
  35.3 33.0 %collective-permute-start.2 = (bf16[128,2048]{1,0:T(8,128)(2,1)S(1)}, bf16[128,2048]{1,0:T(8,128)(2,1)S(1)}, u32[]{:S(2)}, u32[]{:S(2)}) collective-permute-start(bf16[128,2048]{1,0:T(8,128)(2,1)S(1)} %copy-done.7), channel_id=1, source_target_pairs={{0,24},{8,16},{16,8},{24,0},{1,25},{9,17},{17,9},{25,1},{2,26},{10... | collective-permute-start | bytes 1572872 | tf_op jit(solution)/shard_map/ppermute | solution.py:442
  37.8 30.5 %collective-permute-start.1 = (bf16[128,2048]{1,0:T(8,128)(2,1)S(1)}, bf16[128,2048]{1,0:T(8,128)(2,1)S(1)}, u32[]{:S(2)}, u32[]{:S(2)}) collective-permute-start(bf16[128,2048]{1,0:T(8,128)(2,1)S(1)} %copy-done.7), channel_id=1, source_target_pairs={{0,16},{8,24},{16,0},{24,8},{1,17},{9,25},{17,1},{25,9},{2,18},{10... | collective-permute-start | bytes 1572872 | tf_op jit(solution)/shard_map/ppermute | solution.py:442
  38.4 12.1 %collective-permute-start.12 = (bf16[8,128]{1,0:T(8,128)(2,1)S(1)}, bf16[8,128]{1,0:T(8,128)(2,1)S(1)}, u32[]{:S(2)}, u32[]{:S(2)}) collective-permute-start(bf16[8,128]{1,0:T(8,128)(2,1)S(1)} %get-tuple-element.169), channel_id=1, source_target_pairs={{0,24},{8,16},{16,8},{24,0},{1,25},{9,17},{17,9},{25,1},{2,26},{10... | collective-permute-start | bytes 6152 | tf_op jit(solution)/shard_map/ppermute | solution.py:442
  40.0 21.7 %collective-permute-start.11 = (bf16[8,128]{1,0:T(8,128)(2,1)S(1)}, bf16[8,128]{1,0:T(8,128)(2,1)S(1)}, u32[]{:S(2)}, u32[]{:S(2)}) collective-permute-start(bf16[8,128]{1,0:T(8,128)(2,1)S(1)} %get-tuple-element.169), channel_id=1, source_target_pairs={{0,16},{8,24},{16,0},{24,8},{1,17},{9,25},{17,1},{25,9},{2,18},{10... | collective-permute-start | bytes 6152 | tf_op jit(solution)/shard_map/ppermute | solution.py:442
  40.6 22.6 %collective-permute-start.10 = (bf16[8,128]{1,0:T(8,128)(2,1)S(1)}, bf16[8,128]{1,0:T(8,128)(2,1)S(1)}, u32[]{:S(2)}, u32[]{:S(2)}) collective-permute-start(bf16[8,128]{1,0:T(8,128)(2,1)S(1)} %get-tuple-element.169), channel_id=1, source_target_pairs={{0,8},{8,0},{16,24},{24,16},{1,9},{9,1},{17,25},{25,17},{2,10},{10... | collective-permute-start | bytes 6152 | tf_op jit(solution)/shard_map/ppermute | solution.py:442
  50.5 17.9 %collective-permute-start = (bf16[128,2048]{1,0:T(8,128)(2,1)S(1)}, bf16[128,2048]{1,0:T(8,128)(2,1)S(1)}, u32[]{:S(2)}, u32[]{:S(2)}) collective-permute-start(bf16[128,2048]{1,0:T(8,128)(2,1)S(1)} %copy-done.7), channel_id=1, source_target_pairs={{0,8},{8,0},{16,24},{24,16},{1,9},{9,1},{17,25},{25,17},{2,10},{10... | collective-permute-start | bytes 1572872 | tf_op jit(solution)/shard_map/ppermute | solution.py:442
  61.7 101.6 %collective-permute-start.22 = (bf16[128,2048]{1,0:T(8,128)(2,1)}, bf16[128,2048]{1,0:T(8,128)(2,1)}, u32[]{:S(2)}, u32[]{:S(2)}) collective-permute-start(bf16[128,2048]{1,0:T(8,128)(2,1)} %param.35), channel_id=1, source_target_pairs={{0,8},{8,0},{16,24},{24,16},{1,9},{9,1},{17,25},{25,17},{2,10},{10... | collective-permute-start | bytes 1572872 | tf_op jit(solution)/shard_map/ppermute | solution.py:442
  63.2 103.6 %collective-permute-start.23 = (bf16[128,2048]{1,0:T(8,128)(2,1)}, bf16[128,2048]{1,0:T(8,128)(2,1)}, u32[]{:S(2)}, u32[]{:S(2)}) collective-permute-start(bf16[128,2048]{1,0:T(8,128)(2,1)} %param.35), channel_id=1, source_target_pairs={{0,16},{8,24},{16,0},{24,8},{1,17},{9,25},{17,1},{25,9},{2,18},{10... | collective-permute-start | bytes 1572872 | tf_op jit(solution)/shard_map/ppermute | solution.py:442
  106.4 20.4 %collective-permute-start.13 = (bf16[512,768]{1,0:T(8,128)(2,1)S(1)}, bf16[512,768]{1,0:T(8,128)(2,1)S(1)}, u32[]{:S(2)}, u32[]{:S(2)}) collective-permute-start(bf16[512,768]{1,0:T(8,128)(2,1)S(1)} %get-tuple-element.128), channel_id=1, source_target_pairs={{0,8},{8,0},{16,24},{24,16},{1,9},{9,1},{17,25},{25,17},{2,10},{10... | collective-permute-start | bytes 2359304 | tf_op jit(solution)/shard_map/ppermute | solution.py:442
  107.9 36.3 %collective-permute-start.14 = (bf16[512,768]{1,0:T(8,128)(2,1)S(1)}, bf16[512,768]{1,0:T(8,128)(2,1)S(1)}, u32[]{:S(2)}, u32[]{:S(2)}) collective-permute-start(bf16[512,768]{1,0:T(8,128)(2,1)S(1)} %get-tuple-element.127), channel_id=1, source_target_pairs={{0,16},{8,24},{16,0},{24,8},{1,17},{9,25},{17,1},{25,9},{2,18},{10... | collective-permute-start | bytes 2359304 | tf_op jit(solution)/shard_map/ppermute | solution.py:442
  109.4 34.8 %collective-permute-start.15 = (bf16[512,768]{1,0:T(8,128)(2,1)S(1)}, bf16[512,768]{1,0:T(8,128)(2,1)S(1)}, u32[]{:S(2)}, u32[]{:S(2)}) collective-permute-start(bf16[512,768]{1,0:T(8,128)(2,1)S(1)} %get-tuple-element.126), channel_id=1, source_target_pairs={{0,24},{8,16},{16,8},{24,0},{1,25},{9,17},{17,9},{25,1},{2,26},{10... | collective-permute-start | bytes 2359304 | tf_op jit(solution)/shard_map/ppermute | solution.py:442
  159.1 16.0 %collective-permute-start.18 = (bf16[128,2048]{1,0:T(8,128)(2,1)}, bf16[128,2048]{1,0:T(8,128)(2,1)S(1)}, u32[]{:S(2)}, u32[]{:S(2)}) collective-permute-start(bf16[128,2048]{1,0:T(8,128)(2,1)} %get-tuple-element.68), channel_id=1, source_target_pairs={{0,24},{8,16},{16,8},{24,0},{1,25},{9,17},{17,9},{25,1},{2,26},{10... | collective-permute-start | bytes 1572872 | tf_op jit(solution)/shard_map/ppermute | solution.py:442
  160.7 25.5 %collective-permute-start.17 = (bf16[128,2048]{1,0:T(8,128)(2,1)}, bf16[128,2048]{1,0:T(8,128)(2,1)S(1)}, u32[]{:S(2)}, u32[]{:S(2)}) collective-permute-start(bf16[128,2048]{1,0:T(8,128)(2,1)} %get-tuple-element.67), channel_id=1, source_target_pairs={{0,16},{8,24},{16,0},{24,8},{1,17},{9,25},{17,1},{25,9},{2,18},{10... | collective-permute-start | bytes 1572872 | tf_op jit(solution)/shard_map/ppermute | solution.py:442
  161.6 24.7 %collective-permute-start.16 = (bf16[128,2048]{1,0:T(8,128)(2,1)}, bf16[128,2048]{1,0:T(8,128)(2,1)S(1)}, u32[]{:S(2)}, u32[]{:S(2)}) collective-permute-start(bf16[128,2048]{1,0:T(8,128)(2,1)} %get-tuple-element.66), channel_id=1, source_target_pairs={{0,8},{8,0},{16,24},{24,16},{1,9},{9,1},{17,25},{25,17},{2,10},{10... | collective-permute-start | bytes 1572872 | tf_op jit(solution)/shard_map/ppermute | solution.py:442
  163.3 34.3 %collective-permute-start.24 = (bf16[128,2048]{1,0:T(8,128)(2,1)}, bf16[128,2048]{1,0:T(8,128)(2,1)S(1)}, u32[]{:S(2)}, u32[]{:S(2)}) collective-permute-start(bf16[128,2048]{1,0:T(8,128)(2,1)} %param.35), channel_id=1, source_target_pairs={{0,24},{8,16},{16,8},{24,0},{1,25},{9,17},{17,9},{25,1},{2,26},{10... | collective-permute-start | bytes 1572872 | tf_op jit(solution)/shard_map/ppermute | solution.py:442
  188.1 20.8 %collective-permute-start.19 = (bf16[128,2048]{1,0:T(8,128)(2,1)S(1)}, bf16[128,2048]{1,0:T(8,128)(2,1)S(1)}, u32[]{:S(2)}, u32[]{:S(2)}) collective-permute-start(bf16[128,2048]{1,0:T(8,128)(2,1)S(1)} %multiply_convert_fusion.refs_0_), channel_id=1, source_target_pairs={{0,8},{8,0},{16,24},{24,16},{1,9},{9,1},{17,25},{25,17},{2,10},{10... | collective-permute-start | bytes 1572872 | tf_op jit(solution)/shard_map/ppermute | solution.py:442
  189.0 19.8 %collective-permute-start.20 = (bf16[128,2048]{1,0:T(8,128)(2,1)S(1)}, bf16[128,2048]{1,0:T(8,128)(2,1)S(1)}, u32[]{:S(2)}, u32[]{:S(2)}) collective-permute-start(bf16[128,2048]{1,0:T(8,128)(2,1)S(1)} %multiply_convert_fusion.refs_0_), channel_id=1, source_target_pairs={{0,16},{8,24},{16,0},{24,8},{1,17},{9,25},{17,1},{25,9},{2,18},{10... | collective-permute-start | bytes 1572872 | tf_op jit(solution)/shard_map/ppermute | solution.py:442
  190.1 28.1 %collective-permute-start.21 = (bf16[128,2048]{1,0:T(8,128)(2,1)S(1)}, bf16[128,2048]{1,0:T(8,128)(2,1)}, u32[]{:S(2)}, u32[]{:S(2)}) collective-permute-start(bf16[128,2048]{1,0:T(8,128)(2,1)S(1)} %multiply_convert_fusion.refs_0_), channel_id=1, source_target_pairs={{0,24},{8,16},{16,8},{24,0},{1,25},{9,17},{17,9},{25,1},{2,26},{10... | collective-permute-start | bytes 1572872 | tf_op jit(solution)/shard_map/ppermute | solution.py:442
  259.3 252.7 %reduce-scatter.5.cloned.1.call-start = ((), (), s32[]{:S(2)}) async-start(), calls=%async_computation.7 | async-start | bytes 2359296 | tf_op jit(solution)/shard_map/reduce_scatter | solution.py:500
  260.5 16.7 %collective-permute-start.44 = (f32[4,128]{1,0:T(4,128)S(1)}, f32[4,128]{1,0:T(4,128)S(1)}, u32[]{:S(2)}, u32[]{:S(2)}) collective-permute-start(f32[4,128]{1,0:T(4,128)S(1)} %bitcast.105), channel_id=1, source_target_pairs={{0,16},{8,24},{16,0},{24,8},{1,17},{9,25},{17,1},{25,9},{2,18},{10... | collective-permute-start | bytes 6152 | tf_op jit(solution)/shard_map/ppermute | solution.py:442
  262.1 15.6 %collective-permute-start.45 = (f32[4,128]{1,0:T(4,128)S(1)}, f32[4,128]{1,0:T(4,128)S(1)}, u32[]{:S(2)}, u32[]{:S(2)}) collective-permute-start(f32[4,128]{1,0:T(4,128)S(1)} %bitcast.106), channel_id=1, source_target_pairs={{0,24},{8,16},{16,8},{24,0},{1,25},{9,17},{17,9},{25,1},{2,26},{10... | collective-permute-start | bytes 6152 | tf_op jit(solution)/shard_map/ppermute | solution.py:442
  263.5 45.5 %collective-permute-start.43 = (f32[4,128]{1,0:T(4,128)S(1)}, f32[4,128]{1,0:T(4,128)S(1)}, u32[]{:S(2)}, u32[]{:S(2)}) collective-permute-start(f32[4,128]{1,0:T(4,128)S(1)} %bitcast.107), channel_id=1, source_target_pairs={{0,8},{8,0},{16,24},{24,16},{1,9},{9,1},{17,25},{25,17},{2,10},{10... | collective-permute-start | bytes 6152 | tf_op jit(solution)/shard_map/ppermute | solution.py:442
  274.1 16.0 %collective-permute-start.30 = (bf16[128,2048]{1,0:T(8,128)(2,1)}, bf16[128,2048]{1,0:T(8,128)(2,1)S(1)}, u32[]{:S(2)}, u32[]{:S(2)}) collective-permute-start(bf16[128,2048]{1,0:T(8,128)(2,1)} %get-tuple-element.89), channel_id=1, source_target_pairs={{0,24},{8,16},{16,8},{24,0},{1,25},{9,17},{17,9},{25,1},{2,26},{10... | collective-permute-start | bytes 1572872 | tf_op jit(solution)/shard_map/ppermute | solution.py:442
  276.6 23.7 %collective-permute-start.29 = (bf16[128,2048]{1,0:T(8,128)(2,1)}, bf16[128,2048]{1,0:T(8,128)(2,1)S(1)}, u32[]{:S(2)}, u32[]{:S(2)}) collective-permute-start(bf16[128,2048]{1,0:T(8,128)(2,1)} %get-tuple-element.88), channel_id=1, source_target_pairs={{0,16},{8,24},{16,0},{24,8},{1,17},{9,25},{17,1},{25,9},{2,18},{10... | collective-permute-start | bytes 1572872 | tf_op jit(solution)/shard_map/ppermute | solution.py:442
  277.2 23.2 %collective-permute-start.28 = (bf16[128,2048]{1,0:T(8,128)(2,1)}, bf16[128,2048]{1,0:T(8,128)(2,1)S(1)}, u32[]{:S(2)}, u32[]{:S(2)}) collective-permute-start(bf16[128,2048]{1,0:T(8,128)(2,1)} %get-tuple-element.87), channel_id=1, source_target_pairs={{0,8},{8,0},{16,24},{24,16},{1,9},{9,1},{17,25},{25,17},{2,10},{10... | collective-permute-start | bytes 1572872 | tf_op jit(solution)/shard_map/ppermute | solution.py:442
  303.7 14.9 %collective-permute-start.31 = (bf16[128,2048]{1,0:T(8,128)(2,1)S(1)}, bf16[128,2048]{1,0:T(8,128)(2,1)S(1)}, u32[]{:S(2)}, u32[]{:S(2)}) collective-permute-start(bf16[128,2048]{1,0:T(8,128)(2,1)S(1)} %get-tuple-element.120.refs_1_.refs_3_), channel_id=1, source_target_pairs={{0,8},{8,0},{16,24},{24,16},{1,9},{9,1},{17,25},{25,17},{2,10},{10... | collective-permute-start | bytes 1572872 | tf_op jit(solution)/shard_map/ppermute | solution.py:442
  305.3 24.8 %collective-permute-start.32 = (bf16[128,2048]{1,0:T(8,128)(2,1)S(1)}, bf16[128,2048]{1,0:T(8,128)(2,1)S(1)}, u32[]{:S(2)}, u32[]{:S(2)}) collective-permute-start(bf16[128,2048]{1,0:T(8,128)(2,1)S(1)} %get-tuple-element.120.refs_1_.refs_3_), channel_id=1, source_target_pairs={{0,16},{8,24},{16,0},{24,8},{1,17},{9,25},{17,1},{25,9},{2,18},{10... | collective-permute-start | bytes 1572872 | tf_op jit(solution)/shard_map/ppermute | solution.py:442
  306.0 24.1 %collective-permute-start.33 = (bf16[128,2048]{1,0:T(8,128)(2,1)S(1)}, bf16[128,2048]{1,0:T(8,128)(2,1)}, u32[]{:S(2)}, u32[]{:S(2)}) collective-permute-start(bf16[128,2048]{1,0:T(8,128)(2,1)S(1)} %get-tuple-element.120.refs_1_.refs_3_), channel_id=1, source_target_pairs={{0,24},{8,16},{16,8},{24,0},{1,25},{9,17},{17,9},{25,1},{2,26},{10... | collective-permute-start | bytes 1572872 | tf_op jit(solution)/shard_map/ppermute | solution.py:442
  383.6 10.7 %collective-permute-start.50 = (bf16[4,128,256]{2,1,0:T(8,128)(2,1)S(1)}, bf16[4,128,256]{2,1,0:T(8,128)(2,1)S(1)}, u32[]{:S(2)}, u32[]{:S(2)}) collective-permute-start(bf16[4,128,256]{2,1,0:T(8,128)(2,1)S(1)} %bitcast.86), channel_id=1, source_target_pairs={{0,16},{8,24},{16,0},{24,8},{1,17},{9,25},{17,1},{25,9},{2,18},{10... | collective-permute-start | bytes 786440 | tf_op jit(solution)/shard_map/ppermute | solution.py:442
  384.7 9.6 %collective-permute-start.51 = (bf16[4,128,256]{2,1,0:T(8,128)(2,1)S(1)}, bf16[4,128,256]{2,1,0:T(8,128)(2,1)S(1)}, u32[]{:S(2)}, u32[]{:S(2)}) collective-permute-start(bf16[4,128,256]{2,1,0:T(8,128)(2,1)S(1)} %bitcast.87), channel_id=1, source_target_pairs={{0,24},{8,16},{16,8},{24,0},{1,25},{9,17},{17,9},{25,1},{2,26},{10... | collective-permute-start | bytes 786440 | tf_op jit(solution)/shard_map/ppermute | solution.py:442
  403.3 114.8 %reduce-scatter.11.cloned.1.call-start = ((), (), s32[]{:S(2)}) async-start(), calls=%async_computation.10 | async-start | bytes 3538944 | tf_op jit(solution)/shard_map/reduce_scatter | solution.py:500
  408.9 131.1 %reduce-scatter.7.cloned.1.call-start = ((), (), s32[]{:S(2)}) async-start(), calls=%async_computation.8 | async-start | bytes 5898240 | tf_op jit(solution)/shard_map/reduce_scatter | solution.py:500
  409.9 14.8 %collective-permute-start.52 = (bf16[512,512]{1,0:T(8,128)(2,1)S(1)}, bf16[512,512]{1,0:T(8,128)(2,1)S(1)}, u32[]{:S(2)}, u32[]{:S(2)}) collective-permute-start(bf16[512,512]{1,0:T(8,128)(2,1)S(1)} %copy-done.14), channel_id=1, source_target_pairs={{0,8},{8,0},{16,24},{24,16},{1,9},{9,1},{17,25},{25,17},{2,10},{10... | collective-permute-start | bytes 1572872 | tf_op jit(solution)/shard_map/ppermute | solution.py:442
  411.2 20.8 %collective-permute-start.53 = (bf16[512,512]{1,0:T(8,128)(2,1)S(1)}, bf16[512,512]{1,0:T(8,128)(2,1)S(1)}, u32[]{:S(2)}, u32[]{:S(2)}) collective-permute-start(bf16[512,512]{1,0:T(8,128)(2,1)S(1)} %copy-done.14), channel_id=1, source_target_pairs={{0,16},{8,24},{16,0},{24,8},{1,17},{9,25},{17,1},{25,9},{2,18},{10... | collective-permute-start | bytes 1572872 | tf_op jit(solution)/shard_map/ppermute | solution.py:442
  412.0 20.0 %collective-permute-start.54 = (bf16[512,512]{1,0:T(8,128)(2,1)S(1)}, bf16[512,512]{1,0:T(8,128)(2,1)}, u32[]{:S(2)}, u32[]{:S(2)}) collective-permute-start(bf16[512,512]{1,0:T(8,128)(2,1)S(1)} %copy-done.14), channel_id=1, source_target_pairs={{0,24},{8,16},{16,8},{24,0},{1,25},{9,17},{17,9},{25,1},{2,26},{10... | collective-permute-start | bytes 1572872 | tf_op jit(solution)/shard_map/ppermute | solution.py:442
  446.8 15.0 %collective-permute-start.25 = (bf16[128,2048]{1,0:T(8,128)(2,1)}, bf16[128,2048]{1,0:T(8,128)(2,1)S(1)}, u32[]{:S(2)}, u32[]{:S(2)}) collective-permute-start(bf16[128,2048]{1,0:T(8,128)(2,1)} %get-tuple-element.80), channel_id=1, source_target_pairs={{0,8},{8,0},{16,24},{24,16},{1,9},{9,1},{17,25},{25,17},{2,10},{10... | collective-permute-start | bytes 1572872 | tf_op jit(solution)/shard_map/ppermute | solution.py:442
  447.0 24.0 %collective-permute-start.26 = (bf16[128,2048]{1,0:T(8,128)(2,1)}, bf16[128,2048]{1,0:T(8,128)(2,1)S(1)}, u32[]{:S(2)}, u32[]{:S(2)}) collective-permute-start(bf16[128,2048]{1,0:T(8,128)(2,1)} %get-tuple-element.81), channel_id=1, source_target_pairs={{0,16},{8,24},{16,0},{24,8},{1,17},{9,25},{17,1},{25,9},{2,18},{10... | collective-permute-start | bytes 1572872 | tf_op jit(solution)/shard_map/ppermute | solution.py:442
  447.9 24.8 %collective-permute-start.27 = (bf16[128,2048]{1,0:T(8,128)(2,1)}, bf16[128,2048]{1,0:T(8,128)(2,1)S(1)}, u32[]{:S(2)}, u32[]{:S(2)}) collective-permute-start(bf16[128,2048]{1,0:T(8,128)(2,1)} %get-tuple-element.82), channel_id=1, source_target_pairs={{0,24},{8,16},{16,8},{24,0},{1,25},{9,17},{17,9},{25,1},{2,26},{10... | collective-permute-start | bytes 1572872 | tf_op jit(solution)/shard_map/ppermute | solution.py:442
  450.3 93.9 %collective-permute-start.62 = (bf16[256,2560]{1,0:T(8,128)(2,1)}, bf16[256,2560]{1,0:T(8,128)(2,1)}, u32[]{:S(2)}, u32[]{:S(2)}) collective-permute-start(bf16[256,2560]{1,0:T(8,128)(2,1)} %reduce-scatter.9.cloned.1.call-done.refs_0_), channel_id=1, source_target_pairs={{0,8},{8,0},{16,24},{24,16},{1,9},{9,1},{17,25},{25,17},{2,10},{10... | collective-permute-start | bytes 3932168 | tf_op jit(solution)/shard_map/ppermute | solution.py:442
  450.5 95.2 %collective-permute-start.63 = (bf16[256,2560]{1,0:T(8,128)(2,1)}, bf16[256,2560]{1,0:T(8,128)(2,1)}, u32[]{:S(2)}, u32[]{:S(2)}) collective-permute-start(bf16[256,2560]{1,0:T(8,128)(2,1)} %reduce-scatter.9.cloned.1.call-done.refs_0_), channel_id=1, source_target_pairs={{0,16},{8,24},{16,0},{24,8},{1,17},{9,25},{17,1},{25,9},{2,18},{10... | collective-permute-start | bytes 3932168 | tf_op jit(solution)/shard_map/ppermute | solution.py:442
  462.6 49.4 %collective-permute-start.42 = (bf16[128,2048]{1,0:T(8,128)(2,1)S(1)}, bf16[128,2048]{1,0:T(8,128)(2,1)S(1)}, u32[]{:S(2)}, u32[]{:S(2)}) collective-permute-start(bf16[128,2048]{1,0:T(8,128)(2,1)S(1)} %get-tuple-element.133), channel_id=1, source_target_pairs={{0,24},{8,16},{16,8},{24,0},{1,25},{9,17},{17,9},{25,1},{2,26},{10... | collective-permute-start | bytes 1572872 | tf_op jit(solution)/shard_map/ppermute | solution.py:442
  471.8 46.4 %collective-permute-start.41 = (bf16[128,2048]{1,0:T(8,128)(2,1)}, bf16[128,2048]{1,0:T(8,128)(2,1)S(1)}, u32[]{:S(2)}, u32[]{:S(2)}) collective-permute-start(bf16[128,2048]{1,0:T(8,128)(2,1)} %get-tuple-element.134), channel_id=1, source_target_pairs={{0,16},{8,24},{16,0},{24,8},{1,17},{9,25},{17,1},{25,9},{2,18},{10... | collective-permute-start | bytes 1572872 | tf_op jit(solution)/shard_map/ppermute | solution.py:442
  473.5 46.4 %collective-permute-start.40 = (bf16[128,2048]{1,0:T(8,128)(2,1)}, bf16[128,2048]{1,0:T(8,128)(2,1)S(1)}, u32[]{:S(2)}, u32[]{:S(2)}) collective-permute-start(bf16[128,2048]{1,0:T(8,128)(2,1)} %get-tuple-element.132), channel_id=1, source_target_pairs={{0,8},{8,0},{16,24},{24,16},{1,9},{9,1},{17,25},{25,17},{2,10},{10... | collective-permute-start | bytes 1572872 | tf_op jit(solution)/shard_map/ppermute | solution.py:442
  512.0 29.5 %collective-permute-start.59 = (bf16[256,512]{1,0:T(8,128)(2,1)}, bf16[256,512]{1,0:T(8,128)(2,1)}, u32[]{:S(2)}, u32[]{:S(2)}) collective-permute-start(bf16[256,512]{1,0:T(8,128)(2,1)} %reduce-scatter.5.cloned.1.call-done.refs_0_), channel_id=1, source_target_pairs={{0,8},{8,0},{16,24},{24,16},{1,9},{9,1},{17,25},{25,17},{2,10},{10... | collective-permute-start | bytes 786440 | tf_op jit(solution)/shard_map/ppermute | solution.py:442
  518.2 25.5 %collective-permute-start.67 = (bf16[256,704]{1,0:T(8,128)(2,1)}, bf16[256,704]{1,0:T(8,128)(2,1)S(1)}, u32[]{:S(2)}, u32[]{:S(2)}) collective-permute-start(bf16[256,704]{1,0:T(8,128)(2,1)} %reduce-scatter.11.cloned.1.call-done.refs_0_), channel_id=1, source_target_pairs={{0,16},{8,24},{16,0},{24,8},{1,17},{9,25},{17,1},{25,9},{2,18},{10... | collective-permute-start | bytes 1081352 | tf_op jit(solution)/shard_map/ppermute | solution.py:442
  540.1 17.8 %collective-permute-start.55 = (bf16[256,1280]{1,0:T(8,128)(2,1)}, bf16[256,1280]{1,0:T(8,128)(2,1)S(1)}, u32[]{:S(2)}, u32[]{:S(2)}) collective-permute-start(bf16[256,1280]{1,0:T(8,128)(2,1)} %reduce-scatter.7.cloned.1.call-done.refs_0_), channel_id=1, source_target_pairs={{0,8},{8,0},{16,24},{24,16},{1,9},{9,1},{17,25},{25,17},{2,10},{10... | collective-permute-start | bytes 1966088 | tf_op jit(solution)/shard_map/ppermute | solution.py:442
  541.5 23.4 %collective-permute-start.56 = (bf16[256,1280]{1,0:T(8,128)(2,1)}, bf16[256,1280]{1,0:T(8,128)(2,1)S(1)}, u32[]{:S(2)}, u32[]{:S(2)}) collective-permute-start(bf16[256,1280]{1,0:T(8,128)(2,1)} %reduce-scatter.7.cloned.1.call-done.refs_0_), channel_id=1, source_target_pairs={{0,16},{8,24},{16,0},{24,8},{1,17},{9,25},{17,1},{25,9},{2,18},{10... | collective-permute-start | bytes 1966088 | tf_op jit(solution)/shard_map/ppermute | solution.py:442
  543.7 26.9 %collective-permute-start.60 = (bf16[256,512]{1,0:T(8,128)(2,1)}, bf16[256,512]{1,0:T(8,128)(2,1)S(1)}, u32[]{:S(2)}, u32[]{:S(2)}) collective-permute-start(bf16[256,512]{1,0:T(8,128)(2,1)} %reduce-scatter.5.cloned.1.call-done.refs_0_), channel_id=1, source_target_pairs={{0,16},{8,24},{16,0},{24,8},{1,17},{9,25},{17,1},{25,9},{2,18},{10... | collective-permute-start | bytes 786440 | tf_op jit(solution)/shard_map/ppermute | solution.py:442
  544.2 26.9 %collective-permute-start.61 = (bf16[256,512]{1,0:T(8,128)(2,1)}, bf16[256,512]{1,0:T(8,128)(2,1)S(1)}, u32[]{:S(2)}, u32[]{:S(2)}) collective-permute-start(bf16[256,512]{1,0:T(8,128)(2,1)} %reduce-scatter.5.cloned.1.call-done.refs_0_), channel_id=1, source_target_pairs={{0,24},{8,16},{16,8},{24,0},{1,25},{9,17},{17,9},{25,1},{2,26},{10... | collective-permute-start | bytes 786440 | tf_op jit(solution)/shard_map/ppermute | solution.py:442
  545.7 26.9 %collective-permute-start.66 = (bf16[256,704]{1,0:T(8,128)(2,1)}, bf16[256,704]{1,0:T(8,128)(2,1)}, u32[]{:S(2)}, u32[]{:S(2)}) collective-permute-start(bf16[256,704]{1,0:T(8,128)(2,1)} %reduce-scatter.11.cloned.1.call-done.refs_0_), channel_id=1, source_target_pairs={{0,8},{8,0},{16,24},{24,16},{1,9},{9,1},{17,25},{25,17},{2,10},{10... | collective-permute-start | bytes 1081352 | tf_op jit(solution)/shard_map/ppermute | solution.py:442
  557.9 48.8 %collective-permute-start.64 = (bf16[128,2560]{1,0:T(8,128)(2,1)S(1)}, bf16[128,2560]{1,0:T(8,128)(2,1)}, u32[]{:S(2)}, u32[]{:S(2)}) collective-permute-start(bf16[128,2560]{1,0:T(8,128)(2,1)S(1)} %slice.284), channel_id=1, source_target_pairs={{0,8},{8,0},{16,24},{24,16},{1,9},{9,1},{17,25},{25,17},{2,10},{10... | collective-permute-start | bytes 1966088 | tf_op jit(solution)/shard_map/ppermute | solution.py:442
  565.0 41.7 %collective-permute-start.65 = (bf16[128,2560]{1,0:T(8,128)(2,1)S(1)}, bf16[128,2560]{1,0:T(8,128)(2,1)}, u32[]{:S(2)}, u32[]{:S(2)}) collective-permute-start(bf16[128,2560]{1,0:T(8,128)(2,1)S(1)} %slice.285), channel_id=1, source_target_pairs={{0,16},{8,24},{16,0},{24,8},{1,17},{9,25},{17,1},{25,9},{2,18},{10... | collective-permute-start | bytes 1966088 | tf_op jit(solution)/shard_map/ppermute | solution.py:442
  570.6 19.6 %collective-permute-start.68 = (bf16[128,704]{1,0:T(8,128)(2,1)S(1)}, bf16[128,704]{1,0:T(8,128)(2,1)S(1)}, u32[]{:S(2)}, u32[]{:S(2)}) collective-permute-start(bf16[128,704]{1,0:T(8,128)(2,1)S(1)} %slice.286), channel_id=1, source_target_pairs={{0,8},{8,0},{16,24},{24,16},{1,9},{9,1},{17,25},{25,17},{2,10},{10... | collective-permute-start | bytes 540680 | tf_op jit(solution)/shard_map/ppermute | solution.py:442
  571.2 28.9 %collective-permute-start.57 = (bf16[128,1280]{1,0:T(8,128)(2,1)S(1)}, bf16[128,1280]{1,0:T(8,128)(2,1)S(1)}, u32[]{:S(2)}, u32[]{:S(2)}) collective-permute-start(bf16[128,1280]{1,0:T(8,128)(2,1)S(1)} %slice.280), channel_id=1, source_target_pairs={{0,8},{8,0},{16,24},{24,16},{1,9},{9,1},{17,25},{25,17},{2,10},{10... | collective-permute-start | bytes 983048 | tf_op jit(solution)/shard_map/ppermute | solution.py:442
  572.6 27.5 %collective-permute-start.58 = (bf16[128,1280]{1,0:T(8,128)(2,1)S(1)}, bf16[128,1280]{1,0:T(8,128)(2,1)S(1)}, u32[]{:S(2)}, u32[]{:S(2)}) collective-permute-start(bf16[128,1280]{1,0:T(8,128)(2,1)S(1)} %slice.281), channel_id=1, source_target_pairs={{0,16},{8,24},{16,0},{24,8},{1,17},{9,25},{17,1},{25,9},{2,18},{10... | collective-permute-start | bytes 983048 | tf_op jit(solution)/shard_map/ppermute | solution.py:442
  (70 other events, 1073.9 us)
Sparse Core Ops, SparseCore 0:
  13.9 89.3 all-gather.3
  105.5 84.7 all-gather.5
  192.0 45.3 all-gather.7
  259.5 108.1 reduce-scatter.8
  403.5 33.3 reduce-scatter.4
  439.6 38.8 reduce-scatter.10
  480.8 59.2 reduce-scatter.6

commit v4 on v3

--- a/solution.py
+++ b/solution.py
@@ -43,14 +43,6 @@
 def silu_parts(pre_act):
     sigmoid_val = jax.nn.sigmoid(pre_act)
     return (pre_act * sigmoid_val, sigmoid_val * (1.0 + pre_act * (1.0 - sigmoid_val)))
-
-
-def fold(values, rows):
-    n, c = values.shape
-    f = rows // n
-    if f <= 1:
-        return values
-    return values.reshape(n, f, c // f).transpose(1, 0, 2).reshape(rows, c // f)
 
 
 def unfold(values, rows):
@@ -304,17 +296,27 @@
     refs[-1][...] = total.astype(BF)
 
 
-def ffn_weight_kernel(SR, FR, n2_ref, geg_ref, rows_in_ref, e_geg_ref, rows_geo_ref, e_hid_ref, out_ref):
-    cut = 2 * SR + 2 * FR
+def ffn_weight_kernel(
+    SR, FR, n2_ref, geg_ref, rows_in_ref, e_geg_ref, rows_geo_ref, e_hid_ref, *refs
+):
+    out_ref, cut = refs[-1], 2 * SR + 2 * FR
     out_ref[:, : 2 * SR] = t_dot(n2_ref[...], geg_ref[...]).astype(BF)
     out_ref[:, 2 * SR : cut] = t_dot(rows_in_ref[...], e_geg_ref[...]).astype(BF)
     out_ref[:, cut : cut + FR] = t_dot(rows_geo_ref[...], e_hid_ref[...]).astype(BF)
-    if out_ref.shape[1] > cut + FR:
-        out_ref[:, cut + FR :] = jnp.zeros((CHUNK, out_ref.shape[1] - cut - FR), BF)
-
-
-def product_kernel(left_ref, right_ref, out_ref):
-    out_ref[...] = t_dot(left_ref[...], right_ref[...]).astype(BF)
+    cut = cut + FR
+    for more_ref in refs[:-1]:
+        out_ref[:, cut : cut + more_ref.shape[1]] = more_ref[...]
+        cut = cut + more_ref.shape[1]
+    if out_ref.shape[1] > cut:
+        out_ref[:, cut:] = jnp.zeros((CHUNK, out_ref.shape[1] - cut), BF)
+
+
+def product_kernel(left_ref, right_ref, *out_refs):
+    part = t_dot(left_ref[...], right_ref[...]).astype(BF)
+    cut = 0
+    for ref in out_refs:
+        ref[...] = part[:, cut : cut + ref.shape[1]]
+        cut = cut + ref.shape[1]
 
 
 def attention_weight_kernel(R, QW, r_ref, n1_ref, gq_ref, *refs):
@@ -362,8 +364,38 @@
     return pl.BlockSpec(shape, lambda *_: (0,) * len(shape))
 
 
-def join_ffn_kernel(R, SR, FR, blocks, gate_ref, up_ref, e_gate_ref, e_up_ref, e_down_ref):
-    cut = 2 * SR
+def attention_columns_kernel(
+    HR, HS, CH, r_ref, query_ref, down_ref, router_ref, up_ref, out_w_ref, out_ref
+):
+    HN, W, half = HR * DN, DN + DR, DR // 2
+    for h in range(HR):
+        one, two = HN + h * half, HN + 128 + h * half
+        out_ref[:, h * DN : (h + 1) * DN] = query_ref[:, h * W : h * W + DN]
+        out_ref[:, one : one + half] = query_ref[:, h * W + DN : h * W + DN + half]
+        out_ref[:, two : two + half] = query_ref[:, h * W + DN + half : (h + 1) * W]
+    rows, cut = out_ref.shape[0], HN + 256
+    if HR * half < 128:
+        pad = jnp.zeros((rows, 128 - HR * half), BF)
+        out_ref[:, HN + HR * half : HN + 128] = pad
+        out_ref[:, HN + 128 + HR * half : cut] = pad
+    for ref in (down_ref, router_ref):
+        out_ref[:, cut : cut + ref.shape[0]] = ref[...].T
+        cut = cut + ref.shape[0]
+    if CH > cut:
+        out_ref[:, cut:CH] = jnp.zeros((rows, CH - cut), BF)
+    cut = CH + out_w_ref.shape[1]
+    out_ref[:, CH:cut] = out_w_ref[...]
+    width, n = out_ref.shape[1] - cut, up_ref.shape[0]
+    for f in range((DN + DV) // width):
+        for h in range(HS):
+            at, first = (f * HS + h) * n, h * (DN + DV) + f * width
+            out_ref[at : at + n, cut:] = up_ref[:, first : first + width]
+
+
+def join_ffn_kernel(
+    R, SR, FR, blocks, downs, gate_ref, up_ref, e_gate_ref, e_up_ref, e_down_ref, down_ref
+):
+    cut, width = 2 * SR, downs.shape[2]
     for j in range(R):
         gate_ref[:, j * SR : (j + 1) * SR] = blocks[j, :, :SR].astype(F32)
         up_ref[:, j * SR : (j + 1) * SR] = blocks[j, :, SR:cut].astype(F32)
@@ -371,11 +403,10 @@
         e_up_ref[:, j * FR : (j + 1) * FR] = blocks[j, :, cut + FR : cut + 2 * FR].astype(F32)
         e_down = blocks[j, :, cut + 2 * FR : cut + 3 * FR].astype(F32)
         e_down_ref[j * FR : (j + 1) * FR, :] = e_down.T
-
-
-def join_down_kernel(R, SR, blocks, down_ref):
-    for j in range(R):
-        down_ref[j * SR : (j + 1) * SR, :] = blocks[j].astype(F32).T
+        down_ref[j * SR : j * SR + width, :] = downs[j].astype(F32).T
+        if width < SR:
+            more = blocks[j, :, cut + 3 * FR : cut + 3 * FR + SR - width].astype(F32)
+            down_ref[j * SR + width : (j + 1) * SR, :] = more.T
 
 
 def join_attention_kernel(R, HR, blocks, query_ref, out_ref):
@@ -402,23 +433,23 @@
         router_ref[j * NR : (j + 1) * NR, :] = blocks[j, :, W + LR : W + LR + NR].astype(F32).T
 
 
-def join_blocks(kernel, R, r, pieces, outs):
-    rows, width = pieces[0][2].shape
+def join_blocks(kernel, R, r, groups, outs):
+    pieces = [(n, *piece) for n, group in enumerate(groups) for piece in group]
 
     def body(r_ref, *refs):
-        block_ref = refs[-1]
-        for (k, row, values), ref in zip(pieces, refs):
-            block_ref[r_ref[0] ^ k, row : row + values.shape[0], :] = ref[...]
-        kernel(block_ref, *refs[len(pieces) : -1])
+        block_refs = refs[-len(groups) :]
+        for (n, k, row, values), ref in zip(pieces, refs):
+            block_refs[n][r_ref[0] ^ k, row : row + values.shape[0], :] = ref[...]
+        kernel(*block_refs, *refs[len(pieces) : -len(groups)])
 
     return pl.pallas_call(
         body,
         in_specs=[pl.BlockSpec(memory_space=pltpu.SMEM)]
-        + [whole_block(values.shape) for _, _, values in pieces],
+        + [whole_block(piece[3].shape) for piece in pieces],
         out_specs=[whole_block(s) for s in outs],
         out_shape=[jax.ShapeDtypeStruct(s, F32) for s in outs],
-        scratch_shapes=[pltpu.VMEM((R, rows, width), BF)],
-    )(r.reshape(1), *[values for _, _, values in pieces])
+        scratch_shapes=[pltpu.VMEM((R,) + group[0][2].shape, BF) for group in groups],
+    )(r.reshape(1), *[piece[3] for piece in pieces])
 
 
 def make_local(R, S):
@@ -434,7 +465,6 @@
     T = R * TOK
     QW = HR * DN + 256
     half = DR // 2
-    HL = HR * half
     GR = DL // 64
     links = [[(i, i ^ k) for i in range(R)] for k in range(R)]
 
@@ -517,9 +547,6 @@
         CD, CR, CG = QW, QW + KVR + DR, QW + KVR + DR + NE
         CH = -(-CG // 128) * 128
         KW = HS * KR * (DN + DV) // DL
-        kv_piece = (
-            part(kv_up, KR, 0).reshape(KR, HS, DN + DV).transpose(1, 0, 2).reshape(HS * KR, DN + DV)
-        )
 
         def gain_rows(one, two, kv):
             lead = one.shape[:-1]
@@ -534,21 +561,23 @@
             )
             return jnp.pad(rows, pads + [(0, DL - 2 * GR - 1), (0, 0)])
 
-        q_own = part(query_weight, HR * (DN + DR)).reshape(DL, HR, DN + DR)
-        rope_pad = ((0, 0), (0, 128 - HL))
-        attn_own = jnp.concatenate(
-            [
-                q_own[..., :DN].reshape(DL, HR * DN),
-                jnp.pad(q_own[..., DN : DN + half].reshape(DL, HL), rope_pad),
-                jnp.pad(q_own[..., DN + half :].reshape(DL, HL), rope_pad),
-                kv_down,
-                router_weight,
-                *([jnp.zeros((DL, CH - CG), BF)] if CH > CG else []),
-                part(out_weight, DC),
-                fold(kv_piece, DL),
-            ],
-            axis=1,
-        )
+        r_one = r.reshape(1)
+        attn_own = pl.pallas_call(
+            lambda *refs: attention_columns_kernel(HR, HS, CH, *refs),
+            grid_spec=pltpu.PrefetchScalarGridSpec(
+                num_scalar_prefetch=1,
+                grid=(1,),
+                in_specs=[
+                    pl.BlockSpec((DL, HR * (DN + DR)), lambda i, r_ref: (0, r_ref[0])),
+                    whole_block((KVR + DR, DL)),
+                    whole_block((NE, DL)),
+                    pl.BlockSpec((KR, HS * (DN + DV)), lambda i, r_ref: (r_ref[0], 0)),
+                    pl.BlockSpec((DL, DC), lambda i, r_ref: (0, r_ref[0])),
+                ],
+                out_specs=whole_block((DL, CH + DC + KW)),
+            ),
+            out_shape=jax.ShapeDtypeStruct((DL, CH + DC + KW), BF),
+        )(r_one, query_weight, kv_down.T, router_weight.T, kv_up, out_weight)
         attn_all = shard_gather(attn_own)
         head_blocks = []
         for k in range(R):
@@ -563,7 +592,6 @@
             kvus = [unfold_all(b[:, DC:], S // R, DL, HS * KR) for b in head_nat]
             kvu_spec = whole_block((HR * KR, DN + DV))
         out_w_spec = pl.BlockSpec((HR * DV, DC), lambda i, r_ref: (0, 0))
-        r_one = r.reshape(1)
         w_q = attn_all[:, :QW]
         gain_own = jnp.concatenate([norm_gain, mixer_gain, kv_gain])
         shard = lax.axis_index(SHD)
@@ -579,6 +607,7 @@
         gain_kv = gain_all[:, 2 * DL :].reshape(KVR)
 
         EX = (SR + FR) % 128
+        IN = -(-(2 * SR + 2 * FR + EX) // 128) * 128
         down_t = jnp.concatenate([part(shared_down, SR, 0).T, part(expert_down[0], FR, 0).T], axis=1)
         in_all = shard_gather(
             jnp.concatenate(
@@ -588,6 +617,7 @@
                     part(expert_gate[0], FR),
                     part(expert_up[0], FR),
                     down_t[:, SR + FR - EX :],
+                    jnp.zeros((DL, IN - 2 * SR - 2 * FR - EX), BF),
                 ],
                 axis=1,
             ),
@@ -684,7 +714,7 @@
         def chunk_rows(width, column=0):
             return pl.BlockSpec((CHUNK, width), lambda i: (i, column))
 
-        w_in_spec, router_spec = chunk_rows(2 * SR + 2 * FR + EX), chunk_rows(128, CR // 128)
+        w_in_spec, router_spec = chunk_rows(IN), chunk_rows(128, CR // 128)
         more_spec = chunk_rows(128, (2 * SR + 2 * FR) // 128)
         (
             n2, rows_in, act, slope_up, s_hid, e_act, e_slope_up, e_hid, probs_r, rows_w, rows_geo
@@ -699,12 +729,15 @@
             [(T, 2 * SR), (RC, 2 * FR), (T, NE)],
         )
 
-        down_part = pl.pallas_call(
+        GW = -(-(2 * SR + 3 * FR) // 128) * 128
+        DX = SR % 128 if 2 * SR + 3 * FR + SR % 128 <= GW else 0
+        down_widths = [SR - DX] + [DX] * bool(DX)
+        down_part, *down_more = pl.pallas_call(
             product_kernel,
             grid=(STEPS,),
             in_specs=[columns(cot_all), whole_block((T, SR))],
-            out_specs=pl.BlockSpec((CHUNK, SR), lambda i: (i, 0)),
-            out_shape=jax.ShapeDtypeStruct((D, SR), BF),
+            out_specs=[pl.BlockSpec((CHUNK, w), lambda i: (i, 0)) for w in down_widths],
+            out_shape=[jax.ShapeDtypeStruct((D, w), BF) for w in down_widths],
         )(cot_all, s_hid)
         down_red = shard_reduce(down_part)
 
@@ -739,7 +772,6 @@
 
         gn2 = reduce_parts(gn2_parts)
 
-        GW = -(-(2 * SR + 3 * FR) // 128) * 128
         gu_part = pl.pallas_call(
             lambda *refs: ffn_weight_kernel(SR, FR, *refs),
             grid=(STEPS,),
@@ -750,10 +782,11 @@
                 whole_block(e_geg.shape),
                 columns(rows_geo),
                 whole_block(e_hid.shape),
-            ],
+            ]
+            + [chunk_rows(DX)] * len(down_more),
             out_specs=pl.BlockSpec((CHUNK, GW), lambda i: (i, 0)),
             out_shape=jax.ShapeDtypeStruct((D, GW), BF),
-        )(n2, s_geg, rows_in, e_geg, rows_geo, e_hid)
+        )(n2, s_geg, rows_in, e_geg, rows_geo, e_hid, *down_more)
         gu_red = shard_reduce(gu_part)
         operands = (s_hid, rest_all, spread, rows_w, rows_out)
         specs = {
@@ -899,21 +932,18 @@
             )
         tail_red = shard_reduce(tail_part)
 
-        (own_sd,) = join_blocks(
-            lambda *refs: join_down_kernel(R, SR, *refs), R, r, gather_pieces(down_red), [(SH, DL)]
-        )
-        own_sg, own_su, own_eg, own_eu, own_ed = join_blocks(
+        own_sg, own_su, own_eg, own_eu, own_ed, own_sd = join_blocks(
             lambda *refs: join_ffn_kernel(R, SR, FR, *refs),
             R,
             r,
-            gather_pieces(gu_red),
-            [(DL, SH), (DL, SH), (DL, FF), (DL, FF), (FF, DL)],
+            [gather_pieces(gu_red), gather_pieces(down_red)],
+            [(DL, SH), (DL, SH), (DL, FF), (DL, FF), (FF, DL), (SH, DL)],
         )
         own_qw, own_ow = join_blocks(
             lambda *refs: join_attention_kernel(R, HR, *refs),
             R,
             r,
-            gather_pieces(attn_red),
+            [gather_pieces(attn_red)],
             [(DL, H * (DN + DR)), (DL, D)],
         )
         tail_pieces = gather(tail_red)
@@ -923,7 +953,7 @@
                 lambda *refs: join_tail_kernel(R, HS, KR, LR, *refs),
                 R,
                 r,
-                [(k, 0, block) for k, block in enumerate(tail_pieces)],
+                [[(k, 0, block) for k, block in enumerate(tail_pieces)]],
                 [(KVR, HS * (DN + DV)), (KVR + DR, DL), (NE, DL)],
             )
             own_kd, own_rw = own_kd.T, own_rw.T

time: 628 us -> 580 us (0.924)
  waiting for transfers between devices: 296 us -> 259 us
  local copies, waits for them, and re-layouts: 52.5 us -> 42.5 us
    reduce_scatter x4, waiting for transfers between devices: 18 us -> 0.01 us  [shard_reduce(): return lax.psum_scatter(values, SHD, scatter_dimension=0, tiled=True)]
    ppermute x63, waiting for transfers between devices: 244 us -> 232 us  [send(): return lax.ppermute(values, REP, links[k])]
    unnamed x129 -> x93, local copies, waits for them, and re-layouts: 22.3 us -> 14.6 us
    all_gather x3, waiting for transfers between devices: 33.6 us -> 26.6 us  [shard_gather(): return lax.all_gather(values, SHD, axis=0, tiled=True)]
    pallas_call x4 -> x3, Pallas kernels: 19.5 us -> 17.3 us  [join_blocks(): pl.pallas_call(body, in_specs=[pl.BlockSpec(memory_space=pltpu.SMEM)] + [...]
  transfers between devices with their start and end apart: 77 -> 77, of which waited for: 36 -> 33; matrix products, arithmetic and copies ran while one was open for 13% -> 14% of each run, Pallas kernels for 15% -> 16%
where the time goes in v4:
time: 580 us; the launch traced here: 574 us
  waiting for transfers between devices  259 us (45%)
  Pallas kernels  125 us (22%)
  starting transfers between devices  85.6 us (15%)
  local copies, waits for them, and re-layouts  42.5 us (7%)
  other arithmetic  28.4 us (5%)
  matrix products  18.3 us (3%)
  between operations  15.3 us (3%)
    ppermute x63, waiting for transfers between devices, send(): return lax.ppermute(values, REP, links[k])  232 us
    ppermute x63, starting transfers between devices, send(): return lax.ppermute(values, REP, links[k])  75.6 us
    pallas_call x3, Pallas kernels, call(): pl.pallas_call(kernel, grid=(STEPS,), in_specs=[specs.get(n, whole_block(...  37.3 us
    all_gather x3, waiting for transfers between devices, shard_gather(): return lax.all_gather(values, SHD, axis=0, tiled=True)  26.6 us
    pallas_call x3, Pallas kernels, join_blocks(): pl.pallas_call(body, in_specs=[pl.BlockSpec(memory_space=pltpu.SMEM)] + [...  17.3 us
    unnamed x93, local copies, waits for them, and re-layouts  14.6 us
    pallas_call x1, Pallas kernels, local(): forward(r_one, qlat, qlat, lat_n, cosine, sine, bias, *out_ws, *kvus)  13.8 us
    pallas_call x1, Pallas kernels, local(): backward(r_one, *ghb, *out_ws, *kvus, att, probs, kv, q_b, kr_b, cosine,...  13.3 us
  transfers between devices with their start and end apart: 77, of which 33 were waited for; matrix products, arithmetic and copies ran while one was open for 14% of the time, Pallas kernels for 16%

profile of v4, /device:TPU:0, one launch (start us, length us, event | category | flops | bytes accessed | tf_op | source)
XLA Modules:
  0.0 574.1 jit_solution(5515224349357394241)
XLA Ops:
  7.3 2.8 shard_map.297
  14.3 2.2 concatenate.38
  21.2 2.6 collective-permute-start.4
  23.9 2.8 collective-permute-start.6
  30.2 3.6 collective-permute-start.8
  34.6 2.4 collective-permute-start.2
  41.6 8.3 %collective-permute-done.12 = bf16[8,128]{1,0:T(8,128)(2,1)S(1)} collective-permute-done((bf16[8,128]{1,0:T(8,128)(2,1)S(1)}, bf16[8,128]{1,0:T(8,128)(2,1)S(1)}, u32[]{:S(2)}, u32[]{:S(2)}) %collective-permute-start.12) | collective-permute-done | bytes 2080 | tf_op jit(solution)/shard_map/ppermute | solution.py:472
  51.4 9.8 %collective-permute-done.11 = bf16[8,128]{1,0:T(8,128)(2,1)S(1)} collective-permute-done((bf16[8,128]{1,0:T(8,128)(2,1)S(1)}, bf16[8,128]{1,0:T(8,128)(2,1)S(1)}, u32[]{:S(2)}, u32[]{:S(2)}) %collective-permute-start.11) | collective-permute-done | bytes 2080 | tf_op jit(solution)/shard_map/ppermute | solution.py:472
  65.6 2.3 multiply_sine_fusion
  67.8 2.0 fusion.2
  69.9 3.1 fusion.4.refs_1_
  73.0 26.6 %all-gather.4.cloned.1.call-done.refs_5_ = bf16[2048,2176]{1,0:T(8,128)(2,1)} async-done(((bf16[256,2176]{1,0:T(8,128)(2,1)}), bf16[2048,2176]{1,0:T(8,128)(2,1)}) %all-gather.4.cloned.1.call-update) | async-done | bytes 8912912 | tf_op jit(solution)/shard_map/all_gather | solution.py:527
  99.7 3.1 fusion.39
  106.3 6.0 %fusion.refs_1_.refs_2_ = f32[512,1408]{1,0:T(8,128)S(1)} fusion(bf16[512,2048]{1,0:T(8,128)(2,1)S(1)} %copy-done.5, bf16[2048,2176]{1,0:T(8,128)(2,1)} %all-gather.4.cloned.1.call-done.refs_5_), kind=kOutput, calls=%fused_computation.3 | convolution fusion | flops 2952790016 | bytes 10747904 | tf_op jit(solution)/shard_map/dot_general | solution.py:28
  114.8 8.4 %collective-permute-done.13.refs_8_.refs_12_.refs_6_.refs_10_ = bf16[512,768]{1,0:T(8,128)(2,1)S(1)} collective-permute-done((bf16[512,768]{1,0:T(8,128)(2,1)S(1)}, bf16[512,768]{1,0:T(8,128)(2,1)S(1)}, u32[]{:S(2)}, u32[]{:S(2)}) %collective-permute-start.13) | collective-permute-done | bytes 786464 | tf_op jit(solution)/shard_map/ppermute | solution.py:472
  123.2 17.4 %collective-permute-done.14.refs_9_.refs_13_.refs_7_.refs_11_ = bf16[512,768]{1,0:T(8,128)(2,1)} collective-permute-done((bf16[512,768]{1,0:T(8,128)(2,1)S(1)}, bf16[512,768]{1,0:T(8,128)(2,1)}, u32[]{:S(2)}, u32[]{:S(2)}) %collective-permute-start.14) | collective-permute-done | bytes 786464 | tf_op jit(solution)/shard_map/ppermute | solution.py:472
  140.7 13.8 %shard_map.298 = (bf16[512,512]{1,0:T(8,128)(2,1)}, f32[16,128,128]{2,1,0:T(8,128)}, bf16[512,768]{1,0:T(8,128)(2,1)}, bf16[512,256]{1,0:T(8,128)(2,1)}, bf16[51...) custom-call(s32[1]{0:T(128)} %bitcast.refs_0_.r_ref, ...), custom_call_target="tpu_custom_call" | custom-call | tf_op jit(solution)/shard_map/pallas_call | solution.py:676
  162.3 8.1 %collective-permute-done.18 = bf16[128,2048]{1,0:T(8,128)(2,1)S(1)} collective-permute-done((bf16[128,2048]{1,0:T(8,128)(2,1)}, bf16[128,2048]{1,0:T(8,128)(2,1)S(1)}, u32[]{:S(2)}, u32[]{:S(2)}) %collective-permute-start.18) | collective-permute-done | bytes 524320 | tf_op jit(solution)/shard_map/ppermute | solution.py:472
  170.4 11.1 %collective-permute-done.17 = bf16[128,2048]{1,0:T(8,128)(2,1)S(1)} collective-permute-done((bf16[128,2048]{1,0:T(8,128)(2,1)}, bf16[128,2048]{1,0:T(8,128)(2,1)S(1)}, u32[]{:S(2)}, u32[]{:S(2)}) %collective-permute-start.17) | collective-permute-done | bytes 524320 | tf_op jit(solution)/shard_map/ppermute | solution.py:472
  188.0 4.9 collective-permute-done.24
  194.4 9.9 %collective-permute-done.19.refs_1_ = bf16[128,2048]{1,0:T(8,128)(2,1)} collective-permute-done((bf16[128,2048]{1,0:T(8,128)(2,1)}, bf16[128,2048]{1,0:T(8,128)(2,1)}, u32[]{:S(2)}, u32[]{:S(2)}) %collective-permute-start.19) | collective-permute-done | bytes 524320 | tf_op jit(solution)/shard_map/ppermute | solution.py:472
  204.3 9.3 %collective-permute-done.21.refs_3_ = bf16[128,2048]{1,0:T(8,128)(2,1)} collective-permute-done((bf16[128,2048]{1,0:T(8,128)(2,1)}, bf16[128,2048]{1,0:T(8,128)(2,1)}, u32[]{:S(2)}, u32[]{:S(2)}) %collective-permute-start.21) | collective-permute-done | bytes 524320 | tf_op jit(solution)/shard_map/ppermute | solution.py:472
  214.4 14.8 %shard_map.299 = (bf16[512,2048]{1,0:T(8,128)(2,1)}, bf16[64,2048]{1,0:T(8,128)(2,1)}, f32[512,704]{1,0:T(8,128)}, f32[512,704]{1,0:T(8,128)}, bf16[512,704]{1,0...) custom-call(bf16[128,2048]{1,0:T(8,128)(2,1)} %multiply_convert_fusi, ...), custom_call_target="tpu_custom_call" | custom-call | tf_op jit(solution)/shard_map/pallas_call | solution.py:697
  229.2 5.4 shard_map.309
  234.7 12.9 %shard_map.300 = (bf16[512,1408]{1,0:T(8,128)(2,1)}, bf16[64,704]{1,0:T(8,128)(2,1)}, f32[64,2048]{1,0:T(8,128)}, f32[512,128]{1,0:T(8,128)}, bf16[512,64]{1,0:T(8,128)(2,1)}) custom-call(bf16[512,2048]{1,0:T(8,128)(2,1)} %copy-done.4, bf16[2048,1024]{1,0:T(8,128)(2,1)} %all-gather.8.cloned.1.call-done.refs_1_, ...), custom_call_target="tpu_custom_call" | custom-call | tf_op jit(solution)/shard_map/pallas_call | solution.py:697
  247.6 9.5 %shard_map.310 = bf16[2048,2560]{1,0:T(8,128)(2,1)} custom-call(bf16[512,2048]{1,0:T(8,128)(2,1)} %get-tuple-element.103.refs_2_.refs_0_, bf16[512,1408]{1,0:T(8,128)(2,1)} %get-tuple-element.86.refs_0_.refs_1_, bf16[64,2048]{1,0:T(8,128)(2,1)} %get-tuple-element.111.refs_2_, bf16[64,704]{1,0:T(8,128)(2,1)} %get-tuple-element.87.refs_1_.refs_3_, ...), custom_call_target="tpu_custom_call" | custom-call | tf_op jit(solution)/shard_map/pallas_call | solution.py:775
  257.8 9.6 %shard_map.303 = (bf16[128,2048]{1,0:T(8,128)(2,1)}, bf16[128,2048]{1,0:T(8,128)(2,1)}, bf16[128,2048]{1,0:T(8,128)(2,1)}, bf16[128,2048]{1,0:T(8,128)(2,1)}) custom-call(bf16[512,1408]{1,0:T(8,128)(2,1)} %get-tuple-element.86.refs_0_.refs_1_, bf16[64,704]{1,0:T(8,128)(2,1)} %get-tuple-element.87.refs_1_.refs_3_, bf16[512,64]{1,0:T(8,128)(2,1)} %get-tuple-element.88.refs_2_, ...), custom_call_target="tpu_custom_call" | custom-call | tf_op jit(solution)/shard_map/pallas_call | solution.py:697
  267.4 2.1 collective-permute-start.30
  270.9 12.5 %collective-permute-done.30 = bf16[128,2048]{1,0:T(8,128)(2,1)S(1)} collective-permute-done((bf16[128,2048]{1,0:T(8,128)(2,1)}, bf16[128,2048]{1,0:T(8,128)(2,1)S(1)}, u32[]{:S(2)}, u32[]{:S(2)}) %collective-permute-start.30) | collective-permute-done | bytes 524320 | tf_op jit(solution)/shard_map/ppermute | solution.py:472
  283.4 9.8 %collective-permute-done.29 = bf16[128,2048]{1,0:T(8,128)(2,1)S(1)} collective-permute-done((bf16[128,2048]{1,0:T(8,128)(2,1)}, bf16[128,2048]{1,0:T(8,128)(2,1)S(1)}, u32[]{:S(2)}, u32[]{:S(2)}) %collective-permute-start.29) | collective-permute-done | bytes 524320 | tf_op jit(solution)/shard_map/ppermute | solution.py:472
  295.1 1.7 fusion.36
  302.4 9.2 %collective-permute-done.31.refs_2_.refs_4_ = bf16[128,2048]{1,0:T(8,128)(2,1)S(1)} collective-permute-done((bf16[128,2048]{1,0:T(8,128)(2,1)S(1)}, bf16[128,2048]{1,0:T(8,128)(2,1)S(1)}, u32[]{:S(2)}, u32[]{:S(2)}) %collective-permute-start.31) | collective-permute-done | bytes 524320 | tf_op jit(solution)/shard_map/ppermute | solution.py:472
  313.2 11.1 %collective-permute-done.32.refs_3_.refs_5_ = bf16[128,2048]{1,0:T(8,128)(2,1)S(1)} collective-permute-done((bf16[128,2048]{1,0:T(8,128)(2,1)S(1)}, bf16[128,2048]{1,0:T(8,128)(2,1)S(1)}, u32[]{:S(2)}, u32[]{:S(2)}) %collective-permute-start.32) | collective-permute-done | bytes 524320 | tf_op jit(solution)/shard_map/ppermute | solution.py:472
  325.3 13.3 %shard_map.304 = (bf16[512,768]{1,0:T(8,128)(2,1)}, bf16[512,1024]{1,0:T(8,128)(2,1)}, bf16[128,640]{1,0:T(8,128)(2,1)}, bf16[128,640]{1,0:T(8,128)(2,1)}, bf16[...) custom-call(s32[1]{0:T(128)} %bitcast.refs_0_.r_ref, bf16[128,2048]{1,0:T(8,128)(2,1)} %copy-done.9, ...), custom_call_target="tpu_custom_call" | custom-call | tf_op jit(solution)/shard_map/pallas_call | solution.py:847
  338.6 7.0 %collective-permute-done.53.refs_9_ = bf16[512,512]{1,0:T(8,128)(2,1)} collective-permute-done((bf16[512,512]{1,0:T(8,128)(2,1)S(1)}, bf16[512,512]{1,0:T(8,128)(2,1)}, u32[]{:S(2)}, u32[]{:S(2)}) %collective-permute-start.53) | collective-permute-done | bytes 524320 | tf_op jit(solution)/shard_map/ppermute | solution.py:472
  345.7 7.9 %shard_map.306 = bf16[2048,1280]{1,0:T(8,128)(2,1)} custom-call(s32[1]{0:T(128)} %bitcast.refs_0_.r_ref, bf16[512,2048]{1,0:T(8,128)(2,1)} %fusion.4.refs_1_, bf16[512,768]{1,0:T(8,128)(2,1)} %get-tuple-element.98.refs_2_, bf16[128,2048]{1,0:T(8,128)(2,1)} %copy-done.9, bf16[128,2048]{1,0:T(8,128)(2,1)} %copy-done.13, bf16[128,2048]{1,0:T(8,128)(2,1)} %copy-done.14, ...), custom_call_target="tpu_custom_call" | custom-call | tf_op jit(solution)/shard_map/pallas_call | solution.py:850
  356.5 1.7 collective-permute-start.43
  362.0 1.8 collective-permute-start.35
  365.0 2.5 collective-permute-done.36
  375.3 1.7 convolution_convert_fusion
  377.0 1.7 copy.67
  380.6 2.4 fusion.18
  383.1 6.7 %fusion.6 = (f32[2048]{0:T(1024)S(1)}, bf16[512,2048]{1,0:T(8,128)(2,1)}, f32[512,2048]{1,0:T(8,128)}) fusion(f32[512]{0:T(512)S(1)} %add_rsqrt_fusion.1, bf16[128,2048]{1,0:T(8,128)(2,1)S(1)} %copy-done.18, bf16[128,2048]{1,0:T(8,128)(2,1)} %collective-permute-done.1, bf16[128,2048]{1,0:T(8,128)(2,1)} %collective-permute-done, ...), kind=kOutput, calls=%fused_computation.9 | convolution fusion | flops 1624242176 | bytes 16525312 | tf_op jit(solution)/shard_map/dot_general | solution.py:32
  394.3 1.8 copy.73
  402.8 4.1 collective-permute-done.50.refs_8_
  407.7 8.3 %shard_map.305 = bf16[2048,512]{1,0:T(8,128)(2,1)} custom-call(s32[1]{0:T(128)} %bitcast.refs_0_.r_ref, bf16[512,2048]{1,0:T(8,128)(2,1)} %fusion.4.refs_1_, bf16[512,2048]{1,0:T(8,128)(2,1)} %get-tuple-element.103.refs_2_.refs_0_, bf16[512,144]{1,0:T(8,128)(2,1)} %copy-done.10, bf16[512,16]{1,0:T(8,128)(2,1)} %fusion.24.refs_4_, ...), custom_call_target="tpu_custom_call" | custom-call | tf_op jit(solution)/shard_map/pallas_call | solution.py:904
  416.0 6.0 %shard_map.301 = (bf16[128,2048]{1,0:T(8,128)(2,1)}, bf16[128,2048]{1,0:T(8,128)(2,1)}, bf16[128,2048]{1,0:T(8,128)(2,1)}, bf16[128,2048]{1,0:T(8,128)(2,1)}) custom-call(bf16[512,704]{1,0:T(8,128)(2,1)} %get-tuple-element.72.refs_0_.right_ref, bf16[2048,1024]{1,0:T(8,128)(2,1)} %all-gather.8.cloned.1.call-done.refs_1_, ...), custom_call_target="tpu_custom_call" | custom-call | tf_op jit(solution)/shard_map/pallas_call | solution.py:796
  425.5 2.6 fusion.40
  430.3 6.8 %collective-permute-done.25.refs_1_ = bf16[128,2048]{1,0:T(8,128)(2,1)S(1)} collective-permute-done((bf16[128,2048]{1,0:T(8,128)(2,1)}, bf16[128,2048]{1,0:T(8,128)(2,1)S(1)}, u32[]{:S(2)}, u32[]{:S(2)}) %collective-permute-start.25) | collective-permute-done | bytes 524320 | tf_op jit(solution)/shard_map/ppermute | solution.py:472
  438.6 19.7 %collective-permute-done.26.refs_2_ = bf16[128,2048]{1,0:T(8,128)(2,1)} collective-permute-done((bf16[128,2048]{1,0:T(8,128)(2,1)}, bf16[128,2048]{1,0:T(8,128)(2,1)}, u32[]{:S(2)}, u32[]{:S(2)}) %collective-permute-start.26) | collective-permute-done | bytes 524320 | tf_op jit(solution)/shard_map/ppermute | solution.py:472
  461.8 8.5 %collective-permute-done.41 = bf16[128,2048]{1,0:T(8,128)(2,1)S(1)} collective-permute-done((bf16[128,2048]{1,0:T(8,128)(2,1)}, bf16[128,2048]{1,0:T(8,128)(2,1)S(1)}, u32[]{:S(2)}, u32[]{:S(2)}) %collective-permute-start.41) | collective-permute-done | bytes 524320 | tf_op jit(solution)/shard_map/ppermute | solution.py:472
  471.6 3.0 shard_map.302
  475.3 1.7 fusion.14
  477.0 25.8 %collective-permute-done.66.refs_6_ = bf16[256,640]{1,0:T(8,128)(2,1)S(1)} collective-permute-done((bf16[256,640]{1,0:T(8,128)(2,1)}, bf16[256,640]{1,0:T(8,128)(2,1)S(1)}, u32[]{:S(2)}, u32[]{:S(2)}) %collective-permute-start.66) | collective-permute-done | bytes 327712 | tf_op jit(solution)/shard_map/ppermute | solution.py:472
  503.5 10.5 %collective-permute-done.67.refs_7_ = bf16[256,640]{1,0:T(8,128)(2,1)} collective-permute-done((bf16[256,640]{1,0:T(8,128)(2,1)}, bf16[256,640]{1,0:T(8,128)(2,1)}, u32[]{:S(2)}, u32[]{:S(2)}) %collective-permute-start.67) | collective-permute-done | bytes 327712 | tf_op jit(solution)/shard_map/ppermute | solution.py:472
  514.0 2.9 collective-permute-start.59
  517.8 2.7 fusion.13
  525.6 2.0 collective-permute-start.57
  534.2 1.9 collective-permute-start.68
  536.2 4.6 collective-permute-done.57.refs_3_
  543.0 2.9 shard_map.308
  545.9 5.8 %collective-permute-done.58.refs_4_ = bf16[128,1280]{1,0:T(8,128)(2,1)} collective-permute-done((bf16[128,1280]{1,0:T(8,128)(2,1)S(1)}, bf16[128,1280]{1,0:T(8,128)(2,1)}, u32[]{:S(2)}, u32[]{:S(2)}) %collective-permute-start.58) | collective-permute-done | bytes 327712 | tf_op jit(solution)/shard_map/ppermute | solution.py:472
  551.7 5.2 shard_map.307
  557.8 9.2 %shard_map.311 = (f32[256,2816]{1,0:T(8,128)}, f32[256,2816]{1,0:T(8,128)}, f32[256,1408]{1,0:T(8,128)}, f32[256,1408]{1,0:T(8,128)}, f32[1408,256]{1,0:T(8,128)}, /*index=5*/f32[2816,256]{1,0:T(8,128)}) custom-call(s32[1]{0:T(128)} %bitcast.refs_0_.r_ref, bf16[256,2560]{1,0:T(8,128)(2,1)} %reduce-scatter.9.cloned.1.call-done.refs_0_, ...), custom_call_target="tpu_custom_call" | custom-call | tf_op jit(solution)/shard_map/pallas_call | solution.py:445
  (324 shorter events, 117.1 us)
Async XLA Ops:
  7.2 92.5 %all-gather.4.cloned.1.call-start = ((), (), s32[]{:S(2)}) async-start(), calls=%async_computation.4 | async-start | bytes 10027008 | tf_op jit(solution)/shard_map/all_gather | solution.py:527
  10.1 184.4 %all-gather.6.cloned.1.call-start = ((), (), s32[]{:S(2)}) async-start(), calls=%async_computation.5 | async-start | bytes 10027008 | tf_op jit(solution)/shard_map/all_gather | solution.py:527
  16.6 218.1 %all-gather.8.cloned.1.call-start = ((), (), s32[]{:S(2)}) async-start(), calls=%async_computation.6 | async-start | bytes 4718592 | tf_op jit(solution)/shard_map/all_gather | solution.py:527
  20.7 9.5 %collective-permute-start.3 = (bf16[576]{0:T(1024)(128)(2,1)}, bf16[576]{0:T(1024)(128)(2,1)S(1)}, u32[]{:S(2)}, u32[]{:S(2)}) collective-permute-start(bf16[576]{0:T(1024)(128)(2,1)} %dynamic-update-slice.6), channel_id=1, source_target_pairs={{0,1},{1,0},{2,3},{3,2},{4,5},{5,4},{6,7},{7,6},{8,9},{9,8},{10,11... | collective-permute-start | bytes 3464 | tf_op jit(solution)/shard_map/ppermute | solution.py:599
  21.2 12.6 %collective-permute-start.4 = (bf16[576]{0:T(1024)(128)(2,1)}, bf16[576]{0:T(1024)(128)(2,1)}, u32[]{:S(2)}, u32[]{:S(2)}) collective-permute-start(bf16[576]{0:T(1024)(128)(2,1)} %dynamic-update-slice.6), channel_id=1, source_target_pairs={{0,2},{1,3},{2,0},{3,1},{4,6},{5,7},{6,4},{7,5},{8,10},{9,11},{10,... | collective-permute-start | bytes 3464 | tf_op jit(solution)/shard_map/ppermute | solution.py:599
  23.7 10.9 %collective-permute-start.5 = (bf16[576]{0:T(1024)(128)(2,1)}, bf16[576]{0:T(1024)(128)(2,1)S(1)}, u32[]{:S(2)}, u32[]{:S(2)}) collective-permute-start(bf16[576]{0:T(1024)(128)(2,1)} %dynamic-update-slice.6), channel_id=1, source_target_pairs={{0,3},{1,2},{2,1},{3,0},{4,7},{5,6},{6,5},{7,4},{8,11},{9,10},{10,... | collective-permute-start | bytes 3464 | tf_op jit(solution)/shard_map/ppermute | solution.py:599
  23.9 13.1 %collective-permute-start.6 = (bf16[576]{0:T(1024)(128)(2,1)}, bf16[576]{0:T(1024)(128)(2,1)S(1)}, u32[]{:S(2)}, u32[]{:S(2)}) collective-permute-start(bf16[576]{0:T(1024)(128)(2,1)} %dynamic-update-slice.6), channel_id=1, source_target_pairs={{0,4},{1,5},{2,6},{3,7},{4,0},{5,1},{6,2},{7,3},{8,12},{9,13},{10,... | collective-permute-start | bytes 3464 | tf_op jit(solution)/shard_map/ppermute | solution.py:599
  26.6 11.0 %collective-permute-start.7 = (bf16[576]{0:T(1024)(128)(2,1)}, bf16[576]{0:T(1024)(128)(2,1)S(1)}, u32[]{:S(2)}, u32[]{:S(2)}) collective-permute-start(bf16[576]{0:T(1024)(128)(2,1)} %dynamic-update-slice.6), channel_id=1, source_target_pairs={{0,5},{1,4},{2,7},{3,6},{4,1},{5,0},{6,3},{7,2},{8,13},{9,12},{10,... | collective-permute-start | bytes 3464 | tf_op jit(solution)/shard_map/ppermute | solution.py:599
  27.8 430.5 %reduce-scatter.9.cloned.1.call-start = ((), (), s32[]{:S(2)}) async-start(), calls=%async_computation.9 | async-start | bytes 11796480 | tf_op jit(solution)/shard_map/reduce_scatter | solution.py:530
  30.2 9.0 %collective-permute-start.8 = (bf16[576]{0:T(1024)(128)(2,1)}, bf16[576]{0:T(1024)(128)(2,1)S(1)}, u32[]{:S(2)}, u32[]{:S(2)}) collective-permute-start(bf16[576]{0:T(1024)(128)(2,1)} %dynamic-update-slice.6), channel_id=1, source_target_pairs={{0,6},{1,7},{2,4},{3,5},{4,2},{5,3},{6,0},{7,1},{8,14},{9,15},{10,... | collective-permute-start | bytes 3464 | tf_op jit(solution)/shard_map/ppermute | solution.py:599
  34.6 33.2 %collective-permute-start.2 = (bf16[128,2048]{1,0:T(8,128)(2,1)}, bf16[128,2048]{1,0:T(8,128)(2,1)S(1)}, u32[]{:S(2)}, u32[]{:S(2)}) collective-permute-start(bf16[128,2048]{1,0:T(8,128)(2,1)} %param.18), channel_id=1, source_target_pairs={{0,24},{8,16},{16,8},{24,0},{1,25},{9,17},{17,9},{25,1},{2,26},{10... | collective-permute-start | bytes 1572872 | tf_op jit(solution)/shard_map/ppermute | solution.py:472
  37.0 30.8 %collective-permute-start.1 = (bf16[128,2048]{1,0:T(8,128)(2,1)}, bf16[128,2048]{1,0:T(8,128)(2,1)}, u32[]{:S(2)}, u32[]{:S(2)}) collective-permute-start(bf16[128,2048]{1,0:T(8,128)(2,1)} %param.18), channel_id=1, source_target_pairs={{0,16},{8,24},{16,0},{24,8},{1,17},{9,25},{17,1},{25,9},{2,18},{10... | collective-permute-start | bytes 1572872 | tf_op jit(solution)/shard_map/ppermute | solution.py:472
  37.6 12.2 %collective-permute-start.12 = (bf16[8,128]{1,0:T(8,128)(2,1)S(1)}, bf16[8,128]{1,0:T(8,128)(2,1)S(1)}, u32[]{:S(2)}, u32[]{:S(2)}) collective-permute-start(bf16[8,128]{1,0:T(8,128)(2,1)S(1)} %get-tuple-element.173), channel_id=1, source_target_pairs={{0,24},{8,16},{16,8},{24,0},{1,25},{9,17},{17,9},{25,1},{2,26},{10... | collective-permute-start | bytes 6152 | tf_op jit(solution)/shard_map/ppermute | solution.py:472
  39.2 21.9 %collective-permute-start.11 = (bf16[8,128]{1,0:T(8,128)(2,1)S(1)}, bf16[8,128]{1,0:T(8,128)(2,1)S(1)}, u32[]{:S(2)}, u32[]{:S(2)}) collective-permute-start(bf16[8,128]{1,0:T(8,128)(2,1)S(1)} %get-tuple-element.173), channel_id=1, source_target_pairs={{0,16},{8,24},{16,0},{24,8},{1,17},{9,25},{17,1},{25,9},{2,18},{10... | collective-permute-start | bytes 6152 | tf_op jit(solution)/shard_map/ppermute | solution.py:472
  39.8 22.9 %collective-permute-start.10 = (bf16[8,128]{1,0:T(8,128)(2,1)S(1)}, bf16[8,128]{1,0:T(8,128)(2,1)S(1)}, u32[]{:S(2)}, u32[]{:S(2)}) collective-permute-start(bf16[8,128]{1,0:T(8,128)(2,1)S(1)} %get-tuple-element.173), channel_id=1, source_target_pairs={{0,8},{8,0},{16,24},{24,16},{1,9},{9,1},{17,25},{25,17},{2,10},{10... | collective-permute-start | bytes 6152 | tf_op jit(solution)/shard_map/ppermute | solution.py:472
  49.9 18.0 %collective-permute-start = (bf16[128,2048]{1,0:T(8,128)(2,1)}, bf16[128,2048]{1,0:T(8,128)(2,1)}, u32[]{:S(2)}, u32[]{:S(2)}) collective-permute-start(bf16[128,2048]{1,0:T(8,128)(2,1)} %param.18), channel_id=1, source_target_pairs={{0,8},{8,0},{16,24},{24,16},{1,9},{9,1},{17,25},{25,17},{2,10},{10... | collective-permute-start | bytes 1572872 | tf_op jit(solution)/shard_map/ppermute | solution.py:472
  61.1 97.5 %collective-permute-start.22 = (bf16[128,2048]{1,0:T(8,128)(2,1)}, bf16[128,2048]{1,0:T(8,128)(2,1)}, u32[]{:S(2)}, u32[]{:S(2)}) collective-permute-start(bf16[128,2048]{1,0:T(8,128)(2,1)} %param.35), channel_id=1, source_target_pairs={{0,8},{8,0},{16,24},{24,16},{1,9},{9,1},{17,25},{25,17},{2,10},{10... | collective-permute-start | bytes 1572872 | tf_op jit(solution)/shard_map/ppermute | solution.py:472
  62.6 98.6 %collective-permute-start.23 = (bf16[128,2048]{1,0:T(8,128)(2,1)}, bf16[128,2048]{1,0:T(8,128)(2,1)}, u32[]{:S(2)}, u32[]{:S(2)}) collective-permute-start(bf16[128,2048]{1,0:T(8,128)(2,1)} %param.35), channel_id=1, source_target_pairs={{0,16},{8,24},{16,0},{24,8},{1,17},{9,25},{17,1},{25,9},{2,18},{10... | collective-permute-start | bytes 1572872 | tf_op jit(solution)/shard_map/ppermute | solution.py:472
  102.8 20.4 %collective-permute-start.13 = (bf16[512,768]{1,0:T(8,128)(2,1)S(1)}, bf16[512,768]{1,0:T(8,128)(2,1)S(1)}, u32[]{:S(2)}, u32[]{:S(2)}) collective-permute-start(bf16[512,768]{1,0:T(8,128)(2,1)S(1)} %get-tuple-element.134), channel_id=1, source_target_pairs={{0,8},{8,0},{16,24},{24,16},{1,9},{9,1},{17,25},{25,17},{2,10},{10... | collective-permute-start | bytes 2359304 | tf_op jit(solution)/shard_map/ppermute | solution.py:472
  104.3 36.4 %collective-permute-start.14 = (bf16[512,768]{1,0:T(8,128)(2,1)S(1)}, bf16[512,768]{1,0:T(8,128)(2,1)}, u32[]{:S(2)}, u32[]{:S(2)}) collective-permute-start(bf16[512,768]{1,0:T(8,128)(2,1)S(1)} %get-tuple-element.133), channel_id=1, source_target_pairs={{0,16},{8,24},{16,0},{24,8},{1,17},{9,25},{17,1},{25,9},{2,18},{10... | collective-permute-start | bytes 2359304 | tf_op jit(solution)/shard_map/ppermute | solution.py:472
  105.7 34.9 %collective-permute-start.15 = (bf16[512,768]{1,0:T(8,128)(2,1)S(1)}, bf16[512,768]{1,0:T(8,128)(2,1)}, u32[]{:S(2)}, u32[]{:S(2)}) collective-permute-start(bf16[512,768]{1,0:T(8,128)(2,1)S(1)} %get-tuple-element.132), channel_id=1, source_target_pairs={{0,24},{8,16},{16,8},{24,0},{1,25},{9,17},{17,9},{25,1},{2,26},{10... | collective-permute-start | bytes 2359304 | tf_op jit(solution)/shard_map/ppermute | solution.py:472
  154.4 16.0 %collective-permute-start.18 = (bf16[128,2048]{1,0:T(8,128)(2,1)}, bf16[128,2048]{1,0:T(8,128)(2,1)S(1)}, u32[]{:S(2)}, u32[]{:S(2)}) collective-permute-start(bf16[128,2048]{1,0:T(8,128)(2,1)} %get-tuple-element.71), channel_id=1, source_target_pairs={{0,24},{8,16},{16,8},{24,0},{1,25},{9,17},{17,9},{25,1},{2,26},{10... | collective-permute-start | bytes 1572872 | tf_op jit(solution)/shard_map/ppermute | solution.py:472
  156.0 25.6 %collective-permute-start.17 = (bf16[128,2048]{1,0:T(8,128)(2,1)}, bf16[128,2048]{1,0:T(8,128)(2,1)S(1)}, u32[]{:S(2)}, u32[]{:S(2)}) collective-permute-start(bf16[128,2048]{1,0:T(8,128)(2,1)} %get-tuple-element.70), channel_id=1, source_target_pairs={{0,16},{8,24},{16,0},{24,8},{1,17},{9,25},{17,1},{25,9},{2,18},{10... | collective-permute-start | bytes 1572872 | tf_op jit(solution)/shard_map/ppermute | solution.py:472
  157.2 24.5 %collective-permute-start.16 = (bf16[128,2048]{1,0:T(8,128)(2,1)}, bf16[128,2048]{1,0:T(8,128)(2,1)S(1)}, u32[]{:S(2)}, u32[]{:S(2)}) collective-permute-start(bf16[128,2048]{1,0:T(8,128)(2,1)} %get-tuple-element.69), channel_id=1, source_target_pairs={{0,8},{8,0},{16,24},{24,16},{1,9},{9,1},{17,25},{25,17},{2,10},{10... | collective-permute-start | bytes 1572872 | tf_op jit(solution)/shard_map/ppermute | solution.py:472
  158.6 34.3 %collective-permute-start.24 = (bf16[128,2048]{1,0:T(8,128)(2,1)}, bf16[128,2048]{1,0:T(8,128)(2,1)S(1)}, u32[]{:S(2)}, u32[]{:S(2)}) collective-permute-start(bf16[128,2048]{1,0:T(8,128)(2,1)} %param.35), channel_id=1, source_target_pairs={{0,24},{8,16},{16,8},{24,0},{1,25},{9,17},{17,9},{25,1},{2,26},{10... | collective-permute-start | bytes 1572872 | tf_op jit(solution)/shard_map/ppermute | solution.py:472
  184.5 19.8 %collective-permute-start.19 = (bf16[128,2048]{1,0:T(8,128)(2,1)}, bf16[128,2048]{1,0:T(8,128)(2,1)}, u32[]{:S(2)}, u32[]{:S(2)}) collective-permute-start(bf16[128,2048]{1,0:T(8,128)(2,1)} %multiply_convert_fusion.refs_0_), channel_id=1, source_target_pairs={{0,8},{8,0},{16,24},{24,16},{1,9},{9,1},{17,25},{25,17},{2,10},{10... | collective-permute-start | bytes 1572872 | tf_op jit(solution)/shard_map/ppermute | solution.py:472
  185.6 18.7 %collective-permute-start.20 = (bf16[128,2048]{1,0:T(8,128)(2,1)}, bf16[128,2048]{1,0:T(8,128)(2,1)}, u32[]{:S(2)}, u32[]{:S(2)}) collective-permute-start(bf16[128,2048]{1,0:T(8,128)(2,1)} %multiply_convert_fusion.refs_0_), channel_id=1, source_target_pairs={{0,16},{8,24},{16,0},{24,8},{1,17},{9,25},{17,1},{25,9},{2,18},{10... | collective-permute-start | bytes 1572872 | tf_op jit(solution)/shard_map/ppermute | solution.py:472
  186.5 27.1 %collective-permute-start.21 = (bf16[128,2048]{1,0:T(8,128)(2,1)}, bf16[128,2048]{1,0:T(8,128)(2,1)}, u32[]{:S(2)}, u32[]{:S(2)}) collective-permute-start(bf16[128,2048]{1,0:T(8,128)(2,1)} %multiply_convert_fusion.refs_0_), channel_id=1, source_target_pairs={{0,24},{8,16},{16,8},{24,0},{1,25},{9,17},{17,9},{25,1},{2,26},{10... | collective-permute-start | bytes 1572872 | tf_op jit(solution)/shard_map/ppermute | solution.py:472
  257.1 203.0 %reduce-scatter.11.cloned.1.call-start = ((), (), s32[]{:S(2)}) async-start(), calls=%async_computation.10 | async-start | bytes 2949120 | tf_op jit(solution)/shard_map/reduce_scatter | solution.py:530
  257.7 212.5 %reduce-scatter.7.cloned.1.call-start = ((), (), s32[]{:S(2)}) async-start(), calls=%async_computation.8 | async-start | bytes 5898240 | tf_op jit(solution)/shard_map/reduce_scatter | solution.py:530
  267.4 16.0 %collective-permute-start.30 = (bf16[128,2048]{1,0:T(8,128)(2,1)}, bf16[128,2048]{1,0:T(8,128)(2,1)S(1)}, u32[]{:S(2)}, u32[]{:S(2)}) collective-permute-start(bf16[128,2048]{1,0:T(8,128)(2,1)} %get-tuple-element.92), channel_id=1, source_target_pairs={{0,24},{8,16},{16,8},{24,0},{1,25},{9,17},{17,9},{25,1},{2,26},{10... | collective-permute-start | bytes 1572872 | tf_op jit(solution)/shard_map/ppermute | solution.py:472
  269.5 23.8 %collective-permute-start.29 = (bf16[128,2048]{1,0:T(8,128)(2,1)}, bf16[128,2048]{1,0:T(8,128)(2,1)S(1)}, u32[]{:S(2)}, u32[]{:S(2)}) collective-permute-start(bf16[128,2048]{1,0:T(8,128)(2,1)} %get-tuple-element.91), channel_id=1, source_target_pairs={{0,16},{8,24},{16,0},{24,8},{1,17},{9,25},{17,1},{25,9},{2,18},{10... | collective-permute-start | bytes 1572872 | tf_op jit(solution)/shard_map/ppermute | solution.py:472
  270.6 22.8 %collective-permute-start.28 = (bf16[128,2048]{1,0:T(8,128)(2,1)}, bf16[128,2048]{1,0:T(8,128)(2,1)S(1)}, u32[]{:S(2)}, u32[]{:S(2)}) collective-permute-start(bf16[128,2048]{1,0:T(8,128)(2,1)} %get-tuple-element.90), channel_id=1, source_target_pairs={{0,8},{8,0},{16,24},{24,16},{1,9},{9,1},{17,25},{25,17},{2,10},{10... | collective-permute-start | bytes 1572872 | tf_op jit(solution)/shard_map/ppermute | solution.py:472
  296.7 14.9 %collective-permute-start.31 = (bf16[128,2048]{1,0:T(8,128)(2,1)S(1)}, bf16[128,2048]{1,0:T(8,128)(2,1)S(1)}, u32[]{:S(2)}, u32[]{:S(2)}) collective-permute-start(bf16[128,2048]{1,0:T(8,128)(2,1)S(1)} %get-tuple-element.126.refs_1_.refs_3_), channel_id=1, source_target_pairs={{0,8},{8,0},{16,24},{24,16},{1,9},{9,1},{17,25},{25,17},{2,10},{10... | collective-permute-start | bytes 1572872 | tf_op jit(solution)/shard_map/ppermute | solution.py:472
  298.3 26.0 %collective-permute-start.32 = (bf16[128,2048]{1,0:T(8,128)(2,1)S(1)}, bf16[128,2048]{1,0:T(8,128)(2,1)S(1)}, u32[]{:S(2)}, u32[]{:S(2)}) collective-permute-start(bf16[128,2048]{1,0:T(8,128)(2,1)S(1)} %get-tuple-element.126.refs_1_.refs_3_), channel_id=1, source_target_pairs={{0,16},{8,24},{16,0},{24,8},{1,17},{9,25},{17,1},{25,9},{2,18},{10... | collective-permute-start | bytes 1572872 | tf_op jit(solution)/shard_map/ppermute | solution.py:472
  298.9 25.4 %collective-permute-start.33 = (bf16[128,2048]{1,0:T(8,128)(2,1)S(1)}, bf16[128,2048]{1,0:T(8,128)(2,1)S(1)}, u32[]{:S(2)}, u32[]{:S(2)}) collective-permute-start(bf16[128,2048]{1,0:T(8,128)(2,1)S(1)} %get-tuple-element.126.refs_1_.refs_3_), channel_id=1, source_target_pairs={{0,24},{8,16},{16,8},{24,0},{1,25},{9,17},{17,9},{25,1},{2,26},{10... | collective-permute-start | bytes 1572872 | tf_op jit(solution)/shard_map/ppermute | solution.py:472
  300.3 38.3 %collective-permute-start.52 = (bf16[512,512]{1,0:T(8,128)(2,1)S(1)}, bf16[512,512]{1,0:T(8,128)(2,1)}, u32[]{:S(2)}, u32[]{:S(2)}) collective-permute-start(bf16[512,512]{1,0:T(8,128)(2,1)S(1)} %copy-done.12), channel_id=1, source_target_pairs={{0,8},{8,0},{16,24},{24,16},{1,9},{9,1},{17,25},{25,17},{2,10},{10... | collective-permute-start | bytes 1572872 | tf_op jit(solution)/shard_map/ppermute | solution.py:472
  301.8 43.9 %collective-permute-start.53 = (bf16[512,512]{1,0:T(8,128)(2,1)S(1)}, bf16[512,512]{1,0:T(8,128)(2,1)}, u32[]{:S(2)}, u32[]{:S(2)}) collective-permute-start(bf16[512,512]{1,0:T(8,128)(2,1)S(1)} %copy-done.12), channel_id=1, source_target_pairs={{0,16},{8,24},{16,0},{24,8},{1,17},{9,25},{17,1},{25,9},{2,18},{10... | collective-permute-start | bytes 1572872 | tf_op jit(solution)/shard_map/ppermute | solution.py:472
  311.6 34.1 %collective-permute-start.54 = (bf16[512,512]{1,0:T(8,128)(2,1)S(1)}, bf16[512,512]{1,0:T(8,128)(2,1)}, u32[]{:S(2)}, u32[]{:S(2)}) collective-permute-start(bf16[512,512]{1,0:T(8,128)(2,1)S(1)} %copy-done.12), channel_id=1, source_target_pairs={{0,24},{8,16},{16,8},{24,0},{1,25},{9,17},{17,9},{25,1},{2,26},{10... | collective-permute-start | bytes 1572872 | tf_op jit(solution)/shard_map/ppermute | solution.py:472
  353.6 160.4 %reduce-scatter.5.cloned.1.call-start = ((), (), s32[]{:S(2)}) async-start(), calls=%async_computation.7 | async-start | bytes 2359296 | tf_op jit(solution)/shard_map/reduce_scatter | solution.py:530
  389.8 8.9 %collective-permute-start.48 = (f32[4608]{0:T(1024)S(1)}, f32[4608]{0:T(1024)S(1)}, u32[]{:S(2)}, u32[]{:S(2)}) collective-permute-start(f32[4608]{0:T(1024)S(1)} %pad_maximum_fusion.3), channel_id=1, source_target_pairs={{0,24},{8,16},{16,8},{24,0},{1,25},{9,17},{17,9},{25,1},{2,26},{10... | collective-permute-start | bytes 55304 | tf_op jit(solution)/shard_map/ppermute | solution.py:472
  391.5 8.8 %collective-permute-start.47 = (f32[4608]{0:T(1024)S(1)}, f32[4608]{0:T(1024)S(1)}, u32[]{:S(2)}, u32[]{:S(2)}) collective-permute-start(f32[4608]{0:T(1024)S(1)} %pad_maximum_fusion.3), channel_id=1, source_target_pairs={{0,16},{8,24},{16,0},{24,8},{1,17},{9,25},{17,1},{25,9},{2,18},{10... | collective-permute-start | bytes 55304 | tf_op jit(solution)/shard_map/ppermute | solution.py:472
  397.7 9.2 %collective-permute-start.50 = (bf16[4,128,256]{2,1,0:T(8,128)(2,1)S(1)}, bf16[4,128,256]{2,1,0:T(8,128)(2,1)S(1)}, u32[]{:S(2)}, u32[]{:S(2)}) collective-permute-start(bf16[4,128,256]{2,1,0:T(8,128)(2,1)S(1)} %bitcast.76), channel_id=1, source_target_pairs={{0,16},{8,24},{16,0},{24,8},{1,17},{9,25},{17,1},{25,9},{2,18},{10... | collective-permute-start | bytes 786440 | tf_op jit(solution)/shard_map/ppermute | solution.py:472
  422.0 15.0 %collective-permute-start.25 = (bf16[128,2048]{1,0:T(8,128)(2,1)}, bf16[128,2048]{1,0:T(8,128)(2,1)S(1)}, u32[]{:S(2)}, u32[]{:S(2)}) collective-permute-start(bf16[128,2048]{1,0:T(8,128)(2,1)} %get-tuple-element.83), channel_id=1, source_target_pairs={{0,8},{8,0},{16,24},{24,16},{1,9},{9,1},{17,25},{25,17},{2,10},{10... | collective-permute-start | bytes 1572872 | tf_op jit(solution)/shard_map/ppermute | solution.py:472
  422.8 35.5 %collective-permute-start.26 = (bf16[128,2048]{1,0:T(8,128)(2,1)}, bf16[128,2048]{1,0:T(8,128)(2,1)}, u32[]{:S(2)}, u32[]{:S(2)}) collective-permute-start(bf16[128,2048]{1,0:T(8,128)(2,1)} %get-tuple-element.84), channel_id=1, source_target_pairs={{0,16},{8,24},{16,0},{24,8},{1,17},{9,25},{17,1},{25,9},{2,18},{10... | collective-permute-start | bytes 1572872 | tf_op jit(solution)/shard_map/ppermute | solution.py:472
  424.0 35.8 %collective-permute-start.27 = (bf16[128,2048]{1,0:T(8,128)(2,1)}, bf16[128,2048]{1,0:T(8,128)(2,1)}, u32[]{:S(2)}, u32[]{:S(2)}) collective-permute-start(bf16[128,2048]{1,0:T(8,128)(2,1)} %get-tuple-element.85), channel_id=1, source_target_pairs={{0,24},{8,16},{16,8},{24,0},{1,25},{9,17},{17,9},{25,1},{2,26},{10... | collective-permute-start | bytes 1572872 | tf_op jit(solution)/shard_map/ppermute | solution.py:472
  428.1 32.0 %collective-permute-start.42 = (bf16[128,2048]{1,0:T(8,128)(2,1)}, bf16[128,2048]{1,0:T(8,128)(2,1)S(1)}, u32[]{:S(2)}, u32[]{:S(2)}) collective-permute-start(bf16[128,2048]{1,0:T(8,128)(2,1)} %get-tuple-element.139), channel_id=1, source_target_pairs={{0,24},{8,16},{16,8},{24,0},{1,25},{9,17},{17,9},{25,1},{2,26},{10... | collective-permute-start | bytes 1572872 | tf_op jit(solution)/shard_map/ppermute | solution.py:472
  429.4 40.8 %collective-permute-start.41 = (bf16[128,2048]{1,0:T(8,128)(2,1)}, bf16[128,2048]{1,0:T(8,128)(2,1)S(1)}, u32[]{:S(2)}, u32[]{:S(2)}) collective-permute-start(bf16[128,2048]{1,0:T(8,128)(2,1)} %get-tuple-element.140), channel_id=1, source_target_pairs={{0,16},{8,24},{16,0},{24,8},{1,17},{9,25},{17,1},{25,9},{2,18},{10... | collective-permute-start | bytes 1572872 | tf_op jit(solution)/shard_map/ppermute | solution.py:472
  437.8 36.7 %collective-permute-start.40 = (bf16[128,2048]{1,0:T(8,128)(2,1)}, bf16[128,2048]{1,0:T(8,128)(2,1)S(1)}, u32[]{:S(2)}, u32[]{:S(2)}) collective-permute-start(bf16[128,2048]{1,0:T(8,128)(2,1)} %get-tuple-element.138), channel_id=1, source_target_pairs={{0,8},{8,0},{16,24},{24,16},{1,9},{9,1},{17,25},{25,17},{2,10},{10... | collective-permute-start | bytes 1572872 | tf_op jit(solution)/shard_map/ppermute | solution.py:472
  458.3 65.5 %collective-permute-start.63 = (bf16[256,2560]{1,0:T(8,128)(2,1)}, bf16[256,2560]{1,0:T(8,128)(2,1)}, u32[]{:S(2)}, u32[]{:S(2)}) collective-permute-start(bf16[256,2560]{1,0:T(8,128)(2,1)} %reduce-scatter.9.cloned.1.call-done.refs_0_), channel_id=1, source_target_pairs={{0,16},{8,24},{16,0},{24,8},{1,17},{9,25},{17,1},{25,9},{2,18},{10... | collective-permute-start | bytes 3932168 | tf_op jit(solution)/shard_map/ppermute | solution.py:472
  459.7 65.8 %collective-permute-start.62 = (bf16[256,2560]{1,0:T(8,128)(2,1)}, bf16[256,2560]{1,0:T(8,128)(2,1)}, u32[]{:S(2)}, u32[]{:S(2)}) collective-permute-start(bf16[256,2560]{1,0:T(8,128)(2,1)} %reduce-scatter.9.cloned.1.call-done.refs_0_), channel_id=1, source_target_pairs={{0,8},{8,0},{16,24},{24,16},{1,9},{9,1},{17,25},{25,17},{2,10},{10... | collective-permute-start | bytes 3932168 | tf_op jit(solution)/shard_map/ppermute | solution.py:472
  460.1 42.7 %collective-permute-start.66 = (bf16[256,640]{1,0:T(8,128)(2,1)}, bf16[256,640]{1,0:T(8,128)(2,1)S(1)}, u32[]{:S(2)}, u32[]{:S(2)}) collective-permute-start(bf16[256,640]{1,0:T(8,128)(2,1)} %reduce-scatter.11.cloned.1.call-done.refs_5_), channel_id=1, source_target_pairs={{0,8},{8,0},{16,24},{24,16},{1,9},{9,1},{17,25},{25,17},{2,10},{10... | collective-permute-start | bytes 983048 | tf_op jit(solution)/shard_map/ppermute | solution.py:472
  470.2 46.6 %collective-permute-start.56 = (bf16[256,1280]{1,0:T(8,128)(2,1)}, bf16[256,1280]{1,0:T(8,128)(2,1)}, u32[]{:S(2)}, u32[]{:S(2)}) collective-permute-start(bf16[256,1280]{1,0:T(8,128)(2,1)} %reduce-scatter.7.cloned.1.call-done.refs_0_), channel_id=1, source_target_pairs={{0,16},{8,24},{16,0},{24,8},{1,17},{9,25},{17,1},{25,9},{2,18},{10... | collective-permute-start | bytes 1966088 | tf_op jit(solution)/shard_map/ppermute | solution.py:472
  474.5 39.5 %collective-permute-start.67 = (bf16[256,640]{1,0:T(8,128)(2,1)}, bf16[256,640]{1,0:T(8,128)(2,1)}, u32[]{:S(2)}, u32[]{:S(2)}) collective-permute-start(bf16[256,640]{1,0:T(8,128)(2,1)} %reduce-scatter.11.cloned.1.call-done.refs_5_), channel_id=1, source_target_pairs={{0,16},{8,24},{16,0},{24,8},{1,17},{9,25},{17,1},{25,9},{2,18},{10... | collective-permute-start | bytes 983048 | tf_op jit(solution)/shard_map/ppermute | solution.py:472
  502.9 26.0 %collective-permute-start.55 = (bf16[256,1280]{1,0:T(8,128)(2,1)}, bf16[256,1280]{1,0:T(8,128)(2,1)}, u32[]{:S(2)}, u32[]{:S(2)}) collective-permute-start(bf16[256,1280]{1,0:T(8,128)(2,1)} %reduce-scatter.7.cloned.1.call-done.refs_0_), channel_id=1, source_target_pairs={{0,8},{8,0},{16,24},{24,16},{1,9},{9,1},{17,25},{25,17},{2,10},{10... | collective-permute-start | bytes 1966088 | tf_op jit(solution)/shard_map/ppermute | solution.py:472
  514.0 14.7 %collective-permute-start.59 = (bf16[256,512]{1,0:T(8,128)(2,1)}, bf16[256,512]{1,0:T(8,128)(2,1)S(1)}, u32[]{:S(2)}, u32[]{:S(2)}) collective-permute-start(bf16[256,512]{1,0:T(8,128)(2,1)} %reduce-scatter.5.cloned.1.call-done.refs_0_), channel_id=1, source_target_pairs={{0,8},{8,0},{16,24},{24,16},{1,9},{9,1},{17,25},{25,17},{2,10},{10... | collective-permute-start | bytes 786440 | tf_op jit(solution)/shard_map/ppermute | solution.py:472
  516.9 15.0 %collective-permute-start.60 = (bf16[256,512]{1,0:T(8,128)(2,1)}, bf16[256,512]{1,0:T(8,128)(2,1)S(1)}, u32[]{:S(2)}, u32[]{:S(2)}) collective-permute-start(bf16[256,512]{1,0:T(8,128)(2,1)} %reduce-scatter.5.cloned.1.call-done.refs_0_), channel_id=1, source_target_pairs={{0,16},{8,24},{16,0},{24,8},{1,17},{9,25},{17,1},{25,9},{2,18},{10... | collective-permute-start | bytes 786440 | tf_op jit(solution)/shard_map/ppermute | solution.py:472
  523.8 10.4 %collective-permute-start.61 = (bf16[256,512]{1,0:T(8,128)(2,1)}, bf16[256,512]{1,0:T(8,128)(2,1)S(1)}, u32[]{:S(2)}, u32[]{:S(2)}) collective-permute-start(bf16[256,512]{1,0:T(8,128)(2,1)} %reduce-scatter.5.cloned.1.call-done.refs_0_), channel_id=1, source_target_pairs={{0,24},{8,16},{16,8},{24,0},{1,25},{9,17},{17,9},{25,1},{2,26},{10... | collective-permute-start | bytes 786440 | tf_op jit(solution)/shard_map/ppermute | solution.py:472
  525.6 15.2 %collective-permute-start.57 = (bf16[128,1280]{1,0:T(8,128)(2,1)S(1)}, bf16[128,1280]{1,0:T(8,128)(2,1)S(1)}, u32[]{:S(2)}, u32[]{:S(2)}) collective-permute-start(bf16[128,1280]{1,0:T(8,128)(2,1)S(1)} %slice.265), channel_id=1, source_target_pairs={{0,8},{8,0},{16,24},{24,16},{1,9},{9,1},{17,25},{25,17},{2,10},{10... | collective-permute-start | bytes 983048 | tf_op jit(solution)/shard_map/ppermute | solution.py:472
  528.7 28.2 %collective-permute-start.64 = (bf16[128,2560]{1,0:T(8,128)(2,1)S(1)}, bf16[128,2560]{1,0:T(8,128)(2,1)S(1)}, u32[]{:S(2)}, u32[]{:S(2)}) collective-permute-start(bf16[128,2560]{1,0:T(8,128)(2,1)S(1)} %slice.269), channel_id=1, source_target_pairs={{0,8},{8,0},{16,24},{24,16},{1,9},{9,1},{17,25},{25,17},{2,10},{10... | collective-permute-start | bytes 1966088 | tf_op jit(solution)/shard_map/ppermute | solution.py:472
  528.9 28.1 %collective-permute-start.65 = (bf16[128,2560]{1,0:T(8,128)(2,1)S(1)}, bf16[128,2560]{1,0:T(8,128)(2,1)}, u32[]{:S(2)}, u32[]{:S(2)}) collective-permute-start(bf16[128,2560]{1,0:T(8,128)(2,1)S(1)} %slice.270), channel_id=1, source_target_pairs={{0,16},{8,24},{16,0},{24,8},{1,17},{9,25},{17,1},{25,9},{2,18},{10... | collective-permute-start | bytes 1966088 | tf_op jit(solution)/shard_map/ppermute | solution.py:472
  531.8 19.9 %collective-permute-start.58 = (bf16[128,1280]{1,0:T(8,128)(2,1)S(1)}, bf16[128,1280]{1,0:T(8,128)(2,1)}, u32[]{:S(2)}, u32[]{:S(2)}) collective-permute-start(bf16[128,1280]{1,0:T(8,128)(2,1)S(1)} %slice.266), channel_id=1, source_target_pairs={{0,16},{8,24},{16,0},{24,8},{1,17},{9,25},{17,1},{25,9},{2,18},{10... | collective-permute-start | bytes 983048 | tf_op jit(solution)/shard_map/ppermute | solution.py:472
  534.2 22.7 %collective-permute-start.68 = (bf16[128,640]{1,0:T(8,128)(2,1)}, bf16[128,640]{1,0:T(8,128)(2,1)}, u32[]{:S(2)}, u32[]{:S(2)}) collective-permute-start(bf16[128,640]{1,0:T(8,128)(2,1)} %slice.271), channel_id=1, source_target_pairs={{0,8},{8,0},{16,24},{24,16},{1,9},{9,1},{17,25},{25,17},{2,10},{10... | collective-permute-start | bytes 491528 | tf_op jit(solution)/shard_map/ppermute | solution.py:472
  541.5 15.4 %collective-permute-start.69 = (bf16[128,640]{1,0:T(8,128)(2,1)}, bf16[128,640]{1,0:T(8,128)(2,1)}, u32[]{:S(2)}, u32[]{:S(2)}) collective-permute-start(bf16[128,640]{1,0:T(8,128)(2,1)} %slice.272), channel_id=1, source_target_pairs={{0,16},{8,24},{16,0},{24,8},{1,17},{9,25},{17,1},{25,9},{2,18},{10... | collective-permute-start | bytes 491528 | tf_op jit(solution)/shard_map/ppermute | solution.py:472
  (54 other events, 1021.7 us)
Sparse Core Ops, SparseCore 0:
  10.2 89.4 all-gather.3
  101.9 84.7 all-gather.5
  188.3 45.3 all-gather.7
  257.2 107.0 reduce-scatter.8
  367.1 36.2 reduce-scatter.10
  405.6 58.9 reduce-scatter.6
  467.4 34.4 reduce-scatter.4
